TPU v7x, 32 devices: a whole 2x2x4 slice. The times are simulated.
32 devices in a mesh: dp: 16 (over z, y, x), tensor: 2 (over core).
Axes of the slice: x: 2, y: 2, z: 4, core: 2. Of those that a mesh axis runs over, the one named last changes fastest.
Arguments:
- tokens: bfloat16 [32, 1024, 768], P('dp'), may hold values from -6 to 6
- segments: int32 [32, 1024], P('dp'), may hold values from 0 to 8, as said below
- qkv_weight: bfloat16 [768, 3, 768], P(('dp', 'tensor')), may hold values from -0.21875 to 0.21875
- out_weight: bfloat16 [768, 768], P(('dp', 'tensor')), may hold values from -1.75 to 1.75
- norm_gain: bfloat16 [768, 2], P(('dp', 'tensor')), may hold values from 0.5 to 1.5
- norm_shift: bfloat16 [768, 2], P(('dp', 'tensor')), may hold values from -3 to 3
- gate_up: bfloat16 [768, 2, 3072], P('dp', None, 'tensor'), may hold values from -0.21875 to 0.21875
- down_weight: bfloat16 [768, 3072], P('dp', 'tensor'), may hold values from -0.109375 to 0.109375
- cotangent: bfloat16 [32, 1024, 768], P('dp', 'tensor'), may hold values from -6 to 6
Outputs:
- output: bfloat16 [32, 1024, 768], P('dp', 'tensor')
- input_grad: float32 [32, 1024, 768], P('dp', 'tensor')
- qkv_grad: float32 [768, 3, 768], P(('dp', 'tensor'))
- out_weight_grad: float32 [768, 768], P(('dp', 'tensor'))
- gain_grad: float32 [768, 2], P(('dp', 'tensor'))
- shift_grad: float32 [768, 2], P(('dp', 'tensor'))
- gate_up_grad: float32 [768, 2, 3072], P('dp', None, 'tensor')
- down_grad: float32 [768, 3072], P('dp', 'tensor')
Inputs may be any that keep to these rules, and one draw needn't show every extreme that they name: `segments`: never falling along a sequence; each of the 8 documents has at least one token, and exactly one of them holds 512 tokens, more than any other; the value 8 marks padding, which every sequence has.
All inputs are finite; a program needn't handle non-finite values.
Results may differ from a plain program's by a relative error of at most 0.015.
Values may be sent and summed in bfloat16 or wider, within the bound.
No kernel may reach another device: no remote copies, remote signals or barrier semaphores. Data moves between devices by JAX's collectives and lax.ppermute only.
A program may use at most 320 MiB of HBM per device.

v0:
```python
import jax
import jax.numpy as jnp
from jax import lax
from jax.experimental import pallas as pl
from jax.experimental.pallas import tpu as pltpu
from jax.sharding import PartitionSpec as P

D = 768
HEADS = 12
HEAD = 64
SEQ = 1024
NDOC = 8


EPSILON = 1e-05
MASKED = -1e30


def for_sending(value):
    return jax.tree.map(lambda a: a.astype(jnp.bfloat16) if a.dtype == jnp.float32 else a, value)


def rotary_tables(segment_row):
    labels = jnp.arange(NDOC + 1, dtype=jnp.int32)
    member = (segment_row[:, None] == labels[None, :]).astype(jnp.int32)
    counts = jnp.sum(member, axis=0)
    starts = jnp.concatenate([jnp.zeros((1,), jnp.int32), jnp.cumsum(counts)[:-1]])
    offset = jnp.sum(member * starts[None, :], axis=1)
    position = (jnp.arange(SEQ, dtype=jnp.int32) - offset).astype(jnp.float32)
    exponent = -2.0 * jnp.arange(HEAD // 2).astype(jnp.float32) / HEAD
    frequency = jnp.power(jnp.float32(1000.0), exponent)
    angle = position[:, None] * frequency[None, :]
    return (jnp.cos(angle)[:, None, :], jnp.sin(angle)[:, None, :])


def rotate(vector, cosine, sine):
    half = vector.shape[-1] // 2
    first_half = vector[..., :half]
    second_half = vector[..., half:]
    return jnp.concatenate(
        [first_half * cosine - second_half * sine, second_half * cosine + first_half * sine],
        axis=-1,
    )


def unrotate(gradient, cosine, sine):

    def turned(vector):
        return rotate(vector, cosine, sine)

    _, pullback = jax.vjp(turned, gradient)
    return pullback(gradient)[0]


def layer_norm(vector, gain, shift):
    center = vector - jnp.mean(vector, axis=-1, keepdims=True)
    variance = jnp.mean(center * center, axis=-1, keepdims=True)
    return center * lax.rsqrt(variance + EPSILON) * gain + shift


def swiglu_piece(gate, upper):
    return jax.nn.silu(gate) * upper


def accumulate(total, term):
    if total is None:
        return term
    return tuple((left + right for left, right in zip(total, term)))


def general_device(
    tokens, segments, qkv_weight, out_weight, norm_gain, norm_shift, gate_up, down_weight, cotangent
):
    tensor_size = lax.axis_size("tensor")
    own_rows = SEQ // tensor_size
    row_start = lax.axis_index("tensor") * own_rows
    score_scale = HEAD ** (-0.5)
    qkv_full, out_full, gain_full, shift_full = (
        lax.all_gather(qkv_weight, ("dp", "tensor"), axis=0, tiled=True),
        lax.all_gather(out_weight, ("dp", "tensor"), axis=0, tiled=True),
        lax.all_gather(norm_gain, ("dp", "tensor"), axis=0, tiled=True),
        lax.all_gather(norm_shift, ("dp", "tensor"), axis=0, tiled=True),
    )
    gains = gain_full.astype(jnp.float32)
    shifts = shift_full.astype(jnp.float32)
    gate_up_full, down_full = (
        lax.all_gather(gate_up, "dp", axis=0, tiled=True),
        lax.all_gather(down_weight, "dp", axis=0, tiled=True),
    )
    batches = tokens.shape[0]
    outputs = []
    input_grads = []
    attn_total = None
    mlp_total = None
    for batch_index in range(batches):
        source = tokens[batch_index]
        own_source = lax.dynamic_slice_in_dim(source, row_start, own_rows, 0)
        segment_row = segments[batch_index]
        cosine, sine = rotary_tables(segment_row)
        own_cos = lax.dynamic_slice_in_dim(cosine, row_start, own_rows, 0)
        own_sin = lax.dynamic_slice_in_dim(sine, row_start, own_rows, 0)
        query_proj = jnp.einsum(
            "sd,de->se", own_source, qkv_full[:, 0], preferred_element_type=jnp.float32
        )
        pair_proj = jnp.einsum(
            "sd,dke->ske", source, qkv_full[:, 1:], preferred_element_type=jnp.float32
        )
        keys = rotate(pair_proj[:, 0].reshape(SEQ, HEADS, HEAD), cosine, sine).astype(jnp.bfloat16)
        values = pair_proj[:, 1].reshape(SEQ, HEADS, HEAD).astype(jnp.bfloat16)
        queries = rotate(query_proj.reshape(own_rows, HEADS, HEAD), own_cos, own_sin).astype(
            jnp.bfloat16
        )
        own_segments = lax.dynamic_slice_in_dim(segment_row, row_start, own_rows, 0)
        allowed = (own_segments[:, None] == segment_row[None, :])[None]
        raw_scores = (
            jnp.einsum("qhe,khe->hqk", queries, keys, preferred_element_type=jnp.float32)
            * score_scale
        )
        masked = jnp.where(allowed, raw_scores, MASKED)
        top_score = jnp.max(masked, axis=-1, keepdims=True)
        logsum = top_score + jnp.log(jnp.sum(jnp.exp(masked - top_score), axis=-1, keepdims=True))
        probs_low = jnp.exp(masked - logsum).astype(jnp.bfloat16)
        context = (
            jnp.einsum("hqk,khe->qhe", probs_low, values, preferred_element_type=jnp.float32)
            .reshape(own_rows, D)
            .astype(jnp.bfloat16)
        )
        attended = jnp.dot(context, out_full, preferred_element_type=jnp.float32)
        hidden_in = own_source.astype(jnp.float32) + attended
        normed = layer_norm(hidden_in, gains[:, 0], shifts[:, 0])
        normed_all = lax.all_gather(normed.astype(jnp.bfloat16), "tensor", axis=0, tiled=True)
        gate_pair = jnp.einsum(
            "sd,dkf->skf", normed_all, gate_up_full, preferred_element_type=jnp.float32
        )
        swiglu = swiglu_piece(gate_pair[:, 0], gate_pair[:, 1]).astype(jnp.bfloat16)
        mlp_out = lax.psum_scatter(
            jnp.einsum("sf,df->sd", swiglu, down_full, preferred_element_type=jnp.float32).astype(
                jnp.bfloat16
            ),
            "tensor",
            scatter_dimension=0,
            tiled=True,
        ).astype(jnp.float32)
        resid = normed + mlp_out
        outputs.append(layer_norm(resid, gains[:, 1], shifts[:, 1]).astype(jnp.bfloat16))
        upstream = cotangent[batch_index].astype(jnp.float32)
        _, second_pull = jax.vjp(layer_norm, resid, gains[:, 1], shifts[:, 1])
        resid_grad, gain_two, shift_two = second_pull(upstream)
        mlp_grad = lax.all_gather(resid_grad.astype(jnp.bfloat16), "tensor", axis=0, tiled=True)
        swiglu_grad = jnp.einsum(
            "sd,df->sf", mlp_grad, down_full, preferred_element_type=jnp.float32
        )
        _, glu_pull = jax.vjp(swiglu_piece, gate_pair[:, 0], gate_pair[:, 1])
        gate_grad, upper_grad = glu_pull(swiglu_grad)
        pair_grad = jnp.stack([gate_grad, upper_grad], axis=1).astype(jnp.bfloat16)
        down_term = jnp.einsum("sd,sf->df", mlp_grad, swiglu, preferred_element_type=jnp.float32)
        gate_up_term = jnp.einsum(
            "sd,skf->dkf", normed_all, pair_grad, preferred_element_type=jnp.float32
        )
        normed_grad = resid_grad + lax.psum_scatter(
            jnp.einsum("skf,dkf->sd", pair_grad, gate_up_full, preferred_element_type=jnp.float32),
            "tensor",
            scatter_dimension=0,
            tiled=True,
        )
        _, first_pull = jax.vjp(layer_norm, hidden_in, gains[:, 0], shifts[:, 0])
        hidden_grad, gain_one, shift_one = first_pull(normed_grad)
        attended_grad = hidden_grad.astype(jnp.bfloat16)
        out_term = jnp.einsum(
            "sd,se->de", context, attended_grad, preferred_element_type=jnp.float32
        )
        context_grad = (
            jnp.einsum("se,de->sd", attended_grad, out_full, preferred_element_type=jnp.float32)
            .astype(jnp.bfloat16)
            .reshape(own_rows, HEADS, HEAD)
        )
        probs = jnp.exp(masked - logsum)
        weights_grad = jnp.einsum(
            "qhe,khe->hqk", context_grad, values, preferred_element_type=jnp.float32
        )
        row_delta = jnp.sum(probs * weights_grad, axis=-1, keepdims=True)
        score_grad = (probs * (weights_grad - row_delta)).astype(jnp.bfloat16)
        query_grad = (
            jnp.einsum("hqk,khe->qhe", score_grad, keys, preferred_element_type=jnp.float32)
            * score_scale
        )
        key_part = (
            jnp.einsum("hqk,qhe->khe", score_grad, queries, preferred_element_type=jnp.float32)
            * score_scale
        )
        value_part = jnp.einsum(
            "hqk,qhe->khe", probs_low, context_grad, preferred_element_type=jnp.float32
        )
        key_value = lax.psum_scatter(
            jnp.stack(
                [
                    key_part.reshape(lax.axis_size("tensor") * own_rows, D),
                    value_part.reshape(lax.axis_size("tensor") * own_rows, D),
                ],
                axis=1,
            ).astype(jnp.bfloat16),
            "tensor",
            scatter_dimension=0,
            tiled=True,
        ).astype(jnp.float32)
        query_back = unrotate(query_grad, own_cos, own_sin).reshape(own_rows, D)
        key_back = unrotate(
            key_value[:, 0].reshape(own_rows, HEADS, HEAD), own_cos, own_sin
        ).reshape(own_rows, D)
        proj_grad = jnp.stack([query_back, key_back, key_value[:, 1]], axis=1).astype(jnp.bfloat16)
        input_grads.append(
            hidden_grad
            + jnp.einsum("ske,dke->sd", proj_grad, qkv_full, preferred_element_type=jnp.float32)
        )
        qkv_term = jnp.einsum(
            "sd,ske->dke", own_source, proj_grad, preferred_element_type=jnp.float32
        )
        gain_term = jnp.stack([gain_one, gain_two], axis=1)
        shift_term = jnp.stack([shift_one, shift_two], axis=1)
        attn_terms = (qkv_term, out_term, gain_term, shift_term)
        mlp_terms = (gate_up_term, down_term)
        attn_total = accumulate(attn_total, attn_terms)
        mlp_total = accumulate(mlp_total, mlp_terms)
    attn_final = lax.psum_scatter(attn_total, ("dp", "tensor"), scatter_dimension=0, tiled=True)
    mlp_final = jax.tree.map(
        lambda part: part.astype(jnp.float32),
        lax.psum_scatter(for_sending(mlp_total), "dp", scatter_dimension=0, tiled=True),
    )
    return (
        jnp.stack(outputs, axis=0),
        jnp.stack(input_grads, axis=0),
        attn_final[0],
        attn_final[1],
        attn_final[2],
        attn_final[3],
        mlp_final[0],
        mlp_final[1],
    )


HIDDEN = 1536
WIDE = 3 * HIDDEN
REST = 512
TAIL = 2 * REST
GROUP = 4 * HEAD
GROUPS = D // GROUP
KEYS = 128
LANES = 2 * HEAD
BLOCK = 256
NBLOCK = SEQ // BLOCK
ROWS = 256
STEPS = SEQ // ROWS
CHUNK = 512
PIECE = 256
PIECES = 2 * HIDDEN // PIECE
LOG2E = 1.4426950408889634
F32 = jnp.float32
BF16 = jnp.bfloat16


def across(value, move):
    pairs = []
    for z in range(4):
        for y in range(2):
            for x in range(2):
                for c in range(2):
                    tz, ty, tx, tc = move(z, y, x, c)
                    pairs.append((((z * 2 + y) * 2 + x) * 2 + c, ((tz * 2 + ty) * 2 + tx) * 2 + tc))
    return lax.ppermute(value, ("dp", "tensor"), pairs)


def core_swap(value):
    return across(value, lambda z, y, x, c: (z, y, x, 1 - c))


def first_swap(value):
    return across(value, lambda z, y, x, c: (z, y, 1 - x, c) if c == 0 else (z, 1 - y, x, c))


def second_swap(value):
    return across(value, lambda z, y, x, c: (z, 1 - y, x, c) if c == 0 else (z, y, 1 - x, c))


def depth_shift(value, steps):
    return across(value, lambda z, y, x, c: ((z + steps) % 4, y, x, c))


def slot_blocks(sign, core):
    me = lax.axis_index("dp")
    z, y, x = me // 4, (me // 2) % 2, me % 2
    slot = jnp.arange(16, dtype=jnp.int32)
    second, first, depth = slot // 8, (slot // 4) % 2, slot % 4
    x_bit = jnp.where(core == 0, first, second)
    y_bit = jnp.where(core == 0, second, first)
    return (((z + sign * depth) % 4) * 4 + (y ^ y_bit) * 2 + (x ^ x_bit)).astype(jnp.int32)


def depth_parts(block):
    return [block] + [depth_shift(block, k) for k in (1, 2, 3)]


def depth_ring(block):
    parts = [block]
    for _ in range(3):
        parts.append(depth_shift(parts[-1], 1))
    return parts


def cost(flops, nbytes, trans=0):
    return pl.CostEstimate(flops=int(flops), bytes_accessed=int(nbytes), transcendentals=int(trans))


def params(vmem_mb, sem=("arbitrary",)):
    return pltpu.CompilerParams(dimension_semantics=sem, vmem_limit_bytes=vmem_mb << 20)


ANY = pl.BlockSpec(memory_space=pl.ANY)
AFTER = pl.BlockSpec(memory_space=pltpu.HBM)


def pile(parts, deps=()):
    spans, start = [], 0
    for part in parts:
        spans.append((start, part.shape[0]))
        start += part.shape[0]

    def body(*refs):
        ins, out, sem = refs[: len(parts)], refs[-2], refs[-1]
        copies = [
            pltpu.make_async_copy(ref, out.at[pl.ds(at, n)], sem.at[i])
            for i, (ref, (at, n)) in enumerate(zip(ins, spans))
        ]
        for cp in copies:
            cp.start()
        for cp in copies:
            cp.wait()

    shape = (start,) + parts[0].shape[1:]
    return pl.pallas_call(
        body,
        in_specs=[ANY] * len(parts) + [AFTER] * len(deps),
        out_specs=pl.BlockSpec(memory_space=pltpu.VMEM),
        out_shape=jax.ShapeDtypeStruct(shape, parts[0].dtype),
        scratch_shapes=[pltpu.SemaphoreType.DMA((len(parts),))],
        compiler_params=params(16, None),
        cost_estimate=cost(0, 4 * start * shape[1] * shape[2]),
        name="pile",
    )(*parts, *deps)


def place(core, mine, there):
    def body(c, a, b, out, sem):
        first = pltpu.make_async_copy(a, out.at[c[0]], sem.at[0])
        second = pltpu.make_async_copy(b, out.at[1 - c[0]], sem.at[1])
        first.start()
        second.start()
        first.wait()
        second.wait()

    return pl.pallas_call(
        body,
        grid_spec=pltpu.PrefetchScalarGridSpec(
            num_scalar_prefetch=1,
            grid=(1,),
            in_specs=[ANY, ANY],
            out_specs=pl.BlockSpec((2,) + mine.shape, lambda i, c: (0, 0, 0)),
            scratch_shapes=[pltpu.SemaphoreType.DMA((2,))],
        ),
        out_shape=jax.ShapeDtypeStruct((2,) + mine.shape, mine.dtype),
        compiler_params=params(16),
        cost_estimate=cost(0, 4 * mine.size),
        name="place",
    )(core[None], mine, there)


def assemble(own, other, index, deps=()):
    def body(idx, a, b, c, d, *rest):
        out, sem = rest[-2:]
        copies = []
        for i, ref in enumerate((a, b, c, d)):
            for s in range(8):
                copies.append(
                    pltpu.make_async_copy(ref.at[s], out.at[idx[i * 8 + s]], sem.at[i * 8 + s])
                )
        for cp in copies:
            cp.start()
        for cp in copies:
            cp.wait()

    rows, wide = own[0].shape[1:]
    return pl.pallas_call(
        body,
        grid_spec=pltpu.PrefetchScalarGridSpec(
            num_scalar_prefetch=1,
            grid=(1,),
            in_specs=[ANY] * 4 + [AFTER] * len(deps),
            out_specs=pl.BlockSpec((32, rows, wide), lambda i, c: (0, 0, 0)),
            scratch_shapes=[pltpu.SemaphoreType.DMA((32,))],
        ),
        out_shape=jax.ShapeDtypeStruct((32, rows, wide), BF16),
        compiler_params=params(60),
        cost_estimate=cost(0, 4 * 32 * rows * wide),
        name="assemble",
    )(index, *own, *other, *deps)


def turn(vector, cosine, sine):
    lane = lax.broadcasted_iota(jnp.int32, vector.shape, 1)
    swapped = jnp.where(
        lane % HEAD < HEAD // 2,
        pltpu.roll(vector, LANES - HEAD // 2, 1),
        pltpu.roll(vector, HEAD // 2, 1),
    )
    return vector * cosine + swapped * sine


def dot_nn(a, b):
    return lax.dot_general(a, b, (((1,), (0,)), ((), ())), preferred_element_type=F32)


def dot_nt(a, b):
    return lax.dot_general(a, b, (((1,), (1,)), ((), ())), preferred_element_type=F32)


def dot_tn(a, b):
    return lax.dot_general(a, b, (((0,), (0,)), ((), ())), preferred_element_type=F32)


def stacked(low_lane, pair):
    zero = jnp.zeros_like(pair)
    return jnp.concatenate(
        [jnp.where(low_lane, pair, zero), jnp.where(low_lane, zero, pair)], axis=0
    )


def windows(bnd, i, work):
    blocks = (bnd[NBLOCK + i] - bnd[i] + BLOCK // KEYS - 1) // (BLOCK // KEYS)
    for width in range(1, NBLOCK + 1):

        @pl.when(blocks == width)
        def _():
            low = jnp.minimum(bnd[i], (SEQ - width * BLOCK) // KEYS)
            work(pl.ds(pl.multiple_of(low * KEYS, KEYS), width * BLOCK))


def attn_forward(first, count, bounds, source, weights, cosine, sine, seg_col, seg_row, deps=()):
    def body(bnd, x, wq, wk, wv, cos, sin, sc, sr, *rest):
        q_out, k_out, v_out, ctx_out, lse_out, qm = rest[len(deps) :]
        low_lane = lax.broadcasted_iota(jnp.int32, (BLOCK, LANES), 1) < HEAD

        @pl.loop(0, NBLOCK)
        def _(r):
            rows = pl.ds(pl.multiple_of(r * BLOCK, BLOCK), BLOCK)
            xr, cr, sn = x[rows, :], cos[rows, :], sin[rows, :]
            q_proj, k_proj = dot_nn(xr, wq[...]), dot_nn(xr, wk[...])
            v_out[rows, :] = dot_nn(xr, wv[...]).astype(BF16)
            for p in range(GROUP // LANES):
                ln = slice(p * LANES, (p + 1) * LANES)
                q = turn(q_proj[:, ln], cr, sn).astype(BF16) * jnp.asarray(HEAD**-0.5, BF16)
                q_out[rows, ln] = q
                qm[p, r] = stacked(low_lane, q)
                k_out[rows, ln] = turn(k_proj[:, ln], cr, sn).astype(BF16)

        def block(i, _):
            rows = pl.ds(pl.multiple_of(i * BLOCK, BLOCK), BLOCK)
            own = jnp.concatenate([sc[rows, :], sc[rows, :]], axis=0)

            def work(cols):
                seen = own == sr[:, cols]
                for p in range(GROUP // LANES):
                    ln = slice(p * LANES, (p + 1) * LANES)
                    s = jnp.where(seen, dot_nt(qm[p, i], k_out[cols, ln]) * LOG2E, MASKED)
                    top = jnp.max(s, axis=1, keepdims=True)
                    e = jnp.exp2(s - top)
                    total = jnp.sum(e, axis=1, keepdims=True)
                    mixed = dot_nn(e.astype(BF16), v_out[cols, ln]) / total
                    ctx_out[rows, ln] = jnp.where(low_lane, mixed[:BLOCK], mixed[BLOCK:]).astype(BF16)
                    logs = top + jnp.log2(total)
                    flipped = jnp.where(low_lane, logs[:BLOCK], logs[BLOCK:]).T
                    lse_out[0, 2 * p : 2 * p + 1, rows] = flipped[0:1]
                    lse_out[0, 2 * p + 1 : 2 * p + 2, rows] = flipped[HEAD : HEAD + 1]

            windows(bnd, i, work)
            return 0

        lax.fori_loop(0, NBLOCK, block, 0)

    full = lambda shape: pl.BlockSpec(shape, lambda p, b: (0,) * len(shape))
    column = lambda shift: pl.BlockSpec((D, GROUP), lambda p, b: (0, shift * GROUPS + first + p))
    part = pl.BlockSpec((SEQ, GROUP), lambda p, b: (0, p))
    act = jax.ShapeDtypeStruct((SEQ, count * GROUP), BF16)
    return pl.pallas_call(
        body,
        grid_spec=pltpu.PrefetchScalarGridSpec(
            num_scalar_prefetch=1,
            grid=(count,),
            in_specs=[
                full((SEQ, D)),
                column(0),
                column(1),
                column(2),
                full((SEQ, LANES)),
                full((SEQ, LANES)),
                full((SEQ, 1)),
                full((1, SEQ)),
            ]
            + [AFTER] * len(deps),
            out_specs=[part] * 4 + [pl.BlockSpec((1, 8, SEQ), lambda p, b: (p, 0, 0))],
            scratch_shapes=[pltpu.VMEM((GROUP // LANES, NBLOCK, 2 * BLOCK, LANES), BF16)],
        ),
        out_shape=[act] * 4 + [jax.ShapeDtypeStruct((count, 8, SEQ), F32)],
        compiler_params=params(60),
        cost_estimate=cost(
            count * GROUP * (6 * SEQ * D + 16 * SEQ * SEQ), 8 << 20, count * 4 * SEQ * SEQ
        ),
        name="attn_forward",
    )(bounds, source, weights, weights, weights, cosine, sine, seg_col, seg_row, *deps)


def deal(core, whole, mine, theirs, columns):
    parts = whole.reshape(16, 2, D // 32, whole.shape[1])
    first, second = parts[:, 0], parts[:, 1]
    mine[:, :, columns] = jnp.where(core == 0, first, second).astype(BF16)
    theirs[:, :, columns] = jnp.where(core == 0, second, first).astype(BF16)


def attn_backward(at, grad_at, bounds, saved, ctx_grad, source, cosine, sine, seg_col, seg_row, deps=()):
    def body(bnd, q, k, v, o, do, lse, x, cos, sin, sc, sr, *rest):
        core = bnd[2 * NBLOCK]
        out, mine, theirs, qm, dm, dq, dk, dv, dl = rest[len(deps) :]
        low_lane = lax.broadcasted_iota(jnp.int32, (BLOCK, LANES), 1) < HEAD
        row = lax.broadcasted_iota(jnp.int32, (8, LANES), 0)
        lane = lax.broadcasted_iota(jnp.int32, (8, LANES), 1)
        pick = jnp.where(row == lane // HEAD, 1.0, 0.0).astype(F32)
        for p in range(GROUP // LANES):
            ln = slice(p * LANES, (p + 1) * LANES)

            @pl.loop(0, NBLOCK)
            def _(i):
                rows = pl.ds(pl.multiple_of(i * BLOCK, BLOCK), BLOCK)
                qm[p, i] = stacked(low_lane, q[rows, ln])
                dm[p, i] = stacked(low_lane, do[rows, ln])

            dl[p] = lax.dot_general(
                pick,
                do[:, ln].astype(F32) * o[:, ln].astype(F32),
                (((1,), (1,)), ((), ())),
                preferred_element_type=F32,
                precision=lax.Precision.HIGHEST,
            )
        dk[...] = jnp.zeros_like(dk)
        dv[...] = jnp.zeros_like(dv)

        def block(i, _):
            rows = pl.ds(pl.multiple_of(i * BLOCK, BLOCK), BLOCK)
            own = jnp.concatenate([sr[:, rows], sr[:, rows]], axis=1)

            def work(cols):
                seen = sc[cols, :] == own
                for p in range(GROUP // LANES):
                    ln = slice(p * LANES, (p + 1) * LANES)
                    keys, values, qq, dd = k[cols, ln], v[cols, ln], qm[p, i], dm[p, i]
                    logs = jnp.concatenate(
                        [lse[0, 2 * p : 2 * p + 1, rows], lse[0, 2 * p + 1 : 2 * p + 2, rows]], axis=1
                    )
                    deltas = jnp.concatenate([dl[p, 0:1, rows], dl[p, 1:2, rows]], axis=1)
                    s = dot_nt(keys, qq) * LOG2E - logs
                    probs = jnp.exp2(jnp.where(seen, s, MASKED))
                    g = (probs * (dot_nt(values, dd) - deltas)).astype(BF16)
                    dv[cols, ln] += dot_nn(probs.astype(BF16), dd)
                    dk[cols, ln] += dot_nn(g, qq)
                    both = dot_tn(g, keys)
                    dq[rows, ln] = jnp.where(low_lane, both[:BLOCK], both[BLOCK:])

            windows(bnd, i, work)
            return 0

        lax.fori_loop(0, NBLOCK, block, 0)

        @pl.loop(0, NBLOCK)
        def _(r):
            rows = pl.ds(pl.multiple_of(r * BLOCK, BLOCK), BLOCK)
            cr, sn = cos[rows, :], -sin[rows, :]
            for p in range(GROUP // LANES):
                ln = slice(p * LANES, (p + 1) * LANES)
                out[0, rows, ln] = turn(dq[rows, ln] * (HEAD**-0.5), cr, sn).astype(BF16)
                out[1, rows, ln] = turn(dk[rows, ln], cr, sn).astype(BF16)
                out[2, rows, ln] = dv[rows, ln].astype(BF16)

        for i in range(3):
            deal(core, dot_tn(x[...], out[i]), mine, theirs, slice(i * GROUP, (i + 1) * GROUP))

    full = lambda shape: pl.BlockSpec(shape, lambda p, b: (0,) * len(shape))
    part = pl.BlockSpec((SEQ, GROUP), lambda p, b: (0, at))
    low2 = pltpu.VMEM((GROUP // LANES, NBLOCK, 2 * BLOCK, LANES), BF16)
    wide = pltpu.VMEM((SEQ, GROUP), F32)
    dealt = (16, D // 32, 3 * GROUP)
    return pl.pallas_call(
        body,
        grid_spec=pltpu.PrefetchScalarGridSpec(
            num_scalar_prefetch=1,
            grid=(1,),
            in_specs=[part] * 4
            + [
                pl.BlockSpec((SEQ, GROUP), lambda p, b: (0, grad_at)),
                pl.BlockSpec((1, 8, SEQ), lambda p, b: (at, 0, 0)),
                full((SEQ, D)),
                full((SEQ, LANES)),
                full((SEQ, LANES)),
                full((SEQ, 1)),
                full((1, SEQ)),
            ]
            + [AFTER] * len(deps),
            out_specs=[full((3, SEQ, GROUP)), full(dealt), full(dealt)],
            scratch_shapes=[
                low2,
                low2,
                wide,
                wide,
                wide,
                pltpu.VMEM((GROUP // LANES, 8, SEQ), F32),
            ],
        ),
        out_shape=[
            jax.ShapeDtypeStruct((3, SEQ, GROUP), BF16),
            jax.ShapeDtypeStruct(dealt, BF16),
            jax.ShapeDtypeStruct(dealt, BF16),
        ],
        compiler_params=params(60),
        cost_estimate=cost(GROUP * (40 * SEQ * SEQ + 6 * SEQ * D), 10 << 20, 4 * SEQ * SEQ),
        name="attn_backward",
    )(bounds, *saved[:4], ctx_grad, saved[4], source, cosine, sine, seg_col, seg_row, *deps)


def join_rows(index, here, there, count, columns=512):
    lead, _, wide = here.shape
    rows = D // 16
    each = 16 // count
    steps = wide // columns

    def body(idx, a, b, *outs):
        for s in range(16):
            at = pl.ds(pl.multiple_of(idx[s] * rows, 16), rows)
            total = a[0, at, :].astype(F32) + b[0, at, :].astype(F32)
            outs[s // each][s % each] = total.astype(BF16)

    whole = pl.BlockSpec((1, D, columns), lambda l, n, i: (l, 0, n))
    part = pl.BlockSpec((each, rows, columns), lambda l, n, i: (0, 0, l * steps + n))
    return pl.pallas_call(
        body,
        grid_spec=pltpu.PrefetchScalarGridSpec(
            num_scalar_prefetch=1,
            grid=(lead, steps),
            in_specs=[whole, whole],
            out_specs=[part] * count,
        ),
        out_shape=[jax.ShapeDtypeStruct((each, rows, lead * wide), BF16)] * count,
        compiler_params=params(60, ("arbitrary", "arbitrary")),
        cost_estimate=cost(D * wide * lead, 6 * D * wide * lead),
        name="join_rows",
    )(index, here, there)


def out_grad(core, ctx, right, norms):
    def body(c, *refs):
        parts, (b, nrm, mine, theirs) = refs[:GROUPS], refs[GROUPS:]
        whole = jnp.concatenate([dot_tn(p[...], b[...]) for p in parts], axis=0)
        deal(c[0], whole, mine, theirs, slice(0, D))
        flipped = jnp.concatenate([nrm[...], jnp.zeros((LANES - 8, D), F32)], axis=0).T
        filled = jnp.concatenate([flipped, jnp.zeros((D, LANES), F32)], axis=1)
        deal(c[0], filled, mine, theirs, slice(D, TAIL))

    full = lambda shape: pl.BlockSpec(shape, lambda p, b: (0,) * len(shape))
    dealt = (16, D // 32, TAIL)
    return pl.pallas_call(
        body,
        grid_spec=pltpu.PrefetchScalarGridSpec(
            num_scalar_prefetch=1,
            grid=(1,),
            in_specs=[full((SEQ, GROUP))] * GROUPS + [full((SEQ, D)), full((8, D))],
            out_specs=[full(dealt), full(dealt)],
        ),
        out_shape=[jax.ShapeDtypeStruct(dealt, BF16)] * 2,
        compiler_params=params(60),
        cost_estimate=cost(2 * SEQ * D * D, 8 << 20),
        name="out_grad",
    )(core[None], *ctx, right, norms)


def join_dealt(index, mine, there, deps=()):
    widths = [m.shape[2] for m in mine]
    wide, rows, count = sum(widths), D // 32, len(mine)

    def body(idx, *refs):
        ours, others, keep, send = refs[:count], refs[count : 2 * count], refs[-2], refs[-1]
        for s in range(16):
            start = 0
            for a, b, n in zip(ours, others, widths):
                total = a[idx[s]].astype(F32) + b[idx[s]].astype(F32)
                (keep, send)[s // 8][s % 8, :, start : start + n] = total.astype(BF16)
                start += n

    full = lambda shape: pl.BlockSpec(shape, lambda p, b: (0,) * len(shape))
    half = (8, rows, wide)
    return pl.pallas_call(
        body,
        grid_spec=pltpu.PrefetchScalarGridSpec(
            num_scalar_prefetch=1,
            grid=(1,),
            in_specs=[full((16, rows, n)) for n in widths] * 2 + [AFTER] * len(deps),
            out_specs=[full(half), full(half)],
        ),
        out_shape=[jax.ShapeDtypeStruct(half, BF16)] * 2,
        compiler_params=params(24),
        cost_estimate=cost(D * wide // 2, 3 * D * wide),
        name="join_dealt",
    )(index, *mine, *there, *deps)


def fold(keep, there, count, dtype=BF16, deps=()):
    blocks, rows, wide = keep.shape
    each = blocks // count

    def body(a, b, *rest):
        for n, out in enumerate(rest[len(deps) :]):
            at = slice(n * each, (n + 1) * each)
            out[...] = (a[at].astype(F32) + b[at].astype(F32)).astype(dtype)

    steps = 2 if blocks * rows * wide > 1 << 19 else 1
    columns = wide // steps
    part = pl.BlockSpec((blocks, rows, columns), lambda i: (0, 0, i))
    return pl.pallas_call(
        body,
        grid=(steps,),
        in_specs=[part, part] + [AFTER] * len(deps),
        out_specs=[pl.BlockSpec((each, rows, columns), lambda i: (0, 0, i))] * count,
        out_shape=[jax.ShapeDtypeStruct((each, rows, wide), dtype)] * count,
        compiler_params=params(16),
        cost_estimate=cost(blocks * rows * wide, 6 * blocks * rows * wide),
        name="fold",
    )(keep, there, *deps)


def fold_pair(keep, there, deps=()):
    rows = keep[0].shape[1]
    widths = [k.shape[2] for k in keep]
    wide = sum(widths)

    def body(a, b, c, d, *rest):
        start = 0
        for p, q, n in ((a, c, widths[0]), (b, d, widths[1])):
            for at, out in enumerate(rest[len(deps) :]):
                four = slice(4 * at, 4 * at + 4)
                total = p[four].astype(F32) + q[four].astype(F32)
                out[:, :, start : start + n] = total.astype(BF16)
            start += n

    vmem = pl.BlockSpec(memory_space=pltpu.VMEM)
    return pl.pallas_call(
        body,
        in_specs=[vmem] * 4 + [AFTER] * len(deps),
        out_specs=[vmem] * 2,
        out_shape=[jax.ShapeDtypeStruct((4, rows, wide), BF16)] * 2,
        compiler_params=params(16, None),
        cost_estimate=cost(8 * rows * wide, 48 * rows * wide),
        name="fold_pair",
    )(*keep, *there, *deps)


def finish(parts):
    rows = D // 32

    def body(a, b, c, d, qkv, out, gain, shift):
        total = a[0].astype(F32) + b[0].astype(F32) + c[0].astype(F32) + d[0].astype(F32)
        places = [0, 3 * GROUP, 6 * GROUP + TAIL]
        for i in range(3):
            at = [slice(p + i * GROUP, p + (i + 1) * GROUP) for p in places]
            qkv[:, i, :] = jnp.concatenate([total[:, p] for p in at], axis=1)
        start = 6 * GROUP
        out[...] = total[:, start : start + D]
        gain[...] = total[:, start + D : start + D + 2]
        shift[...] = total[:, start + D + 2 : start + D + 4]

    vmem = pl.BlockSpec(memory_space=pltpu.VMEM)
    shapes = [(rows, 3, D), (rows, D), (rows, 2), (rows, 2)]
    return pl.pallas_call(
        body,
        in_specs=[vmem] * 4,
        out_specs=[vmem] * 4,
        out_shape=[jax.ShapeDtypeStruct(shape, F32) for shape in shapes],
        compiler_params=params(16, None),
        cost_estimate=cost(1 << 18, 1 << 20),
        name="finish",
    )(*parts)


def input_back(core, hidden_grad, projected, weights, deps=()):
    half = SEQ // 2 // BLOCK

    def body(c, hid, a, b, d, w, *rest):
        mine, leave = rest[-2:]
        total = hid[...]
        for g, ref in enumerate((a, b, d)):
            for i in range(3):
                at = i * D + g * GROUP
                total = total + dot_nt(ref[i], w[:, at : at + GROUP])
        own = pl.program_id(0) // half == c[0]

        @pl.when(own)
        def _():
            mine[...] = total

        @pl.when(jnp.logical_not(own))
        def _():
            leave[...] = total

    row = pl.BlockSpec((BLOCK, D), lambda r, c: (r, 0))
    shape = jax.ShapeDtypeStruct((SEQ // 2, D), F32)
    return pl.pallas_call(
        body,
        grid_spec=pltpu.PrefetchScalarGridSpec(
            num_scalar_prefetch=1,
            grid=(SEQ // BLOCK,),
            in_specs=[row]
            + [pl.BlockSpec((3, BLOCK, GROUP), lambda r, c: (0, r, 0))] * 3
            + [pl.BlockSpec((D, 3 * D), lambda r, c: (0, 0))]
            + [AFTER] * len(deps),
            out_specs=[
                pl.BlockSpec((BLOCK, D), lambda r, c: (jnp.clip(r - half * c[0], 0, half - 1), 0)),
                pl.BlockSpec(
                    (BLOCK, D), lambda r, c: (jnp.clip(r - half * (1 - c[0]), 0, half - 1), 0)
                ),
            ],
        ),
        out_shape=[shape, shape],
        compiler_params=params(60),
        cost_estimate=cost(6 * SEQ * D * D, 16 << 20),
        name="input_back",
    )(core[None], hidden_grad, *projected, weights, *deps)


def middle(index, source, ctx, cot, pieces):
    def norm(v):
        center = v - jnp.mean(v, axis=1, keepdims=True)
        scale = lax.rsqrt(jnp.mean(center * center, axis=1, keepdims=True) + EPSILON)
        return center * scale, scale

    def norm_back(u, hat, scale, gain):
        g = u * gain
        return scale * (
            g - jnp.mean(g, axis=1, keepdims=True) - hat * jnp.mean(g * hat, axis=1, keepdims=True)
        )

    def body(idx, x, ctx0, ctx1, ctx2, cot, *refs):
        pieces, refs = refs[:8], refs[8:]
        out, out_leave, gu_own, gu_other, down_own, down_other, hid_out, att_out, ctxg_out, sums = refs[:10]
        (
            w, wo, tail, nrm, factors, acts, low_t, mlp_t, mlp_s, back_s, hat_s, scale_s, pair_s, sem,
        ) = refs[10:]
        step = pl.program_id(0)
        core = idx[32]
        few = D // 32

        def loads(kind, which):
            copies = []
            for rest in (2 * which, 2 * which + 1):
                for s in range(8):
                    block = idx[(0 if kind == "gate" else 33) + rest * 8 + s]
                    at = pl.ds(pl.multiple_of(block * 48, 16), 48)
                    n = rest * 8 + s
                    gate, down = pieces[rest], pieces[4 + rest]
                    if kind == "gate":
                        copies.append(
                            pltpu.make_async_copy(
                                gate.at[s], w.at[which, at, pl.ds(0, 2 * HIDDEN)], sem.at[n]
                            )
                        )
                    elif kind == "down":
                        copies.append(
                            pltpu.make_async_copy(
                                down.at[s, :, pl.ds(0, HIDDEN)],
                                w.at[which, at, pl.ds(2 * HIDDEN, HIDDEN)],
                                sem.at[32 + n],
                            )
                        )
                    else:
                        owner = core if which == 0 else 1 - core
                        for part in range(2):
                            copies.append(
                                pltpu.make_async_copy(
                                    down.at[s, pl.ds(part * few, few), pl.ds(HIDDEN, REST)],
                                    tail.at[part, block * 2 + owner],
                                    sem.at[64 + n + 32 * part],
                                )
                            )
            return copies

        def arrive(kind, which):
            @pl.when(step == 0)
            def _():
                for cp in loads(kind, which):
                    cp.wait()

        @pl.when(step == 0)
        def _():
            for which in range(2):
                for cp in loads("tail", which):
                    cp.start()
            for which in range(2):
                for kind in ("gate", "down"):
                    for cp in loads(kind, which):
                        cp.start()

        arrive("tail", 0)
        arrive("tail", 1)

        @pl.when(step == 0)
        def _():
            joined = jnp.concatenate(
                [tail[0].reshape(D, REST), tail[1].reshape(D, REST)], axis=1
            )
            wo[...] = joined[:, :D]
            nrm[...] = joined[:, D : D + LANES].astype(F32).T[:8]
            sums[...] = jnp.zeros_like(sums)

        gain1, gain2, shift1, shift2 = (nrm[i : i + 1, :] for i in range(4))

        @pl.when(step < STEPS)
        def _():
            rows = pl.ds(pl.multiple_of(step * ROWS, ROWS), ROWS)
            context = jnp.concatenate([ctx0[...], ctx1[...], ctx2[...]], axis=1)
            hidden_in = x[...].astype(F32) + dot_nn(context, wo[...])
            hat1, scale1 = norm(hidden_in)
            hat_s[rows, :] = hat1
            scale_s[rows, :] = scale1
            normed = hat1 * gain1 + shift1
            low = normed.astype(BF16)
            low_t[:, rows] = low.T
            total = normed
            for half in range(2):
                arrive("gate", half)
                arrive("down", half)
                for n in range(HIDDEN // CHUNK):
                    g_at, u_at, d_at = (pl.ds(p * HIDDEN + n * CHUNK, CHUNK) for p in range(3))
                    gate = dot_nn(low, w[half, :, g_at])
                    up = dot_nn(low, w[half, :, u_at])
                    s = jax.nn.sigmoid(gate)
                    silu = gate * s
                    act = (silu * up).astype(BF16)
                    factors[half, rows, g_at] = (up * (s * (1.0 + gate * (1.0 - s)))).astype(BF16)
                    factors[half, rows, u_at] = silu.astype(BF16)
                    acts[half, rows, g_at] = act
                    total = total + dot_nt(act, w[half, :, d_at])
            hat2, scale2 = norm(total)
            result = (hat2 * gain2 + shift2).astype(BF16)
            own = step // (STEPS // 2) == core

            @pl.when(own)
            def _():
                out[...] = result

            @pl.when(jnp.logical_not(own))
            def _():
                out_leave[...] = result

            u2 = cot[...].astype(F32)
            resid = norm_back(u2, hat2, scale2, gain2)
            mlp = resid.astype(BF16)
            mlp_s[rows, :] = mlp
            mlp_t[:, rows] = mlp.T
            back_s[rows, :] = resid
            sums[1:2, :] += jnp.sum(u2 * hat2, axis=0, keepdims=True)
            sums[3:4, :] += jnp.sum(u2, axis=0, keepdims=True)

        @pl.when(jnp.logical_and(step >= STEPS, step < STEPS + PIECES))
        def _():
            at = step - STEPS
            half = 1 - at // (PIECES // 2)
            n = at % (PIECES // 2)
            g_at, u_at, d_at = (
                pl.ds(pl.multiple_of(p * HIDDEN + n * PIECE, PIECE), PIECE) for p in range(3)
            )

            for r in range(STEPS):
                rows = pl.ds(r * ROWS, ROWS)
                grad = dot_nn(mlp_s[rows, :], w[half, :, d_at])
                gate_grad = (grad * factors[half, rows, g_at].astype(F32)).astype(BF16)
                up_grad = (grad * factors[half, rows, u_at].astype(F32)).astype(BF16)
                pair_s[0, rows, :] = gate_grad
                pair_s[1, rows, :] = up_grad
                back_s[rows, :] += dot_nt(gate_grad, w[half, :, g_at]) + dot_nt(
                    up_grad, w[half, :, u_at]
                )

            def store(gu, down):
                for i in range(2):
                    gu[i] = dot_nn(low_t[...], pair_s[i]).astype(BF16)
                down[0] = dot_nn(mlp_t[...], acts[half, :, g_at]).astype(BF16)

            @pl.when(half == 1)
            def _():
                store(gu_other, down_other)

            @pl.when(half == 0)
            def _():
                store(gu_own, down_own)

        @pl.when(step >= STEPS + PIECES)
        def _():
            r = step - STEPS - PIECES
            rows = pl.ds(pl.multiple_of(r * ROWS, ROWS), ROWS)
            back, hat1 = back_s[rows, :], hat_s[rows, :]
            hidden_grad = norm_back(back, hat1, scale_s[rows, :], gain1)
            hid_out[...] = hidden_grad
            att = hidden_grad.astype(BF16)
            att_out[...] = att
            ctxg_out[...] = dot_nt(att, wo[...]).astype(BF16)
            sums[0:1, :] += jnp.sum(back * hat1, axis=0, keepdims=True)
            sums[2:3, :] += jnp.sum(back, axis=0, keepdims=True)

    last = STEPS - 1
    row = lambda n: pl.BlockSpec((ROWS, n), lambda t, i: (jnp.minimum(t, last), 0))
    ending = pl.BlockSpec((ROWS, D), lambda t, i: (jnp.clip(t - STEPS - PIECES, 0, last), 0))
    half = STEPS // 2
    side = lambda t, mine: (jnp.clip(jnp.minimum(t, last) - half * mine, 0, half - 1), 0)
    mine = pl.BlockSpec((ROWS, D), lambda t, i: side(t, i[32]))
    leave = pl.BlockSpec((ROWS, D), lambda t, i: side(t, 1 - i[32]))
    each = PIECES // 2
    own = lambda lead: pl.BlockSpec(
        (lead, D, PIECE), lambda t, i: (0, 0, jnp.clip(t - STEPS - each, 0, each - 1))
    )
    theirs = lambda lead: pl.BlockSpec(
        (lead, D, PIECE), lambda t, i: (0, 0, jnp.clip(t - STEPS, 0, each - 1))
    )
    act = lambda n, t=BF16: jax.ShapeDtypeStruct((n, D), t)
    grads = lambda lead: jax.ShapeDtypeStruct((lead, D, HIDDEN), BF16)
    return pl.pallas_call(
        body,
        grid_spec=pltpu.PrefetchScalarGridSpec(
            num_scalar_prefetch=1,
            grid=(2 * STEPS + PIECES,),
            in_specs=[row(D)] + [row(GROUP)] * GROUPS + [row(D)] + [ANY] * 8,
            out_specs=[mine, leave, own(2), theirs(2), own(1), theirs(1)]
            + [ending] * 3
            + [pl.BlockSpec((8, D), lambda t, i: (0, 0))],
            scratch_shapes=[
                pltpu.VMEM((2, D, WIDE), BF16),
                pltpu.VMEM((D, D), BF16),
                pltpu.VMEM((2, 32, D // 32, REST), BF16),
                pltpu.VMEM((8, D), F32),
                pltpu.VMEM((2, SEQ, 2 * HIDDEN), BF16),
                pltpu.VMEM((2, SEQ, HIDDEN), BF16),
                pltpu.VMEM((D, SEQ), BF16),
                pltpu.VMEM((D, SEQ), BF16),
                pltpu.VMEM((SEQ, D), BF16),
                pltpu.VMEM((SEQ, D), F32),
                pltpu.VMEM((SEQ, D), F32),
                pltpu.VMEM((SEQ, 1), F32),
                pltpu.VMEM((2, SEQ, PIECE), BF16),
                pltpu.SemaphoreType.DMA((128,)),
            ],
        ),
        out_shape=[
            act(SEQ // 2),
            act(SEQ // 2),
            grads(2),
            grads(2),
            grads(1),
            grads(1),
            act(SEQ, F32),
            act(SEQ),
            act(SEQ),
            jax.ShapeDtypeStruct((8, D), F32),
        ],
        compiler_params=params(62),
        cost_estimate=cost(18 * SEQ * D * 2 * HIDDEN + 4 * SEQ * D * D, 40 << 20, 4 * SEQ * HIDDEN),
        name="middle",
    )(index, source, *ctx, cot, *pieces)


def rotary_lanes(segment_row):
    labels = jnp.arange(NDOC + 1, dtype=jnp.int32)
    before = jnp.sum((segment_row[None, :] < labels[:, None]).astype(jnp.int32), axis=1)
    member = segment_row[:, None] == labels[None, :]
    first = jnp.sum(jnp.where(member, before[None, :], 0), axis=1)
    position = (jnp.arange(SEQ, dtype=jnp.int32) - first).astype(F32)
    lane = jnp.arange(LANES) % (HEAD // 2)
    frequency = jnp.power(F32(1000.0), -2.0 * lane.astype(F32) / HEAD)
    angle = position[:, None] * frequency[None, :]
    sign = jnp.where(jnp.arange(LANES) % HEAD < HEAD // 2, -1.0, 1.0)
    ends = jnp.concatenate([before[1:], jnp.full((1,), SEQ, jnp.int32)])
    heads = segment_row[::BLOCK]
    tails = segment_row[BLOCK - 1 :: BLOCK]
    low = jnp.sum(jnp.where(heads[:, None] == labels[None, :], before[None, :], 0), axis=1)
    high = jnp.sum(jnp.where(tails[:, None] == labels[None, :], ends[None, :], 0), axis=1)
    bounds = jnp.concatenate([low // KEYS, (high + KEYS - 1) // KEYS]).astype(jnp.int32)
    return jnp.cos(angle), jnp.sin(angle) * sign[None, :], bounds


def sequence_device(
    tokens, segments, qkv_weight, out_weight, norm_gain, norm_shift, gate_up, down_weight, cotangent
):
    core = lax.axis_index("tensor")
    def ordered(mine, theirs):
        return jnp.where(
            core == 0, jnp.stack([mine, theirs], axis=0), jnp.stack([theirs, mine], axis=0)
        )

    pick = lambda a, i: lax.dynamic_index_in_dim(a, i, 0, keepdims=False)
    source = pick(tokens, core)
    segment_row = pick(segments, core)

    attn_block = qkv_weight.reshape(-1, 3 * D)
    gate_block = gate_up.reshape(-1, 2 * HIDDEN)
    tail_block = jnp.concatenate(
        [out_weight, norm_gain, norm_shift, jnp.zeros((D // 32, TAIL - D - 4), BF16)], axis=1
    )
    down_block = jnp.concatenate(
        [down_weight, jnp.concatenate([tail_block[:, :REST], tail_block[:, REST:]], axis=0)], axis=1
    )
    from_here, from_there = slot_blocks(-1, core), slot_blocks(-1, 1 - core)
    there_blocks = slot_blocks(1, core).reshape(2, 2, 4)
    to_here = there_blocks.transpose(1, 0, 2).reshape(16)
    deep_first = there_blocks.transpose(2, 1, 0).reshape(16)

    cot = ordered(pick(cotangent, core), core_swap(pick(cotangent, 1 - core))).reshape(SEQ, D)
    cosine, sine, bounds = rotary_lanes(segment_row)
    bounds = jnp.concatenate([bounds, core[None]]).astype(jnp.int32)
    tables = (cosine, sine, segment_row[:, None], segment_row[None, :])

    ahead = lambda parts: [part[None] for part in parts]
    gate_parts = depth_ring(gate_block)
    attn_four = pile(ahead(depth_parts(attn_block)), deps=(gate_parts[1],))
    attn_eight = pile(
        [attn_four, first_swap(attn_four)], deps=(gate_parts[2], source, cot, *tables)
    )
    attn_last = second_swap(attn_eight)
    index = jnp.concatenate([from_here * 2 + core, from_there * 2 + 1 - core]).astype(jnp.int32)
    weights = assemble(
        (attn_eight, attn_last),
        (core_swap(attn_eight), core_swap(attn_last)),
        index,
        deps=(gate_parts[3],),
    ).reshape(D, 3 * D)
    gate_four = pile(ahead(gate_parts))
    down_pair = pile([down_block[None], first_swap(down_block)[None]], deps=(gate_four,))
    saved0 = attn_forward(0, 1, bounds, source, weights, *tables, deps=(gate_four, down_pair))
    gate_eight = pile([gate_four, first_swap(gate_four)], deps=(saved0[4],))
    gate_last = second_swap(gate_eight)
    saved1 = attn_forward(1, 1, bounds, source, weights, *tables, deps=(gate_eight,))
    down_eight = pile(depth_parts(down_pair), deps=(saved1[4],))
    saved2 = attn_forward(2, 1, bounds, source, weights, *tables, deps=(down_eight,))
    down_last, late_logs = lax.optimization_barrier((second_swap(down_eight), saved2[4]))
    saved2 = (*saved2[:4], late_logs)
    pieces = (gate_eight, gate_last, core_swap(gate_eight), core_swap(gate_last))
    pieces += (down_eight, down_last, core_swap(down_eight), core_swap(down_last))

    turned = lambda slots: slots.reshape(2, 2, 4).transpose(0, 2, 1).reshape(16)
    index = jnp.concatenate(
        [from_here, from_there, core[None], turned(from_here), turned(from_there)]
    ).astype(jnp.int32)
    ctx = (saved0[3], saved1[3], saved2[3])
    (out, out_leave, gu_here, gu_there, down_here, down_there, hidden_grad, att_grad, ctx_grad, sums) = (
        middle(index, source, ctx, cot, pieces)
    )

    down_there, gu_there = core_swap(down_there), core_swap(gu_there)
    tail_mine, tail_theirs = out_grad(core, ctx, att_grad, sums)
    down_parts = join_rows(deep_first, down_here, down_there, 4)
    gu_keep, gu_send = join_rows(to_here, gu_here, gu_there, 2)
    gu_first = first_swap(gu_send)
    passing = depth_shift(down_parts[3], 1)

    common = (source,) + tables
    back0 = attn_backward(0, 0, bounds, saved0, ctx_grad, *common, deps=(gu_send, down_parts[0]))
    (passing,) = fold(passing, down_parts[2], 1, deps=(back0[1],))
    back1 = attn_backward(0, 1, bounds, saved1, ctx_grad, *common, deps=(passing,))
    passing = depth_shift(passing, 1)
    (passing,) = fold(passing, down_parts[1], 1, deps=(back1[1],))
    gu_keep, gu_send = fold(gu_keep, gu_first, 2, deps=(back1[1],))
    gu_second = second_swap(gu_send)
    early_keep, early_send = join_dealt(
        to_here,
        (back0[1], back1[1], tail_mine),
        (core_swap(back0[2]), core_swap(back1[2]), core_swap(tail_theirs)),
    )
    early_first = first_swap(early_send)
    back2 = attn_backward(0, 2, bounds, saved2, ctx_grad, *common, deps=(gu_send, early_send, passing))

    deep = lambda parts: [parts[0]] + [depth_shift(parts[k], k) for k in (1, 2, 3)]
    passing = depth_shift(passing, 1)
    gu_parts = fold(gu_keep, gu_second, 4, deps=(back2[1],))
    (gu_total,) = fold(depth_shift(gu_parts[3], 1), gu_parts[2], 1)
    down_keep, down_send = fold(passing, down_parts[0], 2, deps=(gu_parts[0],))
    down_keep, down_send = fold(down_keep, first_swap(down_send), 2)
    down_second = second_swap(down_send)
    late_keep, late_send = join_dealt(
        to_here, (back2[1],), (core_swap(back2[2]),), deps=(down_keep, early_first)
    )
    grad, grad_leave = input_back(
        core, hidden_grad, (back0[0], back1[0], back2[0]), weights, deps=(late_send, gu_total)
    )
    (gu_total,) = fold(depth_shift(gu_total, 1), gu_parts[1], 1, deps=(grad,))
    attn_keep, attn_send = fold_pair(
        (early_keep, late_keep), (early_first, first_swap(late_send)), deps=(gu_total,)
    )
    attn_second = second_swap(attn_send)
    outputs = place(core, out, core_swap(out_leave)), place(core, grad, core_swap(grad_leave))
    (gu_total,) = fold(depth_shift(gu_total, 1), gu_parts[0], 1, F32, deps=(attn_send,))
    attn_parts = deep(fold(attn_keep, attn_second, 4, deps=(gu_total, *outputs)))
    down_total = (down_keep.astype(F32) + down_second.astype(F32))[0]
    gu_total = gu_total[0]
    qkv_total, out_total, gain_total, shift_total = finish(attn_parts)

    return (
        *outputs,
        qkv_total,
        out_total,
        gain_total,
        shift_total,
        gu_total.reshape(-1, 2, HIDDEN),
        down_total,
    )


def solution(mesh):
    in_specs = (
        P("dp", None, None),
        P("dp", None),
        P(("dp", "tensor"), None, None),
        P(("dp", "tensor"), None),
        P(("dp", "tensor"), None),
        P(("dp", "tensor"), None),
        P("dp", None, "tensor"),
        P("dp", "tensor"),
        P("dp", "tensor", None),
    )
    out_specs = (
        P("dp", "tensor", None),
        P("dp", "tensor", None),
        P(("dp", "tensor"), None, None),
        P(("dp", "tensor"), None),
        P(("dp", "tensor"), None),
        P(("dp", "tensor"), None),
        P("dp", None, "tensor"),
        P("dp", "tensor"),
    )
    sizes = dict(mesh.shape)

    def per_device(tokens, *others):
        if sizes["dp"] == 16 and sizes["tensor"] == 2 and tokens.shape[0] == 2:
            return sequence_device(tokens, *others)
        return general_device(tokens, *others)

    return jax.shard_map(
        per_device, mesh=mesh, in_specs=in_specs, out_specs=out_specs, check_vma=False
    )
```

profile of v0, /device:TPU:0, one launch (start us, length us, event | category | flops | bytes accessed | tf_op | source)
XLA Modules:
  0.0 406.8 jit_solution(144430718621596264)
XLA Ops:
  1.6 5.0 %collective-permute-start.2 = (bf16[24,2304]{1,0:T(8,128)(2,1)S(1)}, bf16[24,2304]{1,0:T(8,128)(2,1)S(1)}, u32[]{:S(2)}, u32[]{:S(2)}) collective-permute-start(bf16[24,2304]{1,0:T(8,128)(2,1)S(1)} %bitcast.51), channel_id=1, source_target_pairs={{0,24},{1,25},{2,26},{3,27},{4,28},{5,29},{6,30},{7,31},{8,0},{9,1... | collective-permute-start | bytes 331784 | tf_op jit(solution)/shard_map/ppermute | solution.py:269
  8.6 2.5 collective-permute-start.3
  11.2 2.6 constant_dynamic-slice_fusion
  14.5 8.1 %collective-permute-done.1 = bf16[24,2304]{1,0:T(8,128)(2,1)S(1)} collective-permute-done((bf16[24,2304]{1,0:T(8,128)(2,1)S(1)}, bf16[24,2304]{1,0:T(8,128)(2,1)S(1)}, u32[]{:S(2)}, u32[]{:S(2)}) %collective-permute-start.1) | collective-permute-done | bytes 110624 | tf_op jit(solution)/shard_map/ppermute | solution.py:269
  28.9 2.2 maximum_select_fusion
  31.1 5.5 %collective-permute-done.5.refs_2_ = bf16[48,3072]{1,0:T(8,128)(2,1)S(1)} collective-permute-done((bf16[48,3072]{1,0:T(8,128)(2,1)S(1)}, bf16[48,3072]{1,0:T(8,128)(2,1)S(1)}, u32[]{:S(2)}, u32[]{:S(2)}) %collective-permute-start.5) | collective-permute-done | bytes 294944 | tf_op jit(solution)/shard_map/ppermute | solution.py:269
  42.0 10.5 %collective-permute-done.7.b = bf16[8,24,2304]{2,1,0:T(8,128)(2,1)} collective-permute-done((bf16[8,24,2304]{2,1,0:T(8,128)(2,1)S(1)}, bf16[8,24,2304]{2,1,0:T(8,128)(2,1)}, u32[]{:S(2)}, u32[]{:S(2)}) %collective-permute-start.7) | collective-permute-done | bytes 884768 | tf_op jit(solution)/shard_map/ppermute | solution.py:269
  58.6 4.8 %assemble.1 = bf16[32,24,2304]{2,1,0:T(8,128)(2,1)} custom-call(s32[32]{0:T(128)} %pad_add_fusion.2.idx, bf16[8,24,2304]{2,1,0:T(8,128)(2,1)} %copy-done.12, bf16[8,24,2304]{2,1,0:T(8,128)(2,1)} %collective-permute-done.7.b, bf16[8,24,2304]{2,1,0:T(8,128)(2,1)} %copy-done.48, bf16[8,24,2304]{2,1,0:T(8,128)(2,1)} %collective-permute-done.9.d, ...), custom_call_target="tpu_custom_call" | custom-call | bytes 7077888 | tf_op jit(solution)/shard_map/assemble/pallas_call | solution.py:391
  63.4 13.7 %attn_forward.3 = (bf16[1024,256]{1,0:T(8,128)(2,1)}, bf16[1024,256]{1,0:T(8,128)(2,1)}, bf16[1024,256]{1,0:T(8,128)(2,1)}, bf16[1024,256]{1,0:T(8,128)(2,1)}, f32[1,8,1024]{2,1,0:T(8,128)}) custom-call(s32[9]{0:T(128)} %pad_add_fusion.1.bnd, bf16[1024,768]{1,0:T(8,128)(2,1)} %copy-done.7, bf16[768,2304]{1,0:T(8,128)(2,1)} %bitcast.38, ...), custom_call_target="tpu_custom_call" | custom-call | flops 5502926848 | bytes 8388608 | tf_op jit(solution)/shard_map/attn_forward/pallas_call | solution.py:492
  84.5 13.8 %attn_forward.4 = (bf16[1024,256]{1,0:T(8,128)(2,1)}, bf16[1024,256]{1,0:T(8,128)(2,1)}, bf16[1024,256]{1,0:T(8,128)(2,1)}, bf16[1024,256]{1,0:T(8,128)(2,1)}, f32[1,8,1024]{2,1,0:T(8,128)}) custom-call(s32[9]{0:T(128)} %pad_add_fusion.1.bnd, bf16[1024,768]{1,0:T(8,128)(2,1)} %copy-done.7, bf16[768,2304]{1,0:T(8,128)(2,1)} %bitcast.41, ...), custom_call_target="tpu_custom_call" | custom-call | flops 5502926848 | bytes 8388608 | tf_op jit(solution)/shard_map/attn_forward/pallas_call | solution.py:492
  98.3 18.5 %collective-permute-done.14.refs_2_ = bf16[2,48,2048]{2,1,0:T(8,128)(2,1)S(1)} collective-permute-done((bf16[2,48,2048]{2,1,0:T(8,128)(2,1)S(1)}, bf16[2,48,2048]{2,1,0:T(8,128)(2,1)S(1)}, u32[]{:S(2)}, u32[]{:S(2)}) %collective-permute-start.14) | collective-permute-done | bytes 393248 | tf_op jit(solution)/shard_map/ppermute | solution.py:269
  120.5 13.7 %attn_forward.5 = (bf16[1024,256]{1,0:T(8,128)(2,1)}, bf16[1024,256]{1,0:T(8,128)(2,1)}, bf16[1024,256]{1,0:T(8,128)(2,1)}, bf16[1024,256]{1,0:T(8,128)(2,1)}, f32[1,8,1024]{2,1,0:T(8,128)}) custom-call(s32[9]{0:T(128)} %pad_add_fusion.1.bnd, bf16[1024,768]{1,0:T(8,128)(2,1)} %copy-done.7, bf16[768,2304]{1,0:T(8,128)(2,1)} %bitcast.44, ...), custom_call_target="tpu_custom_call" | custom-call | flops 5502926848 | bytes 8388608 | tf_op jit(solution)/shard_map/attn_forward/pallas_call | solution.py:492
  134.2 4.7 %collective-permute-done.19.refs_5_ = bf16[8,48,2048]{2,1,0:T(8,128)(2,1)} collective-permute-done((bf16[8,48,2048]{2,1,0:T(8,128)(2,1)S(1)}, bf16[8,48,2048]{2,1,0:T(8,128)(2,1)}, u32[]{:S(2)}, u32[]{:S(2)}) %collective-permute-start.19) | collective-permute-done | bytes 1572896 | tf_op jit(solution)/shard_map/ppermute | solution.py:269
  139.6 3.0 collective-permute-done.21.refs_7_
  142.6 90.8 %middle.1 = (bf16[512,768]{1,0:T(8,128)(2,1)}, bf16[512,768]{1,0:T(8,128)(2,1)}, bf16[2,768,1536]{2,1,0:T(8,128)(2,1)}, bf16[2,768,1536]{2,1,0:T(8,128)(2,1)}, b...) custom-call(s32[65]{0:T(128)} %concatenate.21.idx, ...), custom_call_target="tpu_custom_call" | custom-call | flops 45902462976 | bytes 41943040 | tf_op jit(solution)/shard_map/middle/pallas_call | solution.py:1037
  235.3 4.4 %out_grad.1 = (bf16[16,24,1024]{2,1,0:T(8,128)(2,1)}, bf16[16,24,1024]{2,1,0:T(8,128)(2,1)}) custom-call(s32[1]{0:T(128)} %bitcast.c, bf16[1024,256]{1,0:T(8,128)(2,1)} %get-tuple-element.78.ctx0.o.refs_0_, bf16[1024,256]{1,0:T(8,128)(2,1)} %get-tuple-element.80.ctx1.o.refs_1_, bf16[1024,256]{1,0:T(8,128)(2,1)} %get-tuple-element.82.ctx2.refs_2_.o, ...), custom_call_target="tpu_custom_call" | custom-call | flops 1207959552 | bytes 8388608 | tf_op jit(solution)/shard_map/out_grad/pallas_call | solution.py:675
  239.9 5.2 %collective-permute-done.24.b = bf16[1,768,1536]{2,1,0:T(8,128)(2,1)S(1)} collective-permute-done((bf16[1,768,1536]{2,1,0:T(8,128)(2,1)}, bf16[1,768,1536]{2,1,0:T(8,128)(2,1)S(1)}, u32[]{:S(2)}, u32[]{:S(2)}) %collective-permute-start.24) | collective-permute-done | bytes 2359328 | tf_op jit(solution)/shard_map/ppermute | solution.py:269
  246.6 5.2 %join_rows.3 = (bf16[4,48,1536]{2,1,0:T(8,128)(2,1)}, bf16[4,48,1536]{2,1,0:T(8,128)(2,1)}, bf16[4,48,1536]{2,1,0:T(8,128)(2,1)}, bf16[4,48,1536]{2,1,0:T(8,128)(2,1)}) custom-call(s32[16]{0:T(128)} %fusion.21.idx, bf16[1,768,1536]{2,1,0:T(8,128)(2,1)} %get-tuple-element.95.a, bf16[1,768,1536]{2,1,0:T(8,128)(2,1)} %copy-done.47), custom_call_target="tpu_custom_call" | custom-call | flops 1179648 | bytes 7077888 | tf_op jit(solution)/shard_map/join_rows/pallas_call | solution.py:649
  252.8 8.1 %join_rows.2 = (bf16[8,48,3072]{2,1,0:T(8,128)(2,1)}, bf16[8,48,3072]{2,1,0:T(8,128)(2,1)}) custom-call(s32[16]{0:T(128)} %fusion.16.idx, bf16[2,768,1536]{2,1,0:T(8,128)(2,1)} %get-tuple-element.92.a, bf16[2,768,1536]{2,1,0:T(8,128)(2,1)} %collective-permute-done.23.b), custom_call_target="tpu_custom_call" | custom-call | flops 2359296 | bytes 14155776 | tf_op jit(solution)/shard_map/join_rows/pallas_call | solution.py:649
  261.3 18.1 %attn_backward.3 = (bf16[3,1024,256]{2,1,0:T(8,128)(2,1)}, bf16[16,24,768]{2,1,0:T(8,128)(2,1)}, bf16[16,24,768]{2,1,0:T(8,128)(2,1)}) custom-call(s32[9]{0:T(128)} %pad_add_fusion.1.bnd, bf16[1024,256]{1,0:T(8,128)(2,1)} %get-tuple-element.88.q, bf16[1024,256]{1,0:T(8,128)(2,1)} %get-tuple-element.89.k, bf16[1024,256]{1,0:T(8,128)(2,1)} %get-tuple-element.90.v, ...), custom_call_target="tpu_custom_call" | custom-call | flops 11945377792 | bytes 10485760 | tf_op jit(solution)/shard_map/attn_backward/pallas_call | solution.py:598
  281.7 3.1 collective-permute-start.30
  284.8 18.3 %attn_backward.4 = (bf16[3,1024,256]{2,1,0:T(8,128)(2,1)}, bf16[16,24,768]{2,1,0:T(8,128)(2,1)}, bf16[16,24,768]{2,1,0:T(8,128)(2,1)}) custom-call(s32[9]{0:T(128)} %pad_add_fusion.1.bnd, bf16[1024,256]{1,0:T(8,128)(2,1)} %get-tuple-element.99.q, bf16[1024,256]{1,0:T(8,128)(2,1)} %get-tuple-element.100.k, bf16[1024,256]{1,0:T(8,128)(2,1)} %get-tuple-element.101.v, ...), custom_call_target="tpu_custom_call" | custom-call | flops 11945377792 | bytes 10485760 | tf_op jit(solution)/shard_map/attn_backward/pallas_call | solution.py:598
  307.4 3.3 join_dealt.2
  316.5 18.0 %attn_backward.5 = (bf16[3,1024,256]{2,1,0:T(8,128)(2,1)}, bf16[16,24,768]{2,1,0:T(8,128)(2,1)}, bf16[16,24,768]{2,1,0:T(8,128)(2,1)}) custom-call(s32[9]{0:T(128)} %pad_add_fusion.1.bnd, bf16[1024,256]{1,0:T(8,128)(2,1)} %get-tuple-element.106.q, bf16[1024,256]{1,0:T(8,128)(2,1)} %get-tuple-element.107.k, bf16[1024,256]{1,0:T(8,128)(2,1)} %get-tuple-element.108.v, ...), custom_call_target="tpu_custom_call" | custom-call | flops 11945377792 | bytes 10485760 | tf_op jit(solution)/shard_map/attn_backward/pallas_call | solution.py:598
  334.6 2.7 collective-permute-done.33.b
  343.6 6.6 %collective-permute-done.36.a = bf16[1,48,3072]{2,1,0:T(8,128)(2,1)S(1)} collective-permute-done((bf16[1,48,3072]{2,1,0:T(8,128)(2,1)S(1)}, bf16[1,48,3072]{2,1,0:T(8,128)(2,1)S(1)}, u32[]{:S(2)}, u32[]{:S(2)}) %collective-permute-start.36) | collective-permute-done | bytes 294944 | tf_op jit(solution)/shard_map/ppermute | solution.py:269
  352.5 9.5 %input_back.1 = (f32[512,768]{1,0:T(8,128)}, f32[512,768]{1,0:T(8,128)}) custom-call(s32[1]{0:T(128)} %bitcast.c, f32[1024,768]{1,0:T(8,128)} %get-tuple-element.87.hid, bf16[3,1024,256]{2,1,0:T(8,128)(2,1)} %get-tuple-element.98.a, bf16[3,1024,256]{2,1,0:T(8,128)(2,1)} %get-tuple-element.105.b, bf16[3,1024,256]{2,1,0:T(8,128)(2,1)} %get-tuple-element.121.d, ...), custom_call_target="tpu_custom_call" | custom-call | flops 3623878656 | bytes 16777216 | tf_op jit(solution)/shard_map/input_back/pallas_call | solution.py:819
  363.0 10.2 %collective-permute-done.39.a = bf16[1,48,3072]{2,1,0:T(8,128)(2,1)S(1)} collective-permute-done((bf16[1,48,3072]{2,1,0:T(8,128)(2,1)S(1)}, bf16[1,48,3072]{2,1,0:T(8,128)(2,1)S(1)}, u32[]{:S(2)}, u32[]{:S(2)}) %collective-permute-start.39) | collective-permute-done | bytes 294944 | tf_op jit(solution)/shard_map/ppermute | solution.py:269
  378.4 7.4 %collective-permute-done.41.a = bf16[1,48,3072]{2,1,0:T(8,128)(2,1)S(1)} collective-permute-done((bf16[1,48,3072]{2,1,0:T(8,128)(2,1)S(1)}, bf16[1,48,3072]{2,1,0:T(8,128)(2,1)S(1)}, u32[]{:S(2)}, u32[]{:S(2)}) %collective-permute-start.41) | collective-permute-done | bytes 294944 | tf_op jit(solution)/shard_map/ppermute | solution.py:269
  390.6 3.7 collective-permute-start.44
  396.3 3.2 collective-permute-done.42.b
  399.6 4.3 %collective-permute-done.43.c = bf16[1,24,3328]{2,1,0:T(8,128)(2,1)S(1)} collective-permute-done((bf16[1,24,3328]{2,1,0:T(8,128)(2,1)}, bf16[1,24,3328]{2,1,0:T(8,128)(2,1)S(1)}, u32[]{:S(2)}, u32[]{:S(2)}) %collective-permute-start.43) | collective-permute-done | bytes 159776 | tf_op jit(solution)/shard_map/ppermute | solution.py:269
  (250 shorter events, 74.3 us)
Async XLA Ops:
  6.6 16.0 %collective-permute-start.1 = (bf16[24,2304]{1,0:T(8,128)(2,1)S(1)}, bf16[24,2304]{1,0:T(8,128)(2,1)S(1)}, u32[]{:S(2)}, u32[]{:S(2)}) collective-permute-start(bf16[24,2304]{1,0:T(8,128)(2,1)S(1)} %bitcast.52), channel_id=1, source_target_pairs={{0,16},{1,17},{2,18},{3,19},{4,20},{5,21},{6,22},{7,23},{8,24},{9,... | collective-permute-start | bytes 331784 | tf_op jit(solution)/shard_map/ppermute | solution.py:269
  6.6 16.0 %collective-permute-start = (bf16[24,2304]{1,0:T(8,128)(2,1)S(1)}, bf16[24,2304]{1,0:T(8,128)(2,1)S(1)}, u32[]{:S(2)}, u32[]{:S(2)}) collective-permute-start(bf16[24,2304]{1,0:T(8,128)(2,1)S(1)} %bitcast.53), channel_id=1, source_target_pairs={{0,8},{1,9},{2,10},{3,11},{4,12},{5,13},{6,14},{7,15},{8,16},{9,17... | collective-permute-start | bytes 331784 | tf_op jit(solution)/shard_map/ppermute | solution.py:269
  8.6 14.0 %collective-permute-start.3 = (bf16[48,3072]{1,0:T(8,128)(2,1)S(1)}, bf16[48,3072]{1,0:T(8,128)(2,1)S(1)}, u32[]{:S(2)}, u32[]{:S(2)}) collective-permute-start(bf16[48,3072]{1,0:T(8,128)(2,1)S(1)} %bitcast.50), channel_id=1, source_target_pairs={{0,8},{1,9},{2,10},{3,11},{4,12},{5,13},{6,14},{7,15},{8,16},{9,17... | collective-permute-start | bytes 884744 | tf_op jit(solution)/shard_map/ppermute | solution.py:269
  13.8 15.1 %collective-permute-start.6 = (bf16[512,768]{1,0:T(8,128)(2,1)}, bf16[512,768]{1,0:T(8,128)(2,1)}, u32[]{:S(2)}, u32[]{:S(2)}) collective-permute-start(bf16[512,768]{1,0:T(8,128)(2,1)} %get-tuple-element.181), channel_id=1, source_target_pairs={{0,1},{1,0},{2,3},{3,2},{4,5},{5,4},{6,7},{7,6},{8,9},{9,8},{10,11... | collective-permute-start | bytes 2359304 | tf_op jit(solution)/shard_map/ppermute | solution.py:269
  37.2 15.3 %collective-permute-start.7 = (bf16[8,24,2304]{2,1,0:T(8,128)(2,1)S(1)}, bf16[8,24,2304]{2,1,0:T(8,128)(2,1)}, u32[]{:S(2)}, u32[]{:S(2)}) collective-permute-start(bf16[8,24,2304]{2,1,0:T(8,128)(2,1)S(1)} %pile.7.a), channel_id=1, source_target_pairs={{0,4},{1,3},{2,6},{3,1},{4,0},{5,7},{6,2},{7,5},{8,12},{9,11},{10,... | collective-permute-start | bytes 2654216 | tf_op jit(solution)/shard_map/ppermute | solution.py:269
  38.1 14.6 %collective-permute-start.10 = (bf16[48,3072]{1,0:T(8,128)(2,1)S(1)}, bf16[48,3072]{1,0:T(8,128)(2,1)S(1)}, u32[]{:S(2)}, u32[]{:S(2)}) collective-permute-start(bf16[48,3072]{1,0:T(8,128)(2,1)S(1)} %collective-permute-done.5.refs_2_), channel_id=1, source_target_pairs={{0,8},{1,9},{2,10},{3,11},{4,12},{5,13},{6,14},{7,15},{8,16},{9,17... | collective-permute-start | bytes 884744 | tf_op jit(solution)/shard_map/ppermute | solution.py:269
  38.9 16.7 %collective-permute-start.11 = (bf16[48,2048]{1,0:T(8,128)(2,1)}, bf16[48,2048]{1,0:T(8,128)(2,1)}, u32[]{:S(2)}, u32[]{:S(2)}) collective-permute-start(bf16[48,2048]{1,0:T(8,128)(2,1)} %get-tuple-element.182), channel_id=1, source_target_pairs={{0,2},{1,5},{2,0},{3,7},{4,6},{5,1},{6,4},{7,3},{8,10},{9,13},{10,... | collective-permute-start | bytes 589832 | tf_op jit(solution)/shard_map/ppermute | solution.py:269
  41.9 15.7 %collective-permute-start.8 = (bf16[8,24,2304]{2,1,0:T(8,128)(2,1)S(1)}, bf16[8,24,2304]{2,1,0:T(8,128)(2,1)S(1)}, u32[]{:S(2)}, u32[]{:S(2)}) collective-permute-start(bf16[8,24,2304]{2,1,0:T(8,128)(2,1)S(1)} %pile.7.a), channel_id=1, source_target_pairs={{0,1},{1,0},{2,3},{3,2},{4,5},{5,4},{6,7},{7,6},{8,9},{9,8},{10,11... | collective-permute-start | bytes 2654216 | tf_op jit(solution)/shard_map/ppermute | solution.py:269
  53.1 24.1 %collective-permute-start.12 = (bf16[4,48,3072]{2,1,0:T(8,128)(2,1)S(1)}, bf16[4,48,3072]{2,1,0:T(8,128)(2,1)S(1)}, u32[]{:S(2)}, u32[]{:S(2)}) collective-permute-start(bf16[4,48,3072]{2,1,0:T(8,128)(2,1)S(1)} %pile.8.refs_2_.rest_0_.refs_0_), channel_id=1, source_target_pairs={{0,2},{1,5},{2,0},{3,7},{4,6},{5,1},{6,4},{7,3},{8,10},{9,13},{10,... | collective-permute-start | bytes 3538952 | tf_op jit(solution)/shard_map/ppermute | solution.py:269
  81.1 38.8 %collective-permute-start.16 = (bf16[8,48,3072]{2,1,0:T(8,128)(2,1)}, bf16[8,48,3072]{2,1,0:T(8,128)(2,1)}, u32[]{:S(2)}, u32[]{:S(2)}) collective-permute-start(bf16[8,48,3072]{2,1,0:T(8,128)(2,1)} %pile.10.rest_0_.refs_0_), channel_id=1, source_target_pairs={{0,4},{1,3},{2,6},{3,1},{4,0},{5,7},{6,2},{7,5},{8,12},{9,11},{10,... | collective-permute-start | bytes 7077896 | tf_op jit(solution)/shard_map/ppermute | solution.py:269
  81.2 17.0 %collective-permute-start.15 = (bf16[2,48,2048]{2,1,0:T(8,128)(2,1)S(1)}, bf16[2,48,2048]{2,1,0:T(8,128)(2,1)S(1)}, u32[]{:S(2)}, u32[]{:S(2)}) collective-permute-start(bf16[2,48,2048]{2,1,0:T(8,128)(2,1)S(1)} %copy-done.23), channel_id=1, source_target_pairs={{0,24},{1,25},{2,26},{3,27},{4,28},{5,29},{6,30},{7,31},{8,0},{9,1... | collective-permute-start | bytes 1179656 | tf_op jit(solution)/shard_map/ppermute | solution.py:269
  82.3 34.4 %collective-permute-start.14 = (bf16[2,48,2048]{2,1,0:T(8,128)(2,1)S(1)}, bf16[2,48,2048]{2,1,0:T(8,128)(2,1)S(1)}, u32[]{:S(2)}, u32[]{:S(2)}) collective-permute-start(bf16[2,48,2048]{2,1,0:T(8,128)(2,1)S(1)} %copy-done.23), channel_id=1, source_target_pairs={{0,16},{1,17},{2,18},{3,19},{4,20},{5,21},{6,22},{7,23},{8,24},{9,... | collective-permute-start | bytes 1179656 | tf_op jit(solution)/shard_map/ppermute | solution.py:269
  82.3 34.4 %collective-permute-start.13 = (bf16[2,48,2048]{2,1,0:T(8,128)(2,1)S(1)}, bf16[2,48,2048]{2,1,0:T(8,128)(2,1)S(1)}, u32[]{:S(2)}, u32[]{:S(2)}) collective-permute-start(bf16[2,48,2048]{2,1,0:T(8,128)(2,1)S(1)} %copy-done.23), channel_id=1, source_target_pairs={{0,8},{1,9},{2,10},{3,11},{4,12},{5,13},{6,14},{7,15},{8,16},{9,17... | collective-permute-start | bytes 1179656 | tf_op jit(solution)/shard_map/ppermute | solution.py:269
  118.3 20.6 %collective-permute-start.19 = (bf16[8,48,2048]{2,1,0:T(8,128)(2,1)S(1)}, bf16[8,48,2048]{2,1,0:T(8,128)(2,1)}, u32[]{:S(2)}, u32[]{:S(2)}) collective-permute-start(bf16[8,48,2048]{2,1,0:T(8,128)(2,1)S(1)} %pile.11.rest_0_.refs_4_), channel_id=1, source_target_pairs={{0,4},{1,3},{2,6},{3,1},{4,0},{5,7},{6,2},{7,5},{8,12},{9,11},{10,... | collective-permute-start | bytes 4718600 | tf_op jit(solution)/shard_map/ppermute | solution.py:269
  120.0 19.7 %collective-permute-start.17 = (bf16[8,48,3072]{2,1,0:T(8,128)(2,1)}, bf16[8,48,3072]{2,1,0:T(8,128)(2,1)}, u32[]{:S(2)}, u32[]{:S(2)}) collective-permute-start(bf16[8,48,3072]{2,1,0:T(8,128)(2,1)} %pile.10.rest_0_.refs_0_), channel_id=1, source_target_pairs={{0,1},{1,0},{2,3},{3,2},{4,5},{5,4},{6,7},{7,6},{8,9},{9,8},{10,11... | collective-permute-start | bytes 7077896 | tf_op jit(solution)/shard_map/ppermute | solution.py:269
  120.0 22.7 %collective-permute-start.18 = (bf16[8,48,3072]{2,1,0:T(8,128)(2,1)}, bf16[8,48,3072]{2,1,0:T(8,128)(2,1)}, u32[]{:S(2)}, u32[]{:S(2)}) collective-permute-start(bf16[8,48,3072]{2,1,0:T(8,128)(2,1)} %collective-permute-done.16.refs_1_), channel_id=1, source_target_pairs={{0,1},{1,0},{2,3},{3,2},{4,5},{5,4},{6,7},{7,6},{8,9},{9,8},{10,11... | collective-permute-start | bytes 7077896 | tf_op jit(solution)/shard_map/ppermute | solution.py:269
  120.5 19.1 %collective-permute-start.20 = (bf16[8,48,2048]{2,1,0:T(8,128)(2,1)S(1)}, bf16[8,48,2048]{2,1,0:T(8,128)(2,1)}, u32[]{:S(2)}, u32[]{:S(2)}) collective-permute-start(bf16[8,48,2048]{2,1,0:T(8,128)(2,1)S(1)} %pile.11.rest_0_.refs_4_), channel_id=1, source_target_pairs={{0,1},{1,0},{2,3},{3,2},{4,5},{5,4},{6,7},{7,6},{8,9},{9,8},{10,11... | collective-permute-start | bytes 4718600 | tf_op jit(solution)/shard_map/ppermute | solution.py:269
  233.5 19.4 %collective-permute-start.23 = (bf16[2,768,1536]{2,1,0:T(8,128)(2,1)}, bf16[2,768,1536]{2,1,0:T(8,128)(2,1)}, u32[]{:S(2)}, u32[]{:S(2)}) collective-permute-start(bf16[2,768,1536]{2,1,0:T(8,128)(2,1)} %get-tuple-element.93), channel_id=1, source_target_pairs={{0,1},{1,0},{2,3},{3,2},{4,5},{5,4},{6,7},{7,6},{8,9},{9,8},{10,11... | collective-permute-start | bytes 14155784 | tf_op jit(solution)/shard_map/ppermute | solution.py:269
  239.7 67.6 %collective-permute-start.29 = (bf16[16,24,1024]{2,1,0:T(8,128)(2,1)}, bf16[16,24,1024]{2,1,0:T(8,128)(2,1)}, u32[]{:S(2)}, u32[]{:S(2)}) collective-permute-start(bf16[16,24,1024]{2,1,0:T(8,128)(2,1)} %get-tuple-element.118), channel_id=1, source_target_pairs={{0,1},{1,0},{2,3},{3,2},{4,5},{5,4},{6,7},{7,6},{8,9},{9,8},{10,11... | collective-permute-start | bytes 2359304 | tf_op jit(solution)/shard_map/ppermute | solution.py:269
  251.8 27.9 %collective-permute-start.25 = (bf16[4,48,1536]{2,1,0:T(8,128)(2,1)}, bf16[4,48,1536]{2,1,0:T(8,128)(2,1)S(1)}, u32[]{:S(2)}, u32[]{:S(2)}) collective-permute-start(bf16[4,48,1536]{2,1,0:T(8,128)(2,1)} %get-tuple-element.102), channel_id=1, source_target_pairs={{0,8},{1,9},{2,10},{3,11},{4,12},{5,13},{6,14},{7,15},{8,16},{9,17... | collective-permute-start | bytes 1769480 | tf_op jit(solution)/shard_map/ppermute | solution.py:269
  261.0 50.9 %collective-permute-start.26 = (bf16[8,48,3072]{2,1,0:T(8,128)(2,1)}, bf16[8,48,3072]{2,1,0:T(8,128)(2,1)S(1)}, u32[]{:S(2)}, u32[]{:S(2)}) collective-permute-start(bf16[8,48,3072]{2,1,0:T(8,128)(2,1)} %get-tuple-element.94.rest_0_), channel_id=1, source_target_pairs={{0,2},{1,5},{2,0},{3,7},{4,6},{5,1},{6,4},{7,3},{8,10},{9,13},{10,... | collective-permute-start | bytes 7077896 | tf_op jit(solution)/shard_map/ppermute | solution.py:269
  279.4 28.0 %collective-permute-start.27 = (bf16[16,24,768]{2,1,0:T(8,128)(2,1)}, bf16[16,24,768]{2,1,0:T(8,128)(2,1)}, u32[]{:S(2)}, u32[]{:S(2)}) collective-permute-start(bf16[16,24,768]{2,1,0:T(8,128)(2,1)} %get-tuple-element.116), channel_id=1, source_target_pairs={{0,1},{1,0},{2,3},{3,2},{4,5},{5,4},{6,7},{7,6},{8,9},{9,8},{10,11... | collective-permute-start | bytes 1769480 | tf_op jit(solution)/shard_map/ppermute | solution.py:269
  281.7 21.4 %collective-permute-start.30 = (bf16[4,48,1536]{2,1,0:T(8,128)(2,1)}, bf16[4,48,1536]{2,1,0:T(8,128)(2,1)}, u32[]{:S(2)}, u32[]{:S(2)}) collective-permute-start(bf16[4,48,1536]{2,1,0:T(8,128)(2,1)} %fold.10.rest_0_), channel_id=1, source_target_pairs={{0,8},{1,9},{2,10},{3,11},{4,12},{5,13},{6,14},{7,15},{8,16},{9,17... | collective-permute-start | bytes 1769480 | tf_op jit(solution)/shard_map/ppermute | solution.py:269
  307.3 32.4 %collective-permute-start.32 = (bf16[4,48,1536]{2,1,0:T(8,128)(2,1)}, bf16[4,48,1536]{2,1,0:T(8,128)(2,1)}, u32[]{:S(2)}, u32[]{:S(2)}) collective-permute-start(bf16[4,48,1536]{2,1,0:T(8,128)(2,1)} %fold.12.rest_2_), channel_id=1, source_target_pairs={{0,8},{1,9},{2,10},{3,11},{4,12},{5,13},{6,14},{7,15},{8,16},{9,17... | collective-permute-start | bytes 1769480 | tf_op jit(solution)/shard_map/ppermute | solution.py:269
  310.7 40.3 %collective-permute-start.35 = (bf16[8,24,2560]{2,1,0:T(8,128)(2,1)}, bf16[8,24,2560]{2,1,0:T(8,128)(2,1)S(1)}, u32[]{:S(2)}, u32[]{:S(2)}) collective-permute-start(bf16[8,24,2560]{2,1,0:T(8,128)(2,1)} %get-tuple-element.119.rest_1_), channel_id=1, source_target_pairs={{0,2},{1,5},{2,0},{3,7},{4,6},{5,1},{6,4},{7,3},{8,10},{9,13},{10,... | collective-permute-start | bytes 2949128 | tf_op jit(solution)/shard_map/ppermute | solution.py:269
  314.9 22.3 %collective-permute-start.33 = (bf16[4,48,3072]{2,1,0:T(8,128)(2,1)}, bf16[4,48,3072]{2,1,0:T(8,128)(2,1)S(1)}, u32[]{:S(2)}, u32[]{:S(2)}) collective-permute-start(bf16[4,48,3072]{2,1,0:T(8,128)(2,1)} %get-tuple-element.112.rest_0_), channel_id=1, source_target_pairs={{0,4},{1,3},{2,6},{3,1},{4,0},{5,7},{6,2},{7,5},{8,12},{9,11},{10,... | collective-permute-start | bytes 3538952 | tf_op jit(solution)/shard_map/ppermute | solution.py:269
  334.6 16.5 %collective-permute-start.31 = (bf16[16,24,768]{2,1,0:T(8,128)(2,1)}, bf16[16,24,768]{2,1,0:T(8,128)(2,1)S(1)}, u32[]{:S(2)}, u32[]{:S(2)}) collective-permute-start(bf16[16,24,768]{2,1,0:T(8,128)(2,1)} %get-tuple-element.123), channel_id=1, source_target_pairs={{0,1},{1,0},{2,3},{3,2},{4,5},{5,4},{6,7},{7,6},{8,9},{9,8},{10,11... | collective-permute-start | bytes 1769480 | tf_op jit(solution)/shard_map/ppermute | solution.py:269
  361.9 23.9 %collective-permute-start.37 = (f32[512,768]{1,0:T(8,128)}, f32[512,768]{1,0:T(8,128)S(1)}, u32[]{:S(2)}, u32[]{:S(2)}) collective-permute-start(f32[512,768]{1,0:T(8,128)} %get-tuple-element.133), channel_id=1, source_target_pairs={{0,1},{1,0},{2,3},{3,2},{4,5},{5,4},{6,7},{7,6},{8,9},{9,8},{10,11... | collective-permute-start | bytes 4718600 | tf_op jit(solution)/shard_map/ppermute | solution.py:269
  362.8 14.2 %collective-permute-start.22 = (bf16[512,768]{1,0:T(8,128)(2,1)}, bf16[512,768]{1,0:T(8,128)(2,1)S(1)}, u32[]{:S(2)}, u32[]{:S(2)}) collective-permute-start(bf16[512,768]{1,0:T(8,128)(2,1)} %get-tuple-element.86), channel_id=1, source_target_pairs={{0,1},{1,0},{2,3},{3,2},{4,5},{5,4},{6,7},{7,6},{8,9},{9,8},{10,11... | collective-permute-start | bytes 2359304 | tf_op jit(solution)/shard_map/ppermute | solution.py:269
  375.8 18.5 %collective-permute-start.45 = (bf16[1,48,1536]{2,1,0:T(8,128)(2,1)}, bf16[1,48,1536]{2,1,0:T(8,128)(2,1)S(1)}, u32[]{:S(2)}, u32[]{:S(2)}) collective-permute-start(bf16[1,48,1536]{2,1,0:T(8,128)(2,1)} %get-tuple-element.147), channel_id=1, source_target_pairs={{0,4},{1,3},{2,6},{3,1},{4,0},{5,7},{6,2},{7,5},{8,12},{9,11},{10,... | collective-permute-start | bytes 442376 | tf_op jit(solution)/shard_map/ppermute | solution.py:269
  390.4 13.4 %collective-permute-start.43 = (bf16[1,24,3328]{2,1,0:T(8,128)(2,1)}, bf16[1,24,3328]{2,1,0:T(8,128)(2,1)S(1)}, u32[]{:S(2)}, u32[]{:S(2)}) collective-permute-start(bf16[1,24,3328]{2,1,0:T(8,128)(2,1)} %get-tuple-element.141), channel_id=1, source_target_pairs={{0,16},{1,17},{2,18},{3,19},{4,20},{5,21},{6,22},{7,23},{8,24},{9,... | collective-permute-start | bytes 479240 | tf_op jit(solution)/shard_map/ppermute | solution.py:269
  390.6 13.3 %collective-permute-start.44 = (bf16[1,24,3328]{2,1,0:T(8,128)(2,1)S(1)}, bf16[1,24,3328]{2,1,0:T(8,128)(2,1)S(1)}, u32[]{:S(2)}, u32[]{:S(2)}) collective-permute-start(bf16[1,24,3328]{2,1,0:T(8,128)(2,1)S(1)} %get-tuple-element.142), channel_id=1, source_target_pairs={{0,24},{1,25},{2,26},{3,27},{4,28},{5,29},{6,30},{7,31},{8,0},{9,1... | collective-permute-start | bytes 479240 | tf_op jit(solution)/shard_map/ppermute | solution.py:269
  (68 other events, 525.1 us)
where the time goes:
time: 412 us; the launch traced here: 407 us
  Pallas kernels  241 us (58%)
  waiting for transfers between devices  89.9 us (22%)
  starting transfers between devices  36.9 us (9%)
  local copies, waits for them, and re-layouts  28.9 us (7%)
  other arithmetic  8.72 us (2%)
    pallas_call x1, Pallas kernels, middle(): pl.pallas_call(body, grid_spec=pltpu.PrefetchScalarGridSpec(num_scalar_pr...  90.8 us
    ppermute x46, waiting for transfers between devices, across(): return lax.ppermute(value, ('dp', 'tensor'), pairs)  89.9 us
    pallas_call x3, Pallas kernels, attn_backward(): pl.pallas_call(body, grid_spec=pltpu.PrefetchScalarGridSpec(num_scalar_pr...  54.5 us
    pallas_call x3, Pallas kernels, attn_forward(): pl.pallas_call(body, grid_spec=pltpu.PrefetchScalarGridSpec(num_scalar_pr...  41.2 us
    ppermute x46, starting transfers between devices, across(): return lax.ppermute(value, ('dp', 'tensor'), pairs)  36.9 us
    unnamed x115, local copies, waits for them, and re-layouts  19.7 us
    pallas_call x2, Pallas kernels, join_rows(): pl.pallas_call(body, grid_spec=pltpu.PrefetchScalarGridSpec(num_scalar_pr...  13.3 us
    pallas_call x1, Pallas kernels, input_back(): pl.pallas_call(body, grid_spec=pltpu.PrefetchScalarGridSpec(num_scalar_pr...  9.45 us
  transfers between devices with their start and end apart: 46, of which 13 were waited for; matrix products, arithmetic and copies ran while one was open for 4% of the time, Pallas kernels for 34%

commit v1 on v0

--- a/solution.py
+++ b/solution.py
@@ -367,7 +367,7 @@
             scratch_shapes=[pltpu.SemaphoreType.DMA((2,))],
         ),
         out_shape=jax.ShapeDtypeStruct((2,) + mine.shape, mine.dtype),
-        compiler_params=params(16),
+        compiler_params=params(60),
         cost_estimate=cost(0, 4 * mine.size),
         name="place",
     )(core[None], mine, there)
@@ -435,9 +435,9 @@
 
 def windows(bnd, i, work):
     blocks = (bnd[NBLOCK + i] - bnd[i] + BLOCK // KEYS - 1) // (BLOCK // KEYS)
-    for width in range(1, NBLOCK + 1):
-
-        @pl.when(blocks == width)
+    for width in range(NBLOCK - 1, NBLOCK + 1):
+
+        @pl.when(jnp.maximum(blocks, NBLOCK - 1) == width)
         def _():
             low = jnp.minimum(bnd[i], (SEQ - width * BLOCK) // KEYS)
             work(pl.ds(pl.multiple_of(low * KEYS, KEYS), width * BLOCK))
@@ -632,13 +632,14 @@
     )(bounds, *saved[:4], ctx_grad, saved[4], source, cosine, sine, seg_col, seg_row, *deps)
 
 
-def join_rows(index, here, there, count, columns=512):
+def join_rows(index, here, there, count, deps=(), columns=512):
     lead, _, wide = here.shape
     rows = D // 16
     each = 16 // count
     steps = wide // columns
 
-    def body(idx, a, b, *outs):
+    def body(idx, a, b, *rest):
+        outs = rest[len(deps) :]
         for s in range(16):
             at = pl.ds(pl.multiple_of(idx[s] * rows, 16), rows)
             total = a[0, at, :].astype(F32) + b[0, at, :].astype(F32)
@@ -651,14 +652,14 @@
         grid_spec=pltpu.PrefetchScalarGridSpec(
             num_scalar_prefetch=1,
             grid=(lead, steps),
-            in_specs=[whole, whole],
+            in_specs=[whole, whole] + [AFTER] * len(deps),
             out_specs=[part] * count,
         ),
         out_shape=[jax.ShapeDtypeStruct((each, rows, lead * wide), BF16)] * count,
         compiler_params=params(60, ("arbitrary", "arbitrary")),
         cost_estimate=cost(D * wide * lead, 6 * D * wide * lead),
         name="join_rows",
-    )(index, here, there)
+    )(index, here, there, *deps)
 
 
 def out_grad(core, ctx, right, norms):
@@ -767,10 +768,11 @@
     )(*keep, *there, *deps)
 
 
-def finish(parts):
+def finish(parts, deps=()):
     rows = D // 32
 
-    def body(a, b, c, d, qkv, out, gain, shift):
+    def body(a, b, c, d, *rest):
+        qkv, out, gain, shift = rest[len(deps) :]
         total = a[0].astype(F32) + b[0].astype(F32) + c[0].astype(F32) + d[0].astype(F32)
         places = [0, 3 * GROUP, 6 * GROUP + TAIL]
         for i in range(3):
@@ -785,13 +787,13 @@
     shapes = [(rows, 3, D), (rows, D), (rows, 2), (rows, 2)]
     return pl.pallas_call(
         body,
-        in_specs=[vmem] * 4,
+        in_specs=[vmem] * 4 + [AFTER] * len(deps),
         out_specs=[vmem] * 4,
         out_shape=[jax.ShapeDtypeStruct(shape, F32) for shape in shapes],
         compiler_params=params(16, None),
         cost_estimate=cost(1 << 18, 1 << 20),
         name="finish",
-    )(*parts)
+    )(*parts, *deps)
 
 
 def input_back(core, hidden_grad, projected, weights, deps=()):
@@ -1145,10 +1147,11 @@
     gate_four = pile(ahead(gate_parts))
     down_pair = pile([down_block[None], first_swap(down_block)[None]], deps=(gate_four,))
     saved0 = attn_forward(0, 1, bounds, source, weights, *tables, deps=(gate_four, down_pair))
-    gate_eight = pile([gate_four, first_swap(gate_four)], deps=(saved0[4],))
+    near, far = depth_shift(down_pair, 1), depth_shift(down_pair, 3)
+    gate_eight = pile([gate_four, first_swap(gate_four)], deps=(saved0[4], near, far))
     gate_last = second_swap(gate_eight)
     saved1 = attn_forward(1, 1, bounds, source, weights, *tables, deps=(gate_eight,))
-    down_eight = pile(depth_parts(down_pair), deps=(saved1[4],))
+    down_eight = pile([down_pair, near, depth_shift(down_pair, 2), far], deps=(saved1[4],))
     saved2 = attn_forward(2, 1, bounds, source, weights, *tables, deps=(down_eight,))
     down_last, late_logs = lax.optimization_barrier((second_swap(down_eight), saved2[4]))
     saved2 = (*saved2[:4], late_logs)
@@ -1164,10 +1167,10 @@
         middle(index, source, ctx, cot, pieces)
     )
 
-    down_there, gu_there = core_swap(down_there), core_swap(gu_there)
+    gu_there, down_there = core_swap(gu_there), core_swap(down_there)
     tail_mine, tail_theirs = out_grad(core, ctx, att_grad, sums)
-    down_parts = join_rows(deep_first, down_here, down_there, 4)
-    gu_keep, gu_send = join_rows(to_here, gu_here, gu_there, 2)
+    gu_keep, gu_send = join_rows(to_here, gu_here, gu_there, 2, deps=(tail_mine,))
+    down_parts = join_rows(deep_first, down_here, down_there, 4, deps=(gu_send,))
     gu_first = first_swap(gu_send)
     passing = depth_shift(down_parts[3], 1)
 
@@ -1183,6 +1186,7 @@
         to_here,
         (back0[1], back1[1], tail_mine),
         (core_swap(back0[2]), core_swap(back1[2]), core_swap(tail_theirs)),
+        deps=(passing, gu_send),
     )
     early_first = first_swap(early_send)
     back2 = attn_backward(0, 2, bounds, saved2, ctx_grad, *common, deps=(gu_send, early_send, passing))
@@ -1190,27 +1194,28 @@
     deep = lambda parts: [parts[0]] + [depth_shift(parts[k], k) for k in (1, 2, 3)]
     passing = depth_shift(passing, 1)
     gu_parts = fold(gu_keep, gu_second, 4, deps=(back2[1],))
-    (gu_total,) = fold(depth_shift(gu_parts[3], 1), gu_parts[2], 1)
     down_keep, down_send = fold(passing, down_parts[0], 2, deps=(gu_parts[0],))
-    down_keep, down_send = fold(down_keep, first_swap(down_send), 2)
+    late_keep, late_send = join_dealt(
+        to_here, (back2[1],), (core_swap(back2[2]),), deps=(down_send, early_first)
+    )
+    late_first = first_swap(late_send)
+    down_keep, down_send = fold(down_keep, first_swap(down_send), 2, deps=(late_send,))
     down_second = second_swap(down_send)
-    late_keep, late_send = join_dealt(
-        to_here, (back2[1],), (core_swap(back2[2]),), deps=(down_keep, early_first)
-    )
+    (gu_total,) = fold(depth_shift(gu_parts[3], 1), gu_parts[2], 1, deps=(down_send,))
+    attn_keep, attn_send = fold_pair(
+        (early_keep, late_keep), (early_first, late_first), deps=(gu_total,)
+    )
+    attn_second = second_swap(attn_send)
     grad, grad_leave = input_back(
-        core, hidden_grad, (back0[0], back1[0], back2[0]), weights, deps=(late_send, gu_total)
+        core, hidden_grad, (back0[0], back1[0], back2[0]), weights, deps=(attn_send,)
     )
     (gu_total,) = fold(depth_shift(gu_total, 1), gu_parts[1], 1, deps=(grad,))
-    attn_keep, attn_send = fold_pair(
-        (early_keep, late_keep), (early_first, first_swap(late_send)), deps=(gu_total,)
-    )
-    attn_second = second_swap(attn_send)
+    attn_parts = deep(fold(attn_keep, attn_second, 4, deps=(gu_total,)))
+    (gu_total,) = fold(depth_shift(gu_total, 1), gu_parts[0], 1, F32, deps=(attn_parts[0],))
     outputs = place(core, out, core_swap(out_leave)), place(core, grad, core_swap(grad_leave))
-    (gu_total,) = fold(depth_shift(gu_total, 1), gu_parts[0], 1, F32, deps=(attn_send,))
-    attn_parts = deep(fold(attn_keep, attn_second, 4, deps=(gu_total, *outputs)))
     down_total = (down_keep.astype(F32) + down_second.astype(F32))[0]
     gu_total = gu_total[0]
-    qkv_total, out_total, gain_total, shift_total = finish(attn_parts)
+    qkv_total, out_total, gain_total, shift_total = finish(attn_parts, deps=outputs)
 
     return (
         *outputs,

time: 412 us -> 390 us (0.947)
  waiting for transfers between devices: 89.9 us -> 66.8 us
    ppermute x46, waiting for transfers between devices: 89.9 us -> 66.8 us  [across(): return lax.ppermute(value, ('dp', 'tensor'), pairs)]
    pallas_call x1, Pallas kernels: 90.8 us -> 81.9 us  [middle(): pl.pallas_call(body, grid_spec=pltpu.PrefetchScalarGridSpec(num_scalar_pr...]
    unnamed x115 -> x127, local copies, waits for them, and re-layouts: 19.7 us -> 20.5 us
  transfers between devices with their start and end apart: 46 -> 46, of which waited for: 13 -> 16; matrix products, arithmetic and copies ran while one was open for 4% -> 5% of each run, Pallas kernels for 34% -> 37%
where the time goes in v1:
time: 390 us; the launch traced here: 382 us
  Pallas kernels  238 us (61%)
  waiting for transfers between devices  66.8 us (17%)
  starting transfers between devices  36.7 us (9%)
  local copies, waits for them, and re-layouts  29.6 us (8%)
  other arithmetic  9.81 us (3%)
    pallas_call x1, Pallas kernels, middle(): pl.pallas_call(body, grid_spec=pltpu.PrefetchScalarGridSpec(num_scalar_pr...  81.9 us
    ppermute x46, waiting for transfers between devices, across(): return lax.ppermute(value, ('dp', 'tensor'), pairs)  66.8 us
    pallas_call x3, Pallas kernels, attn_backward(): pl.pallas_call(body, grid_spec=pltpu.PrefetchScalarGridSpec(num_scalar_pr...  56.1 us
    pallas_call x3, Pallas kernels, attn_forward(): pl.pallas_call(body, grid_spec=pltpu.PrefetchScalarGridSpec(num_scalar_pr...  43.3 us
    ppermute x46, starting transfers between devices, across(): return lax.ppermute(value, ('dp', 'tensor'), pairs)  36.7 us
    unnamed x127, local copies, waits for them, and re-layouts  20.5 us
    pallas_call x2, Pallas kernels, join_rows(): pl.pallas_call(body, grid_spec=pltpu.PrefetchScalarGridSpec(num_scalar_pr...  13.1 us
    pallas_call x1, Pallas kernels, input_back(): pl.pallas_call(body, grid_spec=pltpu.PrefetchScalarGridSpec(num_scalar_pr...  9.19 us
  transfers between devices with their start and end apart: 46, of which 16 were waited for; matrix products, arithmetic and copies ran while one was open for 5% of the time, Pallas kernels for 37%

profile of v1, /device:TPU:0, one launch (start us, length us, event | category | flops | bytes accessed | tf_op | source)
XLA Modules:
  0.0 382.4 jit_solution(16392246007990595524)
XLA Ops:
  1.6 5.0 %collective-permute-start.2 = (bf16[24,2304]{1,0:T(8,128)(2,1)S(1)}, bf16[24,2304]{1,0:T(8,128)(2,1)S(1)}, u32[]{:S(2)}, u32[]{:S(2)}) collective-permute-start(bf16[24,2304]{1,0:T(8,128)(2,1)S(1)} %bitcast.52), channel_id=1, source_target_pairs={{0,24},{1,25},{2,26},{3,27},{4,28},{5,29},{6,30},{7,31},{8,0},{9,1... | collective-permute-start | bytes 331784 | tf_op jit(solution)/shard_map/ppermute | solution.py:269
  11.2 2.6 constant_dynamic-slice_fusion
  14.5 8.1 %collective-permute-done.1 = bf16[24,2304]{1,0:T(8,128)(2,1)S(1)} collective-permute-done((bf16[24,2304]{1,0:T(8,128)(2,1)S(1)}, bf16[24,2304]{1,0:T(8,128)(2,1)S(1)}, u32[]{:S(2)}, u32[]{:S(2)}) %collective-permute-start.1) | collective-permute-done | bytes 110624 | tf_op jit(solution)/shard_map/ppermute | solution.py:269
  31.1 5.5 %collective-permute-done.5.refs_2_ = bf16[48,3072]{1,0:T(8,128)(2,1)S(1)} collective-permute-done((bf16[48,3072]{1,0:T(8,128)(2,1)S(1)}, bf16[48,3072]{1,0:T(8,128)(2,1)S(1)}, u32[]{:S(2)}, u32[]{:S(2)}) %collective-permute-start.5) | collective-permute-done | bytes 294944 | tf_op jit(solution)/shard_map/ppermute | solution.py:269
  42.2 10.3 %collective-permute-done.7.b = bf16[8,24,2304]{2,1,0:T(8,128)(2,1)} collective-permute-done((bf16[8,24,2304]{2,1,0:T(8,128)(2,1)S(1)}, bf16[8,24,2304]{2,1,0:T(8,128)(2,1)}, u32[]{:S(2)}, u32[]{:S(2)}) %collective-permute-start.7) | collective-permute-done | bytes 884768 | tf_op jit(solution)/shard_map/ppermute | solution.py:269
  59.4 4.8 %assemble.1 = bf16[32,24,2304]{2,1,0:T(8,128)(2,1)} custom-call(s32[32]{0:T(128)} %pad_add_fusion.2.idx, bf16[8,24,2304]{2,1,0:T(8,128)(2,1)} %copy-done.11, bf16[8,24,2304]{2,1,0:T(8,128)(2,1)} %collective-permute-done.7.b, bf16[8,24,2304]{2,1,0:T(8,128)(2,1)} %copy-done.53, bf16[8,24,2304]{2,1,0:T(8,128)(2,1)} %collective-permute-done.9.d, ...), custom_call_target="tpu_custom_call" | custom-call | bytes 7077888 | tf_op jit(solution)/shard_map/assemble/pallas_call | solution.py:391
  64.2 14.3 %attn_forward.3 = (bf16[1024,256]{1,0:T(8,128)(2,1)}, bf16[1024,256]{1,0:T(8,128)(2,1)}, bf16[1024,256]{1,0:T(8,128)(2,1)}, bf16[1024,256]{1,0:T(8,128)(2,1)}, f32[1,8,1024]{2,1,0:T(8,128)}) custom-call(s32[9]{0:T(128)} %pad_add_fusion.1.bnd, bf16[1024,768]{1,0:T(8,128)(2,1)} %copy-done.6, bf16[768,2304]{1,0:T(8,128)(2,1)} %bitcast.39, ...), custom_call_target="tpu_custom_call" | custom-call | flops 5502926848 | bytes 8388608 | tf_op jit(solution)/shard_map/attn_forward/pallas_call | solution.py:492
  80.9 3.0 pile.10.rest_0_.refs_0_
  84.5 14.3 %attn_forward.4 = (bf16[1024,256]{1,0:T(8,128)(2,1)}, bf16[1024,256]{1,0:T(8,128)(2,1)}, bf16[1024,256]{1,0:T(8,128)(2,1)}, bf16[1024,256]{1,0:T(8,128)(2,1)}, f32[1,8,1024]{2,1,0:T(8,128)}) custom-call(s32[9]{0:T(128)} %pad_add_fusion.1.bnd, bf16[1024,768]{1,0:T(8,128)(2,1)} %copy-done.6, bf16[768,2304]{1,0:T(8,128)(2,1)} %bitcast.42, ...), custom_call_target="tpu_custom_call" | custom-call | flops 5502926848 | bytes 8388608 | tf_op jit(solution)/shard_map/attn_forward/pallas_call | solution.py:492
  98.8 5.2 %collective-permute-done.15.refs_2_ = bf16[2,48,2048]{2,1,0:T(8,128)(2,1)S(1)} collective-permute-done((bf16[2,48,2048]{2,1,0:T(8,128)(2,1)S(1)}, bf16[2,48,2048]{2,1,0:T(8,128)(2,1)S(1)}, u32[]{:S(2)}, u32[]{:S(2)}) %collective-permute-start.15) | collective-permute-done | bytes 393248 | tf_op jit(solution)/shard_map/ppermute | solution.py:269
  107.1 6.0 %collective-permute-done.16.refs_1_ = bf16[8,48,3072]{2,1,0:T(8,128)(2,1)} collective-permute-done((bf16[8,48,3072]{2,1,0:T(8,128)(2,1)}, bf16[8,48,3072]{2,1,0:T(8,128)(2,1)}, u32[]{:S(2)}, u32[]{:S(2)}) %collective-permute-start.16) | collective-permute-done | bytes 2359328 | tf_op jit(solution)/shard_map/ppermute | solution.py:269
  113.7 14.7 %attn_forward.5 = (bf16[1024,256]{1,0:T(8,128)(2,1)}, bf16[1024,256]{1,0:T(8,128)(2,1)}, bf16[1024,256]{1,0:T(8,128)(2,1)}, bf16[1024,256]{1,0:T(8,128)(2,1)}, f32[1,8,1024]{2,1,0:T(8,128)}) custom-call(s32[9]{0:T(128)} %pad_add_fusion.1.bnd, bf16[1024,768]{1,0:T(8,128)(2,1)} %copy-done.6, bf16[768,2304]{1,0:T(8,128)(2,1)} %bitcast.45, ...), custom_call_target="tpu_custom_call" | custom-call | flops 5502926848 | bytes 8388608 | tf_op jit(solution)/shard_map/attn_forward/pallas_call | solution.py:492
  130.7 3.0 collective-permute-done.21.refs_7_
  133.8 81.9 %middle.1 = (bf16[512,768]{1,0:T(8,128)(2,1)}, bf16[512,768]{1,0:T(8,128)(2,1)}, bf16[2,768,1536]{2,1,0:T(8,128)(2,1)}, bf16[2,768,1536]{2,1,0:T(8,128)(2,1)}, b...) custom-call(s32[65]{0:T(128)} %concatenate.21.idx, ...), custom_call_target="tpu_custom_call" | custom-call | flops 45902462976 | bytes 41943040 | tf_op jit(solution)/shard_map/middle/pallas_call | solution.py:1039
  217.6 4.4 %out_grad.1 = (bf16[16,24,1024]{2,1,0:T(8,128)(2,1)}, bf16[16,24,1024]{2,1,0:T(8,128)(2,1)}) custom-call(s32[1]{0:T(128)} %bitcast.c, bf16[1024,256]{1,0:T(8,128)(2,1)} %get-tuple-element.78.ctx0.refs_0_.o, bf16[1024,256]{1,0:T(8,128)(2,1)} %get-tuple-element.80.ctx1.refs_1_.o, bf16[1024,256]{1,0:T(8,128)(2,1)} %get-tuple-element.82.ctx2.refs_2_.o, ...), custom_call_target="tpu_custom_call" | custom-call | flops 1207959552 | bytes 8388608 | tf_op jit(solution)/shard_map/out_grad/pallas_call | solution.py:676
  222.1 6.4 %collective-permute-done.23.b = bf16[2,768,1536]{2,1,0:T(8,128)(2,1)} collective-permute-done((bf16[2,768,1536]{2,1,0:T(8,128)(2,1)}, bf16[2,768,1536]{2,1,0:T(8,128)(2,1)}, u32[]{:S(2)}, u32[]{:S(2)}) %collective-permute-start.23) | collective-permute-done | bytes 4718624 | tf_op jit(solution)/shard_map/ppermute | solution.py:269
  228.5 7.9 %join_rows.2 = (bf16[8,48,3072]{2,1,0:T(8,128)(2,1)}, bf16[8,48,3072]{2,1,0:T(8,128)(2,1)}) custom-call(s32[16]{0:T(128)} %fusion.16.idx, bf16[2,768,1536]{2,1,0:T(8,128)(2,1)} %get-tuple-element.92.a, bf16[2,768,1536]{2,1,0:T(8,128)(2,1)} %collective-permute-done.23.b, bf16[16,24,1024]{2,1,0:T(8,128)(2,1)} %get-tuple-element.96.rest_0_.refs_2_), custom_call_target="tpu_custom_call" | custom-call | flops 2359296 | bytes 14155776 | tf_op jit(solution)/shard_map/join_rows/pallas_call | solution.py:650
  238.8 5.2 %join_rows.3 = (bf16[4,48,1536]{2,1,0:T(8,128)(2,1)}, bf16[4,48,1536]{2,1,0:T(8,128)(2,1)}, bf16[4,48,1536]{2,1,0:T(8,128)(2,1)}, bf16[4,48,1536]{2,1,0:T(8,128)(2,1)}) custom-call(s32[16]{0:T(128)} %fusion.21.idx, bf16[1,768,1536]{2,1,0:T(8,128)(2,1)} %get-tuple-element.98.a, bf16[1,768,1536]{2,1,0:T(8,128)(2,1)} %copy-done.52, ...), custom_call_target="tpu_custom_call" | custom-call | flops 1179648 | bytes 7077888 | tf_op jit(solution)/shard_map/join_rows/pallas_call | solution.py:650
  244.0 18.7 %attn_backward.3 = (bf16[3,1024,256]{2,1,0:T(8,128)(2,1)}, bf16[16,24,768]{2,1,0:T(8,128)(2,1)}, bf16[16,24,768]{2,1,0:T(8,128)(2,1)}) custom-call(s32[9]{0:T(128)} %pad_add_fusion.1.bnd, bf16[1024,256]{1,0:T(8,128)(2,1)} %get-tuple-element.88.q, bf16[1024,256]{1,0:T(8,128)(2,1)} %get-tuple-element.89.k, bf16[1024,256]{1,0:T(8,128)(2,1)} %get-tuple-element.90.v, ...), custom_call_target="tpu_custom_call" | custom-call | flops 11945377792 | bytes 10485760 | tf_op jit(solution)/shard_map/attn_backward/pallas_call | solution.py:598
  264.7 18.8 %attn_backward.4 = (bf16[3,1024,256]{2,1,0:T(8,128)(2,1)}, bf16[16,24,768]{2,1,0:T(8,128)(2,1)}, bf16[16,24,768]{2,1,0:T(8,128)(2,1)}) custom-call(s32[9]{0:T(128)} %pad_add_fusion.1.bnd, bf16[1024,256]{1,0:T(8,128)(2,1)} %get-tuple-element.102.q, bf16[1024,256]{1,0:T(8,128)(2,1)} %get-tuple-element.103.k, bf16[1024,256]{1,0:T(8,128)(2,1)} %get-tuple-element.104.v, ...), custom_call_target="tpu_custom_call" | custom-call | flops 11945377792 | bytes 10485760 | tf_op jit(solution)/shard_map/attn_backward/pallas_call | solution.py:598
  290.4 3.2 fold.11
  295.2 3.0 join_dealt.2
  300.8 18.6 %attn_backward.5 = (bf16[3,1024,256]{2,1,0:T(8,128)(2,1)}, bf16[16,24,768]{2,1,0:T(8,128)(2,1)}, bf16[16,24,768]{2,1,0:T(8,128)(2,1)}) custom-call(s32[9]{0:T(128)} %pad_add_fusion.1.bnd, bf16[1024,256]{1,0:T(8,128)(2,1)} %get-tuple-element.109.q, bf16[1024,256]{1,0:T(8,128)(2,1)} %get-tuple-element.110.k, bf16[1024,256]{1,0:T(8,128)(2,1)} %get-tuple-element.111.v, ...), custom_call_target="tpu_custom_call" | custom-call | flops 11945377792 | bytes 10485760 | tf_op jit(solution)/shard_map/attn_backward/pallas_call | solution.py:598
  328.2 2.6 collective-permute-done.37.b
  331.4 3.0 collective-permute-done.36.a
  335.9 9.2 %input_back.1 = (f32[512,768]{1,0:T(8,128)}, f32[512,768]{1,0:T(8,128)}) custom-call(s32[1]{0:T(128)} %bitcast.c, f32[1024,768]{1,0:T(8,128)} %get-tuple-element.87.hid, bf16[3,1024,256]{2,1,0:T(8,128)(2,1)} %get-tuple-element.101.a, bf16[3,1024,256]{2,1,0:T(8,128)(2,1)} %get-tuple-element.108.b, bf16[3,1024,256]{2,1,0:T(8,128)(2,1)} %get-tuple-element.121.d, ...), custom_call_target="tpu_custom_call" | custom-call | flops 3623878656 | bytes 16777216 | tf_op jit(solution)/shard_map/input_back/pallas_call | solution.py:821
  350.2 2.7 place.2.rest_0_
  352.8 4.5 %collective-permute-done.40.a = bf16[1,48,3072]{2,1,0:T(8,128)(2,1)S(1)} collective-permute-done((bf16[1,48,3072]{2,1,0:T(8,128)(2,1)S(1)}, bf16[1,48,3072]{2,1,0:T(8,128)(2,1)S(1)}, u32[]{:S(2)}, u32[]{:S(2)}) %collective-permute-start.40) | collective-permute-done | bytes 294944 | tf_op jit(solution)/shard_map/ppermute | solution.py:269
  357.8 4.3 %collective-permute-start.42 = (bf16[1,24,3328]{2,1,0:T(8,128)(2,1)S(1)}, bf16[1,24,3328]{2,1,0:T(8,128)(2,1)S(1)}, u32[]{:S(2)}, u32[]{:S(2)}) collective-permute-start(bf16[1,24,3328]{2,1,0:T(8,128)(2,1)S(1)} %get-tuple-element.141), channel_id=1, source_target_pairs={{0,16},{1,17},{2,18},{3,19},{4,20},{5,21},{6,22},{7,23},{8,24},{9,... | collective-permute-start | bytes 479240 | tf_op jit(solution)/shard_map/ppermute | solution.py:269
  363.8 5.6 %collective-permute-done.44.a = bf16[1,48,3072]{2,1,0:T(8,128)(2,1)S(1)} collective-permute-done((bf16[1,48,3072]{2,1,0:T(8,128)(2,1)S(1)}, bf16[1,48,3072]{2,1,0:T(8,128)(2,1)S(1)}, u32[]{:S(2)}, u32[]{:S(2)}) %collective-permute-start.44) | collective-permute-done | bytes 294944 | tf_op jit(solution)/shard_map/ppermute | solution.py:269
  370.7 3.7 place.3.rest_1_
  374.4 2.9 collective-permute-done.42.c
  (262 shorter events, 77.0 us)
Async XLA Ops:
  6.6 16.0 %collective-permute-start.1 = (bf16[24,2304]{1,0:T(8,128)(2,1)S(1)}, bf16[24,2304]{1,0:T(8,128)(2,1)S(1)}, u32[]{:S(2)}, u32[]{:S(2)}) collective-permute-start(bf16[24,2304]{1,0:T(8,128)(2,1)S(1)} %bitcast.53), channel_id=1, source_target_pairs={{0,16},{1,17},{2,18},{3,19},{4,20},{5,21},{6,22},{7,23},{8,24},{9,... | collective-permute-start | bytes 331784 | tf_op jit(solution)/shard_map/ppermute | solution.py:269
  6.6 16.0 %collective-permute-start = (bf16[24,2304]{1,0:T(8,128)(2,1)S(1)}, bf16[24,2304]{1,0:T(8,128)(2,1)S(1)}, u32[]{:S(2)}, u32[]{:S(2)}) collective-permute-start(bf16[24,2304]{1,0:T(8,128)(2,1)S(1)} %bitcast.54), channel_id=1, source_target_pairs={{0,8},{1,9},{2,10},{3,11},{4,12},{5,13},{6,14},{7,15},{8,16},{9,17... | collective-permute-start | bytes 331784 | tf_op jit(solution)/shard_map/ppermute | solution.py:269
  8.6 14.0 %collective-permute-start.3 = (bf16[48,3072]{1,0:T(8,128)(2,1)S(1)}, bf16[48,3072]{1,0:T(8,128)(2,1)S(1)}, u32[]{:S(2)}, u32[]{:S(2)}) collective-permute-start(bf16[48,3072]{1,0:T(8,128)(2,1)S(1)} %bitcast.51), channel_id=1, source_target_pairs={{0,8},{1,9},{2,10},{3,11},{4,12},{5,13},{6,14},{7,15},{8,16},{9,17... | collective-permute-start | bytes 884744 | tf_op jit(solution)/shard_map/ppermute | solution.py:269
  13.8 15.1 %collective-permute-start.6 = (bf16[512,768]{1,0:T(8,128)(2,1)}, bf16[512,768]{1,0:T(8,128)(2,1)}, u32[]{:S(2)}, u32[]{:S(2)}) collective-permute-start(bf16[512,768]{1,0:T(8,128)(2,1)} %get-tuple-element.181), channel_id=1, source_target_pairs={{0,1},{1,0},{2,3},{3,2},{4,5},{5,4},{6,7},{7,6},{8,9},{9,8},{10,11... | collective-permute-start | bytes 2359304 | tf_op jit(solution)/shard_map/ppermute | solution.py:269
  23.2 13.3 %collective-permute-start.4 = (bf16[4,24,2304]{2,1,0:T(8,128)(2,1)S(1)}, bf16[4,24,2304]{2,1,0:T(8,128)(2,1)S(1)}, u32[]{:S(2)}, u32[]{:S(2)}) collective-permute-start(bf16[4,24,2304]{2,1,0:T(8,128)(2,1)S(1)} %pile.6.refs_0_), channel_id=1, source_target_pairs={{0,2},{1,5},{2,0},{3,7},{4,6},{5,1},{6,4},{7,3},{8,10},{9,13},{10,... | collective-permute-start | bytes 1327112 | tf_op jit(solution)/shard_map/ppermute | solution.py:269
  37.2 15.3 %collective-permute-start.7 = (bf16[8,24,2304]{2,1,0:T(8,128)(2,1)S(1)}, bf16[8,24,2304]{2,1,0:T(8,128)(2,1)}, u32[]{:S(2)}, u32[]{:S(2)}) collective-permute-start(bf16[8,24,2304]{2,1,0:T(8,128)(2,1)S(1)} %pile.7.a), channel_id=1, source_target_pairs={{0,4},{1,3},{2,6},{3,1},{4,0},{5,7},{6,2},{7,5},{8,12},{9,11},{10,... | collective-permute-start | bytes 2654216 | tf_op jit(solution)/shard_map/ppermute | solution.py:269
  38.1 14.6 %collective-permute-start.10 = (bf16[48,3072]{1,0:T(8,128)(2,1)S(1)}, bf16[48,3072]{1,0:T(8,128)(2,1)S(1)}, u32[]{:S(2)}, u32[]{:S(2)}) collective-permute-start(bf16[48,3072]{1,0:T(8,128)(2,1)S(1)} %collective-permute-done.5.refs_2_), channel_id=1, source_target_pairs={{0,8},{1,9},{2,10},{3,11},{4,12},{5,13},{6,14},{7,15},{8,16},{9,17... | collective-permute-start | bytes 884744 | tf_op jit(solution)/shard_map/ppermute | solution.py:269
  39.1 16.6 %collective-permute-start.11 = (bf16[48,2048]{1,0:T(8,128)(2,1)S(1)}, bf16[48,2048]{1,0:T(8,128)(2,1)S(1)}, u32[]{:S(2)}, u32[]{:S(2)}) collective-permute-start(bf16[48,2048]{1,0:T(8,128)(2,1)S(1)} %get-tuple-element.182), channel_id=1, source_target_pairs={{0,2},{1,5},{2,0},{3,7},{4,6},{5,1},{6,4},{7,3},{8,10},{9,13},{10,... | collective-permute-start | bytes 589832 | tf_op jit(solution)/shard_map/ppermute | solution.py:269
  42.1 16.4 %collective-permute-start.8 = (bf16[8,24,2304]{2,1,0:T(8,128)(2,1)S(1)}, bf16[8,24,2304]{2,1,0:T(8,128)(2,1)S(1)}, u32[]{:S(2)}, u32[]{:S(2)}) collective-permute-start(bf16[8,24,2304]{2,1,0:T(8,128)(2,1)S(1)} %pile.7.a), channel_id=1, source_target_pairs={{0,1},{1,0},{2,3},{3,2},{4,5},{5,4},{6,7},{7,6},{8,9},{9,8},{10,11... | collective-permute-start | bytes 2654216 | tf_op jit(solution)/shard_map/ppermute | solution.py:269
  53.0 25.5 %collective-permute-start.12 = (bf16[4,48,3072]{2,1,0:T(8,128)(2,1)S(1)}, bf16[4,48,3072]{2,1,0:T(8,128)(2,1)}, u32[]{:S(2)}, u32[]{:S(2)}) collective-permute-start(bf16[4,48,3072]{2,1,0:T(8,128)(2,1)S(1)} %pile.8.refs_2_.rest_0_.refs_0_), channel_id=1, source_target_pairs={{0,2},{1,5},{2,0},{3,7},{4,6},{5,1},{6,4},{7,3},{8,10},{9,13},{10,... | collective-permute-start | bytes 3538952 | tf_op jit(solution)/shard_map/ppermute | solution.py:269
  56.2 22.3 %collective-permute-start.14 = (bf16[2,48,2048]{2,1,0:T(8,128)(2,1)S(1)}, bf16[2,48,2048]{2,1,0:T(8,128)(2,1)S(1)}, u32[]{:S(2)}, u32[]{:S(2)}) collective-permute-start(bf16[2,48,2048]{2,1,0:T(8,128)(2,1)S(1)} %pile.9.rest_1_.refs_0_), channel_id=1, source_target_pairs={{0,24},{1,25},{2,26},{3,27},{4,28},{5,29},{6,30},{7,31},{8,0},{9,1... | collective-permute-start | bytes 1179656 | tf_op jit(solution)/shard_map/ppermute | solution.py:269
  56.9 21.6 %collective-permute-start.13 = (bf16[2,48,2048]{2,1,0:T(8,128)(2,1)S(1)}, bf16[2,48,2048]{2,1,0:T(8,128)(2,1)S(1)}, u32[]{:S(2)}, u32[]{:S(2)}) collective-permute-start(bf16[2,48,2048]{2,1,0:T(8,128)(2,1)S(1)} %pile.9.rest_1_.refs_0_), channel_id=1, source_target_pairs={{0,8},{1,9},{2,10},{3,11},{4,12},{5,13},{6,14},{7,15},{8,16},{9,17... | collective-permute-start | bytes 1179656 | tf_op jit(solution)/shard_map/ppermute | solution.py:269
  83.9 29.2 %collective-permute-start.16 = (bf16[8,48,3072]{2,1,0:T(8,128)(2,1)}, bf16[8,48,3072]{2,1,0:T(8,128)(2,1)}, u32[]{:S(2)}, u32[]{:S(2)}) collective-permute-start(bf16[8,48,3072]{2,1,0:T(8,128)(2,1)} %pile.10.rest_0_.refs_0_), channel_id=1, source_target_pairs={{0,4},{1,3},{2,6},{3,1},{4,0},{5,7},{6,2},{7,5},{8,12},{9,11},{10,... | collective-permute-start | bytes 7077896 | tf_op jit(solution)/shard_map/ppermute | solution.py:269
  84.0 20.0 %collective-permute-start.15 = (bf16[2,48,2048]{2,1,0:T(8,128)(2,1)S(1)}, bf16[2,48,2048]{2,1,0:T(8,128)(2,1)S(1)}, u32[]{:S(2)}, u32[]{:S(2)}) collective-permute-start(bf16[2,48,2048]{2,1,0:T(8,128)(2,1)S(1)} %copy-done.24), channel_id=1, source_target_pairs={{0,16},{1,17},{2,18},{3,19},{4,20},{5,21},{6,22},{7,23},{8,24},{9,... | collective-permute-start | bytes 1179656 | tf_op jit(solution)/shard_map/ppermute | solution.py:269
  105.6 24.4 %collective-permute-start.19 = (bf16[8,48,2048]{2,1,0:T(8,128)(2,1)S(1)}, bf16[8,48,2048]{2,1,0:T(8,128)(2,1)}, u32[]{:S(2)}, u32[]{:S(2)}) collective-permute-start(bf16[8,48,2048]{2,1,0:T(8,128)(2,1)S(1)} %pile.11.rest_0_.refs_4_), channel_id=1, source_target_pairs={{0,4},{1,3},{2,6},{3,1},{4,0},{5,7},{6,2},{7,5},{8,12},{9,11},{10,... | collective-permute-start | bytes 4718600 | tf_op jit(solution)/shard_map/ppermute | solution.py:269
  107.1 23.6 %collective-permute-start.17 = (bf16[8,48,3072]{2,1,0:T(8,128)(2,1)}, bf16[8,48,3072]{2,1,0:T(8,128)(2,1)}, u32[]{:S(2)}, u32[]{:S(2)}) collective-permute-start(bf16[8,48,3072]{2,1,0:T(8,128)(2,1)} %pile.10.rest_0_.refs_0_), channel_id=1, source_target_pairs={{0,1},{1,0},{2,3},{3,2},{4,5},{5,4},{6,7},{7,6},{8,9},{9,8},{10,11... | collective-permute-start | bytes 7077896 | tf_op jit(solution)/shard_map/ppermute | solution.py:269
  113.1 20.6 %collective-permute-start.18 = (bf16[8,48,3072]{2,1,0:T(8,128)(2,1)}, bf16[8,48,3072]{2,1,0:T(8,128)(2,1)}, u32[]{:S(2)}, u32[]{:S(2)}) collective-permute-start(bf16[8,48,3072]{2,1,0:T(8,128)(2,1)} %collective-permute-done.16.refs_1_), channel_id=1, source_target_pairs={{0,1},{1,0},{2,3},{3,2},{4,5},{5,4},{6,7},{7,6},{8,9},{9,8},{10,11... | collective-permute-start | bytes 7077896 | tf_op jit(solution)/shard_map/ppermute | solution.py:269
  113.1 17.6 %collective-permute-start.20 = (bf16[8,48,2048]{2,1,0:T(8,128)(2,1)S(1)}, bf16[8,48,2048]{2,1,0:T(8,128)(2,1)}, u32[]{:S(2)}, u32[]{:S(2)}) collective-permute-start(bf16[8,48,2048]{2,1,0:T(8,128)(2,1)S(1)} %pile.11.rest_0_.refs_4_), channel_id=1, source_target_pairs={{0,1},{1,0},{2,3},{3,2},{4,5},{5,4},{6,7},{7,6},{8,9},{9,8},{10,11... | collective-permute-start | bytes 4718600 | tf_op jit(solution)/shard_map/ppermute | solution.py:269
  215.9 21.4 %collective-permute-start.24 = (bf16[1,768,1536]{2,1,0:T(8,128)(2,1)}, bf16[1,768,1536]{2,1,0:T(8,128)(2,1)S(1)}, u32[]{:S(2)}, u32[]{:S(2)}) collective-permute-start(bf16[1,768,1536]{2,1,0:T(8,128)(2,1)} %get-tuple-element.99), channel_id=1, source_target_pairs={{0,1},{1,0},{2,3},{3,2},{4,5},{5,4},{6,7},{7,6},{8,9},{9,8},{10,11... | collective-permute-start | bytes 7077896 | tf_op jit(solution)/shard_map/ppermute | solution.py:269
  222.0 73.2 %collective-permute-start.29 = (bf16[16,24,1024]{2,1,0:T(8,128)(2,1)}, bf16[16,24,1024]{2,1,0:T(8,128)(2,1)S(1)}, u32[]{:S(2)}, u32[]{:S(2)}) collective-permute-start(bf16[16,24,1024]{2,1,0:T(8,128)(2,1)} %get-tuple-element.118), channel_id=1, source_target_pairs={{0,1},{1,0},{2,3},{3,2},{4,5},{5,4},{6,7},{7,6},{8,9},{9,8},{10,11... | collective-permute-start | bytes 2359304 | tf_op jit(solution)/shard_map/ppermute | solution.py:269
  236.4 54.0 %collective-permute-start.26 = (bf16[8,48,3072]{2,1,0:T(8,128)(2,1)}, bf16[8,48,3072]{2,1,0:T(8,128)(2,1)}, u32[]{:S(2)}, u32[]{:S(2)}) collective-permute-start(bf16[8,48,3072]{2,1,0:T(8,128)(2,1)} %get-tuple-element.97.rest_0_), channel_id=1, source_target_pairs={{0,2},{1,5},{2,0},{3,7},{4,6},{5,1},{6,4},{7,3},{8,10},{9,13},{10,... | collective-permute-start | bytes 7077896 | tf_op jit(solution)/shard_map/ppermute | solution.py:269
  244.0 18.7 %collective-permute-start.25 = (bf16[4,48,1536]{2,1,0:T(8,128)(2,1)}, bf16[4,48,1536]{2,1,0:T(8,128)(2,1)S(1)}, u32[]{:S(2)}, u32[]{:S(2)}) collective-permute-start(bf16[4,48,1536]{2,1,0:T(8,128)(2,1)} %get-tuple-element.105), channel_id=1, source_target_pairs={{0,8},{1,9},{2,10},{3,11},{4,12},{5,13},{6,14},{7,15},{8,16},{9,17... | collective-permute-start | bytes 1769480 | tf_op jit(solution)/shard_map/ppermute | solution.py:269
  262.6 32.5 %collective-permute-start.27 = (bf16[16,24,768]{2,1,0:T(8,128)(2,1)}, bf16[16,24,768]{2,1,0:T(8,128)(2,1)}, u32[]{:S(2)}, u32[]{:S(2)}) collective-permute-start(bf16[16,24,768]{2,1,0:T(8,128)(2,1)} %get-tuple-element.116), channel_id=1, source_target_pairs={{0,1},{1,0},{2,3},{3,2},{4,5},{5,4},{6,7},{7,6},{8,9},{9,8},{10,11... | collective-permute-start | bytes 1769480 | tf_op jit(solution)/shard_map/ppermute | solution.py:269
  264.7 19.3 %collective-permute-start.30 = (bf16[4,48,1536]{2,1,0:T(8,128)(2,1)}, bf16[4,48,1536]{2,1,0:T(8,128)(2,1)S(1)}, u32[]{:S(2)}, u32[]{:S(2)}) collective-permute-start(bf16[4,48,1536]{2,1,0:T(8,128)(2,1)} %fold.10.rest_0_), channel_id=1, source_target_pairs={{0,8},{1,9},{2,10},{3,11},{4,12},{5,13},{6,14},{7,15},{8,16},{9,17... | collective-permute-start | bytes 1769480 | tf_op jit(solution)/shard_map/ppermute | solution.py:269
  288.2 34.4 %collective-permute-start.32 = (bf16[4,48,1536]{2,1,0:T(8,128)(2,1)S(1)}, bf16[4,48,1536]{2,1,0:T(8,128)(2,1)}, u32[]{:S(2)}, u32[]{:S(2)}) collective-permute-start(bf16[4,48,1536]{2,1,0:T(8,128)(2,1)S(1)} %fold.12.refs_6_.rest_2_), channel_id=1, source_target_pairs={{0,8},{1,9},{2,10},{3,11},{4,12},{5,13},{6,14},{7,15},{8,16},{9,17... | collective-permute-start | bytes 1769480 | tf_op jit(solution)/shard_map/ppermute | solution.py:269
  294.6 25.6 %collective-permute-start.33 = (bf16[4,48,3072]{2,1,0:T(8,128)(2,1)}, bf16[4,48,3072]{2,1,0:T(8,128)(2,1)S(1)}, u32[]{:S(2)}, u32[]{:S(2)}) collective-permute-start(bf16[4,48,3072]{2,1,0:T(8,128)(2,1)} %get-tuple-element.115.refs_7_.rest_0_), channel_id=1, source_target_pairs={{0,4},{1,3},{2,6},{3,1},{4,0},{5,7},{6,2},{7,5},{8,12},{9,11},{10,... | collective-permute-start | bytes 3538952 | tf_op jit(solution)/shard_map/ppermute | solution.py:269
  299.1 28.2 %collective-permute-start.34 = (bf16[8,24,2560]{2,1,0:T(8,128)(2,1)}, bf16[8,24,2560]{2,1,0:T(8,128)(2,1)S(1)}, u32[]{:S(2)}, u32[]{:S(2)}) collective-permute-start(bf16[8,24,2560]{2,1,0:T(8,128)(2,1)} %get-tuple-element.120.rest_1_), channel_id=1, source_target_pairs={{0,2},{1,5},{2,0},{3,7},{4,6},{5,1},{6,4},{7,3},{8,10},{9,13},{10,... | collective-permute-start | bytes 2949128 | tf_op jit(solution)/shard_map/ppermute | solution.py:269
  345.1 25.7 %collective-permute-start.38 = (f32[512,768]{1,0:T(8,128)}, f32[512,768]{1,0:T(8,128)}, u32[]{:S(2)}, u32[]{:S(2)}) collective-permute-start(f32[512,768]{1,0:T(8,128)} %get-tuple-element.136), channel_id=1, source_target_pairs={{0,1},{1,0},{2,3},{3,2},{4,5},{5,4},{6,7},{7,6},{8,9},{9,8},{10,11... | collective-permute-start | bytes 4718600 | tf_op jit(solution)/shard_map/ppermute | solution.py:269
  347.0 15.1 %collective-permute-start.45 = (bf16[1,48,1536]{2,1,0:T(8,128)(2,1)}, bf16[1,48,1536]{2,1,0:T(8,128)(2,1)}, u32[]{:S(2)}, u32[]{:S(2)}) collective-permute-start(bf16[1,48,1536]{2,1,0:T(8,128)(2,1)} %get-tuple-element.133.rest_0_), channel_id=1, source_target_pairs={{0,4},{1,3},{2,6},{3,1},{4,0},{5,7},{6,2},{7,5},{8,12},{9,11},{10,... | collective-permute-start | bytes 442376 | tf_op jit(solution)/shard_map/ppermute | solution.py:269
  357.7 16.8 %collective-permute-start.41 = (bf16[1,24,3328]{2,1,0:T(8,128)(2,1)S(1)}, bf16[1,24,3328]{2,1,0:T(8,128)(2,1)S(1)}, u32[]{:S(2)}, u32[]{:S(2)}) collective-permute-start(bf16[1,24,3328]{2,1,0:T(8,128)(2,1)S(1)} %get-tuple-element.140), channel_id=1, source_target_pairs={{0,8},{1,9},{2,10},{3,11},{4,12},{5,13},{6,14},{7,15},{8,16},{9,17... | collective-permute-start | bytes 479240 | tf_op jit(solution)/shard_map/ppermute | solution.py:269
  357.8 19.6 %collective-permute-start.42 = (bf16[1,24,3328]{2,1,0:T(8,128)(2,1)S(1)}, bf16[1,24,3328]{2,1,0:T(8,128)(2,1)S(1)}, u32[]{:S(2)}, u32[]{:S(2)}) collective-permute-start(bf16[1,24,3328]{2,1,0:T(8,128)(2,1)S(1)} %get-tuple-element.141), channel_id=1, source_target_pairs={{0,16},{1,17},{2,18},{3,19},{4,20},{5,21},{6,22},{7,23},{8,24},{9,... | collective-permute-start | bytes 479240 | tf_op jit(solution)/shard_map/ppermute | solution.py:269
  362.1 15.3 %collective-permute-start.43 = (bf16[1,24,3328]{2,1,0:T(8,128)(2,1)S(1)}, bf16[1,24,3328]{2,1,0:T(8,128)(2,1)S(1)}, u32[]{:S(2)}, u32[]{:S(2)}) collective-permute-start(bf16[1,24,3328]{2,1,0:T(8,128)(2,1)S(1)} %get-tuple-element.142), channel_id=1, source_target_pairs={{0,24},{1,25},{2,26},{3,27},{4,28},{5,29},{6,30},{7,31},{8,0},{9,1... | collective-permute-start | bytes 479240 | tf_op jit(solution)/shard_map/ppermute | solution.py:269
  (74 other events, 531.9 us)

commit v2 on v1

--- a/solution.py
+++ b/solution.py
@@ -349,13 +349,17 @@
 
 
 def place(core, mine, there):
-    def body(c, a, b, out, sem):
-        first = pltpu.make_async_copy(a, out.at[c[0]], sem.at[0])
-        second = pltpu.make_async_copy(b, out.at[1 - c[0]], sem.at[1])
+    def body(c, a, b, out, token, held, sem):
+        first = pltpu.make_async_copy(a, held.at[c[0]], sem.at[0])
+        second = pltpu.make_async_copy(b, held.at[1 - c[0]], sem.at[1])
         first.start()
         second.start()
         first.wait()
         second.wait()
+        last = pltpu.make_async_copy(held, out, sem.at[2])
+        last.start()
+        last.wait()
+        token[...] = jnp.zeros_like(token)
 
     return pl.pallas_call(
         body,
@@ -363,10 +367,13 @@
             num_scalar_prefetch=1,
             grid=(1,),
             in_specs=[ANY, ANY],
-            out_specs=pl.BlockSpec((2,) + mine.shape, lambda i, c: (0, 0, 0)),
-            scratch_shapes=[pltpu.SemaphoreType.DMA((2,))],
+            out_specs=[AFTER, pl.BlockSpec((8, LANES), lambda i, c: (0, 0))],
+            scratch_shapes=[
+                pltpu.VMEM((2,) + mine.shape, mine.dtype),
+                pltpu.SemaphoreType.DMA((3,)),
+            ],
         ),
-        out_shape=jax.ShapeDtypeStruct((2,) + mine.shape, mine.dtype),
+        out_shape=[jax.ShapeDtypeStruct((2,) + mine.shape, mine.dtype), TOKEN],
         compiler_params=params(60),
         cost_estimate=cost(0, 4 * mine.size),
         name="place",
@@ -424,6 +431,9 @@
 
 def dot_tn(a, b):
     return lax.dot_general(a, b, (((0,), (0,)), ((), ())), preferred_element_type=F32)
+
+
+TOKEN = jax.ShapeDtypeStruct((8, LANES), F32)
 
 
 def stacked(low_lane, pair):
@@ -527,7 +537,8 @@
 def attn_backward(at, grad_at, bounds, saved, ctx_grad, source, cosine, sine, seg_col, seg_row, deps=()):
     def body(bnd, q, k, v, o, do, lse, x, cos, sin, sc, sr, *rest):
         core = bnd[2 * NBLOCK]
-        out, mine, theirs, qm, dm, dq, dk, dv, dl = rest[len(deps) :]
+        out, mine, theirs, token, qm, dm, dq, dk, dv, dl = rest[len(deps) :]
+        token[...] = jnp.zeros_like(token)
         low_lane = lax.broadcasted_iota(jnp.int32, (BLOCK, LANES), 1) < HEAD
         row = lax.broadcasted_iota(jnp.int32, (8, LANES), 0)
         lane = lax.broadcasted_iota(jnp.int32, (8, LANES), 1)
@@ -611,7 +622,7 @@
                 full((1, SEQ)),
             ]
             + [AFTER] * len(deps),
-            out_specs=[full((3, SEQ, GROUP)), full(dealt), full(dealt)],
+            out_specs=[full((3, SEQ, GROUP)), full(dealt), full(dealt), full((8, LANES))],
             scratch_shapes=[
                 low2,
                 low2,
@@ -625,6 +636,7 @@
             jax.ShapeDtypeStruct((3, SEQ, GROUP), BF16),
             jax.ShapeDtypeStruct(dealt, BF16),
             jax.ShapeDtypeStruct(dealt, BF16),
+            TOKEN,
         ],
         compiler_params=params(60),
         cost_estimate=cost(GROUP * (40 * SEQ * SEQ + 6 * SEQ * D), 10 << 20, 4 * SEQ * SEQ),
@@ -800,7 +812,8 @@
     half = SEQ // 2 // BLOCK
 
     def body(c, hid, a, b, d, w, *rest):
-        mine, leave = rest[-2:]
+        mine, leave, token = rest[-3:]
+        token[...] = jnp.zeros_like(token)
         total = hid[...]
         for g, ref in enumerate((a, b, d)):
             for i in range(3):
@@ -832,9 +845,10 @@
                 pl.BlockSpec(
                     (BLOCK, D), lambda r, c: (jnp.clip(r - half * (1 - c[0]), 0, half - 1), 0)
                 ),
+                pl.BlockSpec((8, LANES), lambda r, c: (0, 0)),
             ],
         ),
-        out_shape=[shape, shape],
+        out_shape=[shape, shape, TOKEN],
         compiler_params=params(60),
         cost_estimate=cost(6 * SEQ * D * D, 16 << 20),
         name="input_back",
@@ -1168,19 +1182,20 @@
     )
 
     gu_there, down_there = core_swap(gu_there), core_swap(down_there)
+    output, placed = place(core, out, core_swap(out_leave))
     tail_mine, tail_theirs = out_grad(core, ctx, att_grad, sums)
-    gu_keep, gu_send = join_rows(to_here, gu_here, gu_there, 2, deps=(tail_mine,))
+    gu_keep, gu_send = join_rows(to_here, gu_here, gu_there, 2, deps=(tail_mine, placed))
     down_parts = join_rows(deep_first, down_here, down_there, 4, deps=(gu_send,))
     gu_first = first_swap(gu_send)
     passing = depth_shift(down_parts[3], 1)
 
     common = (source,) + tables
     back0 = attn_backward(0, 0, bounds, saved0, ctx_grad, *common, deps=(gu_send, down_parts[0]))
-    (passing,) = fold(passing, down_parts[2], 1, deps=(back0[1],))
+    (passing,) = fold(passing, down_parts[2], 1, deps=(back0[3],))
     back1 = attn_backward(0, 1, bounds, saved1, ctx_grad, *common, deps=(passing,))
     passing = depth_shift(passing, 1)
-    (passing,) = fold(passing, down_parts[1], 1, deps=(back1[1],))
-    gu_keep, gu_send = fold(gu_keep, gu_first, 2, deps=(back1[1],))
+    (passing,) = fold(passing, down_parts[1], 1, deps=(back1[3],))
+    gu_keep, gu_send = fold(gu_keep, gu_first, 2, deps=(back1[3],))
     gu_second = second_swap(gu_send)
     early_keep, early_send = join_dealt(
         to_here,
@@ -1193,7 +1208,7 @@
 
     deep = lambda parts: [parts[0]] + [depth_shift(parts[k], k) for k in (1, 2, 3)]
     passing = depth_shift(passing, 1)
-    gu_parts = fold(gu_keep, gu_second, 4, deps=(back2[1],))
+    gu_parts = fold(gu_keep, gu_second, 4, deps=(back2[3],))
     down_keep, down_send = fold(passing, down_parts[0], 2, deps=(gu_parts[0],))
     late_keep, late_send = join_dealt(
         to_here, (back2[1],), (core_swap(back2[2]),), deps=(down_send, early_first)
@@ -1206,19 +1221,22 @@
         (early_keep, late_keep), (early_first, late_first), deps=(gu_total,)
     )
     attn_second = second_swap(attn_send)
-    grad, grad_leave = input_back(
+    grad, grad_leave, added = input_back(
         core, hidden_grad, (back0[0], back1[0], back2[0]), weights, deps=(attn_send,)
     )
-    (gu_total,) = fold(depth_shift(gu_total, 1), gu_parts[1], 1, deps=(grad,))
-    attn_parts = deep(fold(attn_keep, attn_second, 4, deps=(gu_total,)))
-    (gu_total,) = fold(depth_shift(gu_total, 1), gu_parts[0], 1, F32, deps=(attn_parts[0],))
-    outputs = place(core, out, core_swap(out_leave)), place(core, grad, core_swap(grad_leave))
+    (gu_total,) = fold(depth_shift(gu_total, 1), gu_parts[1], 1, deps=(added,))
+    attn_parts = list(fold(attn_keep, attn_second, 4, deps=(gu_total,)))
+    grad_leave, attn_parts[0] = lax.optimization_barrier((grad_leave, attn_parts[0]))
+    attn_parts = deep(attn_parts)
+    grad, placed = place(core, grad, core_swap(grad_leave))
+    (gu_total,) = fold(depth_shift(gu_total, 1), gu_parts[0], 1, F32)
     down_total = (down_keep.astype(F32) + down_second.astype(F32))[0]
     gu_total = gu_total[0]
-    qkv_total, out_total, gain_total, shift_total = finish(attn_parts, deps=outputs)
+    qkv_total, out_total, gain_total, shift_total = finish(attn_parts, deps=(placed,))
 
     return (
-        *outputs,
+        output,
+        grad,
         qkv_total,
         out_total,
         gain_total,

time: 390 us -> 383 us (0.982)
  starting transfers between devices: 36.7 us -> 42.4 us
  waiting for transfers between devices: 66.8 us -> 61.3 us
  Pallas kernels: 238 us -> 234 us
    ppermute x46, starting transfers between devices: 36.7 us -> 42.4 us  [across(): return lax.ppermute(value, ('dp', 'tensor'), pairs)]
    ppermute x46, waiting for transfers between devices: 66.8 us -> 61.3 us  [across(): return lax.ppermute(value, ('dp', 'tensor'), pairs)]
    unnamed x127 -> x121, local copies, waits for them, and re-layouts: 20.5 us -> 19.2 us
  transfers between devices with their start and end apart: 46 -> 46, of which waited for: 16 -> 13; matrix products, arithmetic and copies ran while one was open for 5% -> 5% of each run, Pallas kernels for 37% -> 39%
where the time goes in v2:
time: 383 us; the launch traced here: 377 us
  Pallas kernels  234 us (61%)
  waiting for transfers between devices  61.3 us (16%)
  starting transfers between devices  42.4 us (11%)
  local copies, waits for them, and re-layouts  28.4 us (7%)
  other arithmetic  8.99 us (2%)
    pallas_call x1, Pallas kernels, middle(): pl.pallas_call(body, grid_spec=pltpu.PrefetchScalarGridSpec(num_scalar_pr...  81.9 us
    ppermute x46, waiting for transfers between devices, across(): return lax.ppermute(value, ('dp', 'tensor'), pairs)  61.3 us
    pallas_call x3, Pallas kernels, attn_backward(): pl.pallas_call(body, grid_spec=pltpu.PrefetchScalarGridSpec(num_scalar_pr...  54.1 us
    ppermute x46, starting transfers between devices, across(): return lax.ppermute(value, ('dp', 'tensor'), pairs)  42.4 us
    pallas_call x3, Pallas kernels, attn_forward(): pl.pallas_call(body, grid_spec=pltpu.PrefetchScalarGridSpec(num_scalar_pr...  41.7 us
    unnamed x121, local copies, waits for them, and re-layouts  19.2 us
    pallas_call x2, Pallas kernels, join_rows(): pl.pallas_call(body, grid_spec=pltpu.PrefetchScalarGridSpec(num_scalar_pr...  13.1 us
    pallas_call x1, Pallas kernels, input_back(): pl.pallas_call(body, grid_spec=pltpu.PrefetchScalarGridSpec(num_scalar_pr...  9.45 us
  transfers between devices with their start and end apart: 46, of which 13 were waited for; matrix products, arithmetic and copies ran while one was open for 5% of the time, Pallas kernels for 39%

profile of v2, /device:TPU:0, one launch (start us, length us, event | category | flops | bytes accessed | tf_op | source)
XLA Modules:
  0.0 377.2 jit_solution(1249579362802007468)
XLA Ops:
  1.6 5.0 %collective-permute-start.2 = (bf16[24,2304]{1,0:T(8,128)(2,1)S(1)}, bf16[24,2304]{1,0:T(8,128)(2,1)S(1)}, u32[]{:S(2)}, u32[]{:S(2)}) collective-permute-start(bf16[24,2304]{1,0:T(8,128)(2,1)S(1)} %bitcast.52), channel_id=1, source_target_pairs={{0,24},{1,25},{2,26},{3,27},{4,28},{5,29},{6,30},{7,31},{8,0},{9,1... | collective-permute-start | bytes 331784 | tf_op jit(solution)/shard_map/ppermute | solution.py:269
  11.2 2.6 constant_dynamic-slice_fusion
  14.5 8.1 %collective-permute-done.1 = bf16[24,2304]{1,0:T(8,128)(2,1)S(1)} collective-permute-done((bf16[24,2304]{1,0:T(8,128)(2,1)S(1)}, bf16[24,2304]{1,0:T(8,128)(2,1)S(1)}, u32[]{:S(2)}, u32[]{:S(2)}) %collective-permute-start.1) | collective-permute-done | bytes 110624 | tf_op jit(solution)/shard_map/ppermute | solution.py:269
  31.1 5.5 %collective-permute-done.5.refs_2_ = bf16[48,3072]{1,0:T(8,128)(2,1)S(1)} collective-permute-done((bf16[48,3072]{1,0:T(8,128)(2,1)S(1)}, bf16[48,3072]{1,0:T(8,128)(2,1)S(1)}, u32[]{:S(2)}, u32[]{:S(2)}) %collective-permute-start.5) | collective-permute-done | bytes 294944 | tf_op jit(solution)/shard_map/ppermute | solution.py:269
  42.2 10.3 %collective-permute-done.7.b = bf16[8,24,2304]{2,1,0:T(8,128)(2,1)} collective-permute-done((bf16[8,24,2304]{2,1,0:T(8,128)(2,1)S(1)}, bf16[8,24,2304]{2,1,0:T(8,128)(2,1)}, u32[]{:S(2)}, u32[]{:S(2)}) %collective-permute-start.7) | collective-permute-done | bytes 884768 | tf_op jit(solution)/shard_map/ppermute | solution.py:269
  59.5 4.8 %assemble.1 = bf16[32,24,2304]{2,1,0:T(8,128)(2,1)} custom-call(s32[32]{0:T(128)} %pad_add_fusion.2.idx, bf16[8,24,2304]{2,1,0:T(8,128)(2,1)} %copy-done.6, bf16[8,24,2304]{2,1,0:T(8,128)(2,1)} %collective-permute-done.7.b, bf16[8,24,2304]{2,1,0:T(8,128)(2,1)} %copy-done.51, bf16[8,24,2304]{2,1,0:T(8,128)(2,1)} %collective-permute-done.9.d, ...), custom_call_target="tpu_custom_call" | custom-call | bytes 7077888 | tf_op jit(solution)/shard_map/assemble/pallas_call | solution.py:398
  64.3 13.8 %attn_forward.3 = (bf16[1024,256]{1,0:T(8,128)(2,1)}, bf16[1024,256]{1,0:T(8,128)(2,1)}, bf16[1024,256]{1,0:T(8,128)(2,1)}, bf16[1024,256]{1,0:T(8,128)(2,1)}, f32[1,8,1024]{2,1,0:T(8,128)}) custom-call(s32[9]{0:T(128)} %pad_add_fusion.1.bnd, bf16[1024,768]{1,0:T(8,128)(2,1)} %copy-done.4, bf16[768,2304]{1,0:T(8,128)(2,1)} %bitcast.39, ...), custom_call_target="tpu_custom_call" | custom-call | flops 5502926848 | bytes 8388608 | tf_op jit(solution)/shard_map/attn_forward/pallas_call | solution.py:502
  80.4 3.0 pile.10.rest_0_.refs_0_
  85.1 13.8 %attn_forward.4 = (bf16[1024,256]{1,0:T(8,128)(2,1)}, bf16[1024,256]{1,0:T(8,128)(2,1)}, bf16[1024,256]{1,0:T(8,128)(2,1)}, bf16[1024,256]{1,0:T(8,128)(2,1)}, f32[1,8,1024]{2,1,0:T(8,128)}) custom-call(s32[9]{0:T(128)} %pad_add_fusion.1.bnd, bf16[1024,768]{1,0:T(8,128)(2,1)} %copy-done.4, bf16[768,2304]{1,0:T(8,128)(2,1)} %bitcast.42, ...), custom_call_target="tpu_custom_call" | custom-call | flops 5502926848 | bytes 8388608 | tf_op jit(solution)/shard_map/attn_forward/pallas_call | solution.py:502
  98.9 4.7 %collective-permute-done.15.refs_2_ = bf16[2,48,2048]{2,1,0:T(8,128)(2,1)S(1)} collective-permute-done((bf16[2,48,2048]{2,1,0:T(8,128)(2,1)S(1)}, bf16[2,48,2048]{2,1,0:T(8,128)(2,1)S(1)}, u32[]{:S(2)}, u32[]{:S(2)}) %collective-permute-start.15) | collective-permute-done | bytes 393248 | tf_op jit(solution)/shard_map/ppermute | solution.py:269
  106.7 6.0 %collective-permute-done.16.refs_1_ = bf16[8,48,3072]{2,1,0:T(8,128)(2,1)} collective-permute-done((bf16[8,48,3072]{2,1,0:T(8,128)(2,1)}, bf16[8,48,3072]{2,1,0:T(8,128)(2,1)}, u32[]{:S(2)}, u32[]{:S(2)}) %collective-permute-start.16) | collective-permute-done | bytes 2359328 | tf_op jit(solution)/shard_map/ppermute | solution.py:269
  113.2 14.2 %attn_forward.5 = (bf16[1024,256]{1,0:T(8,128)(2,1)}, bf16[1024,256]{1,0:T(8,128)(2,1)}, bf16[1024,256]{1,0:T(8,128)(2,1)}, bf16[1024,256]{1,0:T(8,128)(2,1)}, f32[1,8,1024]{2,1,0:T(8,128)}) custom-call(s32[9]{0:T(128)} %pad_add_fusion.1.bnd, bf16[1024,768]{1,0:T(8,128)(2,1)} %copy-done.4, bf16[768,2304]{1,0:T(8,128)(2,1)} %bitcast.45, ...), custom_call_target="tpu_custom_call" | custom-call | flops 5502926848 | bytes 8388608 | tf_op jit(solution)/shard_map/attn_forward/pallas_call | solution.py:502
  130.3 3.0 collective-permute-done.21.refs_7_
  133.3 81.9 %middle.1 = (bf16[512,768]{1,0:T(8,128)(2,1)}, bf16[512,768]{1,0:T(8,128)(2,1)}, bf16[2,768,1536]{2,1,0:T(8,128)(2,1)}, bf16[2,768,1536]{2,1,0:T(8,128)(2,1)}, b...) custom-call(s32[65]{0:T(128)} %concatenate.21.idx, ...), custom_call_target="tpu_custom_call" | custom-call | flops 45902462976 | bytes 41943040 | tf_op jit(solution)/shard_map/middle/pallas_call | solution.py:1053
  217.3 4.5 %out_grad.1 = (bf16[16,24,1024]{2,1,0:T(8,128)(2,1)}, bf16[16,24,1024]{2,1,0:T(8,128)(2,1)}) custom-call(s32[1]{0:T(128)} %bitcast.c, bf16[1024,256]{1,0:T(8,128)(2,1)} %get-tuple-element.88.ctx0.refs_0_.o, bf16[1024,256]{1,0:T(8,128)(2,1)} %get-tuple-element.90.ctx1.refs_1_.o, bf16[1024,256]{1,0:T(8,128)(2,1)} %get-tuple-element.92.ctx2.refs_2_.o, ...), custom_call_target="tpu_custom_call" | custom-call | flops 1207959552 | bytes 8388608 | tf_op jit(solution)/shard_map/out_grad/pallas_call | solution.py:688
  222.2 5.5 %collective-permute-done.22.b = bf16[512,768]{1,0:T(8,128)(2,1)S(1)} collective-permute-done((bf16[512,768]{1,0:T(8,128)(2,1)}, bf16[512,768]{1,0:T(8,128)(2,1)S(1)}, u32[]{:S(2)}, u32[]{:S(2)}) %collective-permute-start.22) | collective-permute-done | bytes 786464 | tf_op jit(solution)/shard_map/ppermute | solution.py:269
  228.6 3.1 place.2
  231.7 7.9 %join_rows.2 = (bf16[8,48,3072]{2,1,0:T(8,128)(2,1)}, bf16[8,48,3072]{2,1,0:T(8,128)(2,1)}) custom-call(s32[16]{0:T(128)} %fusion.16.idx, bf16[2,768,1536]{2,1,0:T(8,128)(2,1)} %get-tuple-element.103.a, bf16[2,768,1536]{2,1,0:T(8,128)(2,1)} %collective-permute-done.23.b, bf16[16,24,1024]{2,1,0:T(8,128)(2,1)} %get-tuple-element.107.rest_0_.refs_2_, ...), custom_call_target="tpu_custom_call" | custom-call | flops 2359296 | bytes 14155776 | tf_op jit(solution)/shard_map/join_rows/pallas_call | solution.py:662
  242.5 5.2 %join_rows.3 = (bf16[4,48,1536]{2,1,0:T(8,128)(2,1)}, bf16[4,48,1536]{2,1,0:T(8,128)(2,1)}, bf16[4,48,1536]{2,1,0:T(8,128)(2,1)}, bf16[4,48,1536]{2,1,0:T(8,128)(2,1)}) custom-call(s32[16]{0:T(128)} %fusion.21.idx, bf16[1,768,1536]{2,1,0:T(8,128)(2,1)} %get-tuple-element.110.a, bf16[1,768,1536]{2,1,0:T(8,128)(2,1)} %copy-done.50, ...), custom_call_target="tpu_custom_call" | custom-call | flops 1179648 | bytes 7077888 | tf_op jit(solution)/shard_map/join_rows/pallas_call | solution.py:662
  247.7 18.0 %attn_backward.3 = (bf16[3,1024,256]{2,1,0:T(8,128)(2,1)}, bf16[16,24,768]{2,1,0:T(8,128)(2,1)}, bf16[16,24,768]{2,1,0:T(8,128)(2,1)}, f32[8,128]{1,0:T(8,128)}) custom-call(s32[9]{0:T(128)} %pad_add_fusion.1.bnd, bf16[1024,256]{1,0:T(8,128)(2,1)} %get-tuple-element.99.q, bf16[1024,256]{1,0:T(8,128)(2,1)} %get-tuple-element.100.k, ...), custom_call_target="tpu_custom_call" | custom-call | flops 11945377792 | bytes 10485760 | tf_op jit(solution)/shard_map/attn_backward/pallas_call | solution.py:609
  268.5 18.2 %attn_backward.4 = (bf16[3,1024,256]{2,1,0:T(8,128)(2,1)}, bf16[16,24,768]{2,1,0:T(8,128)(2,1)}, bf16[16,24,768]{2,1,0:T(8,128)(2,1)}, f32[8,128]{1,0:T(8,128)}) custom-call(s32[9]{0:T(128)} %pad_add_fusion.1.bnd, bf16[1024,256]{1,0:T(8,128)(2,1)} %get-tuple-element.114.q, bf16[1024,256]{1,0:T(8,128)(2,1)} %get-tuple-element.115.k, ...), custom_call_target="tpu_custom_call" | custom-call | flops 11945377792 | bytes 10485760 | tf_op jit(solution)/shard_map/attn_backward/pallas_call | solution.py:609
  293.0 3.3 fold.11
  299.7 3.0 join_dealt.2
  304.0 18.0 %attn_backward.5 = (bf16[3,1024,256]{2,1,0:T(8,128)(2,1)}, bf16[16,24,768]{2,1,0:T(8,128)(2,1)}, bf16[16,24,768]{2,1,0:T(8,128)(2,1)}, f32[8,128]{1,0:T(8,128)}) custom-call(s32[9]{0:T(128)} %pad_add_fusion.1.bnd, bf16[1024,256]{1,0:T(8,128)(2,1)} %get-tuple-element.121.q, bf16[1024,256]{1,0:T(8,128)(2,1)} %get-tuple-element.122.k, ...), custom_call_target="tpu_custom_call" | custom-call | flops 11945377792 | bytes 10485760 | tf_op jit(solution)/shard_map/attn_backward/pallas_call | solution.py:609
  326.1 3.2 collective-permute-start.37
  331.3 2.8 collective-permute-done.37.b
  334.1 4.9 %collective-permute-done.36.a = bf16[1,48,3072]{2,1,0:T(8,128)(2,1)S(1)} collective-permute-done((bf16[1,48,3072]{2,1,0:T(8,128)(2,1)S(1)}, bf16[1,48,3072]{2,1,0:T(8,128)(2,1)S(1)}, u32[]{:S(2)}, u32[]{:S(2)}) %collective-permute-start.36) | collective-permute-done | bytes 294944 | tf_op jit(solution)/shard_map/ppermute | solution.py:269
  340.3 9.4 %input_back.1 = (f32[512,768]{1,0:T(8,128)}, f32[512,768]{1,0:T(8,128)}, f32[8,128]{1,0:T(8,128)}) custom-call(s32[1]{0:T(128)} %bitcast.c, f32[1024,768]{1,0:T(8,128)} %get-tuple-element.98.hid, bf16[3,1024,256]{2,1,0:T(8,128)(2,1)} %get-tuple-element.113.a, bf16[3,1024,256]{2,1,0:T(8,128)(2,1)} %get-tuple-element.120.b, ...), custom_call_target="tpu_custom_call" | custom-call | flops 3623878656 | bytes 16777216 | tf_op jit(solution)/shard_map/input_back/pallas_call | solution.py:834
  356.5 2.9 collective-permute-start.43
  360.2 3.8 %collective-permute-done.44.a = bf16[1,48,3072]{2,1,0:T(8,128)(2,1)S(1)} collective-permute-done((bf16[1,48,3072]{2,1,0:T(8,128)(2,1)S(1)}, bf16[1,48,3072]{2,1,0:T(8,128)(2,1)S(1)}, u32[]{:S(2)}, u32[]{:S(2)}) %collective-permute-start.44) | collective-permute-done | bytes 294944 | tf_op jit(solution)/shard_map/ppermute | solution.py:269
  365.4 4.2 %place.3 = (f32[2,512,768]{2,1,0:T(8,128)}, f32[8,128]{1,0:T(8,128)}) custom-call(s32[1]{0:T(128)} %bitcast.c, f32[512,768]{1,0:T(8,128)} %get-tuple-element.150.a, f32[512,768]{1,0:T(8,128)} %collective-permute-done.40.b), custom_call_target="tpu_custom_call" | custom-call | bytes 1572864 | tf_op jit(solution)/shard_map/place/pallas_call | solution.py:364
  369.6 3.7 collective-permute-done.42.c
  (256 shorter events, 76.9 us)
Async XLA Ops:
  6.6 16.0 %collective-permute-start.1 = (bf16[24,2304]{1,0:T(8,128)(2,1)S(1)}, bf16[24,2304]{1,0:T(8,128)(2,1)S(1)}, u32[]{:S(2)}, u32[]{:S(2)}) collective-permute-start(bf16[24,2304]{1,0:T(8,128)(2,1)S(1)} %bitcast.53), channel_id=1, source_target_pairs={{0,16},{1,17},{2,18},{3,19},{4,20},{5,21},{6,22},{7,23},{8,24},{9,... | collective-permute-start | bytes 331784 | tf_op jit(solution)/shard_map/ppermute | solution.py:269
  6.6 16.0 %collective-permute-start = (bf16[24,2304]{1,0:T(8,128)(2,1)S(1)}, bf16[24,2304]{1,0:T(8,128)(2,1)S(1)}, u32[]{:S(2)}, u32[]{:S(2)}) collective-permute-start(bf16[24,2304]{1,0:T(8,128)(2,1)S(1)} %bitcast.54), channel_id=1, source_target_pairs={{0,8},{1,9},{2,10},{3,11},{4,12},{5,13},{6,14},{7,15},{8,16},{9,17... | collective-permute-start | bytes 331784 | tf_op jit(solution)/shard_map/ppermute | solution.py:269
  8.6 14.0 %collective-permute-start.3 = (bf16[48,3072]{1,0:T(8,128)(2,1)S(1)}, bf16[48,3072]{1,0:T(8,128)(2,1)S(1)}, u32[]{:S(2)}, u32[]{:S(2)}) collective-permute-start(bf16[48,3072]{1,0:T(8,128)(2,1)S(1)} %bitcast.51), channel_id=1, source_target_pairs={{0,8},{1,9},{2,10},{3,11},{4,12},{5,13},{6,14},{7,15},{8,16},{9,17... | collective-permute-start | bytes 884744 | tf_op jit(solution)/shard_map/ppermute | solution.py:269
  13.8 15.1 %collective-permute-start.6 = (bf16[512,768]{1,0:T(8,128)(2,1)}, bf16[512,768]{1,0:T(8,128)(2,1)}, u32[]{:S(2)}, u32[]{:S(2)}) collective-permute-start(bf16[512,768]{1,0:T(8,128)(2,1)} %get-tuple-element.201), channel_id=1, source_target_pairs={{0,1},{1,0},{2,3},{3,2},{4,5},{5,4},{6,7},{7,6},{8,9},{9,8},{10,11... | collective-permute-start | bytes 2359304 | tf_op jit(solution)/shard_map/ppermute | solution.py:269
  23.2 13.3 %collective-permute-start.4 = (bf16[4,24,2304]{2,1,0:T(8,128)(2,1)S(1)}, bf16[4,24,2304]{2,1,0:T(8,128)(2,1)S(1)}, u32[]{:S(2)}, u32[]{:S(2)}) collective-permute-start(bf16[4,24,2304]{2,1,0:T(8,128)(2,1)S(1)} %pile.6.refs_0_), channel_id=1, source_target_pairs={{0,2},{1,5},{2,0},{3,7},{4,6},{5,1},{6,4},{7,3},{8,10},{9,13},{10,... | collective-permute-start | bytes 1327112 | tf_op jit(solution)/shard_map/ppermute | solution.py:269
  37.2 15.3 %collective-permute-start.7 = (bf16[8,24,2304]{2,1,0:T(8,128)(2,1)S(1)}, bf16[8,24,2304]{2,1,0:T(8,128)(2,1)}, u32[]{:S(2)}, u32[]{:S(2)}) collective-permute-start(bf16[8,24,2304]{2,1,0:T(8,128)(2,1)S(1)} %pile.7.a), channel_id=1, source_target_pairs={{0,4},{1,3},{2,6},{3,1},{4,0},{5,7},{6,2},{7,5},{8,12},{9,11},{10,... | collective-permute-start | bytes 2654216 | tf_op jit(solution)/shard_map/ppermute | solution.py:269
  38.1 14.6 %collective-permute-start.10 = (bf16[48,3072]{1,0:T(8,128)(2,1)S(1)}, bf16[48,3072]{1,0:T(8,128)(2,1)S(1)}, u32[]{:S(2)}, u32[]{:S(2)}) collective-permute-start(bf16[48,3072]{1,0:T(8,128)(2,1)S(1)} %collective-permute-done.5.refs_2_), channel_id=1, source_target_pairs={{0,8},{1,9},{2,10},{3,11},{4,12},{5,13},{6,14},{7,15},{8,16},{9,17... | collective-permute-start | bytes 884744 | tf_op jit(solution)/shard_map/ppermute | solution.py:269
  39.1 16.7 %collective-permute-start.11 = (bf16[48,2048]{1,0:T(8,128)(2,1)S(1)}, bf16[48,2048]{1,0:T(8,128)(2,1)S(1)}, u32[]{:S(2)}, u32[]{:S(2)}) collective-permute-start(bf16[48,2048]{1,0:T(8,128)(2,1)S(1)} %get-tuple-element.202), channel_id=1, source_target_pairs={{0,2},{1,5},{2,0},{3,7},{4,6},{5,1},{6,4},{7,3},{8,10},{9,13},{10,... | collective-permute-start | bytes 589832 | tf_op jit(solution)/shard_map/ppermute | solution.py:269
  42.1 16.5 %collective-permute-start.8 = (bf16[8,24,2304]{2,1,0:T(8,128)(2,1)S(1)}, bf16[8,24,2304]{2,1,0:T(8,128)(2,1)S(1)}, u32[]{:S(2)}, u32[]{:S(2)}) collective-permute-start(bf16[8,24,2304]{2,1,0:T(8,128)(2,1)S(1)} %pile.7.a), channel_id=1, source_target_pairs={{0,1},{1,0},{2,3},{3,2},{4,5},{5,4},{6,7},{7,6},{8,9},{9,8},{10,11... | collective-permute-start | bytes 2654216 | tf_op jit(solution)/shard_map/ppermute | solution.py:269
  53.1 25.0 %collective-permute-start.12 = (bf16[4,48,3072]{2,1,0:T(8,128)(2,1)S(1)}, bf16[4,48,3072]{2,1,0:T(8,128)(2,1)}, u32[]{:S(2)}, u32[]{:S(2)}) collective-permute-start(bf16[4,48,3072]{2,1,0:T(8,128)(2,1)S(1)} %pile.8.refs_2_.rest_0_.refs_0_), channel_id=1, source_target_pairs={{0,2},{1,5},{2,0},{3,7},{4,6},{5,1},{6,4},{7,3},{8,10},{9,13},{10,... | collective-permute-start | bytes 3538952 | tf_op jit(solution)/shard_map/ppermute | solution.py:269
  56.3 21.8 %collective-permute-start.14 = (bf16[2,48,2048]{2,1,0:T(8,128)(2,1)S(1)}, bf16[2,48,2048]{2,1,0:T(8,128)(2,1)S(1)}, u32[]{:S(2)}, u32[]{:S(2)}) collective-permute-start(bf16[2,48,2048]{2,1,0:T(8,128)(2,1)S(1)} %pile.9.rest_1_.refs_0_), channel_id=1, source_target_pairs={{0,24},{1,25},{2,26},{3,27},{4,28},{5,29},{6,30},{7,31},{8,0},{9,1... | collective-permute-start | bytes 1179656 | tf_op jit(solution)/shard_map/ppermute | solution.py:269
  56.9 21.1 %collective-permute-start.13 = (bf16[2,48,2048]{2,1,0:T(8,128)(2,1)S(1)}, bf16[2,48,2048]{2,1,0:T(8,128)(2,1)S(1)}, u32[]{:S(2)}, u32[]{:S(2)}) collective-permute-start(bf16[2,48,2048]{2,1,0:T(8,128)(2,1)S(1)} %pile.9.rest_1_.refs_0_), channel_id=1, source_target_pairs={{0,8},{1,9},{2,10},{3,11},{4,12},{5,13},{6,14},{7,15},{8,16},{9,17... | collective-permute-start | bytes 1179656 | tf_op jit(solution)/shard_map/ppermute | solution.py:269
  83.5 29.2 %collective-permute-start.16 = (bf16[8,48,3072]{2,1,0:T(8,128)(2,1)}, bf16[8,48,3072]{2,1,0:T(8,128)(2,1)}, u32[]{:S(2)}, u32[]{:S(2)}) collective-permute-start(bf16[8,48,3072]{2,1,0:T(8,128)(2,1)} %pile.10.rest_0_.refs_0_), channel_id=1, source_target_pairs={{0,4},{1,3},{2,6},{3,1},{4,0},{5,7},{6,2},{7,5},{8,12},{9,11},{10,... | collective-permute-start | bytes 7077896 | tf_op jit(solution)/shard_map/ppermute | solution.py:269
  84.3 19.2 %collective-permute-start.15 = (bf16[2,48,2048]{2,1,0:T(8,128)(2,1)S(1)}, bf16[2,48,2048]{2,1,0:T(8,128)(2,1)S(1)}, u32[]{:S(2)}, u32[]{:S(2)}) collective-permute-start(bf16[2,48,2048]{2,1,0:T(8,128)(2,1)S(1)} %copy-done.15), channel_id=1, source_target_pairs={{0,16},{1,17},{2,18},{3,19},{4,20},{5,21},{6,22},{7,23},{8,24},{9,... | collective-permute-start | bytes 1179656 | tf_op jit(solution)/shard_map/ppermute | solution.py:269
  105.1 24.4 %collective-permute-start.19 = (bf16[8,48,2048]{2,1,0:T(8,128)(2,1)S(1)}, bf16[8,48,2048]{2,1,0:T(8,128)(2,1)}, u32[]{:S(2)}, u32[]{:S(2)}) collective-permute-start(bf16[8,48,2048]{2,1,0:T(8,128)(2,1)S(1)} %pile.11.rest_0_.refs_4_), channel_id=1, source_target_pairs={{0,4},{1,3},{2,6},{3,1},{4,0},{5,7},{6,2},{7,5},{8,12},{9,11},{10,... | collective-permute-start | bytes 4718600 | tf_op jit(solution)/shard_map/ppermute | solution.py:269
  106.7 23.6 %collective-permute-start.17 = (bf16[8,48,3072]{2,1,0:T(8,128)(2,1)}, bf16[8,48,3072]{2,1,0:T(8,128)(2,1)}, u32[]{:S(2)}, u32[]{:S(2)}) collective-permute-start(bf16[8,48,3072]{2,1,0:T(8,128)(2,1)} %pile.10.rest_0_.refs_0_), channel_id=1, source_target_pairs={{0,1},{1,0},{2,3},{3,2},{4,5},{5,4},{6,7},{7,6},{8,9},{9,8},{10,11... | collective-permute-start | bytes 7077896 | tf_op jit(solution)/shard_map/ppermute | solution.py:269
  112.7 20.6 %collective-permute-start.18 = (bf16[8,48,3072]{2,1,0:T(8,128)(2,1)}, bf16[8,48,3072]{2,1,0:T(8,128)(2,1)}, u32[]{:S(2)}, u32[]{:S(2)}) collective-permute-start(bf16[8,48,3072]{2,1,0:T(8,128)(2,1)} %collective-permute-done.16.refs_1_), channel_id=1, source_target_pairs={{0,1},{1,0},{2,3},{3,2},{4,5},{5,4},{6,7},{7,6},{8,9},{9,8},{10,11... | collective-permute-start | bytes 7077896 | tf_op jit(solution)/shard_map/ppermute | solution.py:269
  112.7 17.6 %collective-permute-start.20 = (bf16[8,48,2048]{2,1,0:T(8,128)(2,1)S(1)}, bf16[8,48,2048]{2,1,0:T(8,128)(2,1)}, u32[]{:S(2)}, u32[]{:S(2)}) collective-permute-start(bf16[8,48,2048]{2,1,0:T(8,128)(2,1)S(1)} %pile.11.rest_0_.refs_4_), channel_id=1, source_target_pairs={{0,1},{1,0},{2,3},{3,2},{4,5},{5,4},{6,7},{7,6},{8,9},{9,8},{10,11... | collective-permute-start | bytes 4718600 | tf_op jit(solution)/shard_map/ppermute | solution.py:269
  215.2 16.5 %collective-permute-start.23 = (bf16[2,768,1536]{2,1,0:T(8,128)(2,1)}, bf16[2,768,1536]{2,1,0:T(8,128)(2,1)}, u32[]{:S(2)}, u32[]{:S(2)}) collective-permute-start(bf16[2,768,1536]{2,1,0:T(8,128)(2,1)} %get-tuple-element.104), channel_id=1, source_target_pairs={{0,1},{1,0},{2,3},{3,2},{4,5},{5,4},{6,7},{7,6},{8,9},{9,8},{10,11... | collective-permute-start | bytes 14155784 | tf_op jit(solution)/shard_map/ppermute | solution.py:269
  215.4 25.6 %collective-permute-start.24 = (bf16[1,768,1536]{2,1,0:T(8,128)(2,1)}, bf16[1,768,1536]{2,1,0:T(8,128)(2,1)S(1)}, u32[]{:S(2)}, u32[]{:S(2)}) collective-permute-start(bf16[1,768,1536]{2,1,0:T(8,128)(2,1)} %get-tuple-element.111), channel_id=1, source_target_pairs={{0,1},{1,0},{2,3},{3,2},{4,5},{5,4},{6,7},{7,6},{8,9},{9,8},{10,11... | collective-permute-start | bytes 7077896 | tf_op jit(solution)/shard_map/ppermute | solution.py:269
  221.8 77.9 %collective-permute-start.29 = (bf16[16,24,1024]{2,1,0:T(8,128)(2,1)}, bf16[16,24,1024]{2,1,0:T(8,128)(2,1)S(1)}, u32[]{:S(2)}, u32[]{:S(2)}) collective-permute-start(bf16[16,24,1024]{2,1,0:T(8,128)(2,1)} %get-tuple-element.132), channel_id=1, source_target_pairs={{0,1},{1,0},{2,3},{3,2},{4,5},{5,4},{6,7},{7,6},{8,9},{9,8},{10,11... | collective-permute-start | bytes 2359304 | tf_op jit(solution)/shard_map/ppermute | solution.py:269
  239.6 53.3 %collective-permute-start.26 = (bf16[8,48,3072]{2,1,0:T(8,128)(2,1)}, bf16[8,48,3072]{2,1,0:T(8,128)(2,1)}, u32[]{:S(2)}, u32[]{:S(2)}) collective-permute-start(bf16[8,48,3072]{2,1,0:T(8,128)(2,1)} %get-tuple-element.109.rest_0_), channel_id=1, source_target_pairs={{0,2},{1,5},{2,0},{3,7},{4,6},{5,1},{6,4},{7,3},{8,10},{9,13},{10,... | collective-permute-start | bytes 7077896 | tf_op jit(solution)/shard_map/ppermute | solution.py:269
  247.6 18.0 %collective-permute-start.25 = (bf16[4,48,1536]{2,1,0:T(8,128)(2,1)}, bf16[4,48,1536]{2,1,0:T(8,128)(2,1)S(1)}, u32[]{:S(2)}, u32[]{:S(2)}) collective-permute-start(bf16[4,48,1536]{2,1,0:T(8,128)(2,1)} %get-tuple-element.117), channel_id=1, source_target_pairs={{0,8},{1,9},{2,10},{3,11},{4,12},{5,13},{6,14},{7,15},{8,16},{9,17... | collective-permute-start | bytes 1769480 | tf_op jit(solution)/shard_map/ppermute | solution.py:269
  265.6 34.0 %collective-permute-start.27 = (bf16[16,24,768]{2,1,0:T(8,128)(2,1)}, bf16[16,24,768]{2,1,0:T(8,128)(2,1)}, u32[]{:S(2)}, u32[]{:S(2)}) collective-permute-start(bf16[16,24,768]{2,1,0:T(8,128)(2,1)} %get-tuple-element.130), channel_id=1, source_target_pairs={{0,1},{1,0},{2,3},{3,2},{4,5},{5,4},{6,7},{7,6},{8,9},{9,8},{10,11... | collective-permute-start | bytes 1769480 | tf_op jit(solution)/shard_map/ppermute | solution.py:269
  267.4 19.4 %collective-permute-start.30 = (bf16[4,48,1536]{2,1,0:T(8,128)(2,1)}, bf16[4,48,1536]{2,1,0:T(8,128)(2,1)S(1)}, u32[]{:S(2)}, u32[]{:S(2)}) collective-permute-start(bf16[4,48,1536]{2,1,0:T(8,128)(2,1)} %fold.10.rest_0_), channel_id=1, source_target_pairs={{0,8},{1,9},{2,10},{3,11},{4,12},{5,13},{6,14},{7,15},{8,16},{9,17... | collective-permute-start | bytes 1769480 | tf_op jit(solution)/shard_map/ppermute | solution.py:269
  290.6 34.2 %collective-permute-start.32 = (bf16[4,48,1536]{2,1,0:T(8,128)(2,1)S(1)}, bf16[4,48,1536]{2,1,0:T(8,128)(2,1)}, u32[]{:S(2)}, u32[]{:S(2)}) collective-permute-start(bf16[4,48,1536]{2,1,0:T(8,128)(2,1)S(1)} %fold.12.refs_6_.rest_2_), channel_id=1, source_target_pairs={{0,8},{1,9},{2,10},{3,11},{4,12},{5,13},{6,14},{7,15},{8,16},{9,17... | collective-permute-start | bytes 1769480 | tf_op jit(solution)/shard_map/ppermute | solution.py:269
  297.3 25.5 %collective-permute-start.33 = (bf16[4,48,3072]{2,1,0:T(8,128)(2,1)}, bf16[4,48,3072]{2,1,0:T(8,128)(2,1)S(1)}, u32[]{:S(2)}, u32[]{:S(2)}) collective-permute-start(bf16[4,48,3072]{2,1,0:T(8,128)(2,1)} %get-tuple-element.127.refs_7_.rest_0_), channel_id=1, source_target_pairs={{0,4},{1,3},{2,6},{3,1},{4,0},{5,7},{6,2},{7,5},{8,12},{9,11},{10,... | collective-permute-start | bytes 3538952 | tf_op jit(solution)/shard_map/ppermute | solution.py:269
  303.6 25.8 %collective-permute-start.34 = (bf16[8,24,2560]{2,1,0:T(8,128)(2,1)}, bf16[8,24,2560]{2,1,0:T(8,128)(2,1)S(1)}, u32[]{:S(2)}, u32[]{:S(2)}) collective-permute-start(bf16[8,24,2560]{2,1,0:T(8,128)(2,1)} %get-tuple-element.134.rest_1_), channel_id=1, source_target_pairs={{0,2},{1,5},{2,0},{3,7},{4,6},{5,1},{6,4},{7,3},{8,10},{9,13},{10,... | collective-permute-start | bytes 2949128 | tf_op jit(solution)/shard_map/ppermute | solution.py:269
  350.7 14.7 %collective-permute-start.40 = (f32[512,768]{1,0:T(8,128)}, f32[512,768]{1,0:T(8,128)}, u32[]{:S(2)}, u32[]{:S(2)}) collective-permute-start(f32[512,768]{1,0:T(8,128)} %get-tuple-element.156), channel_id=1, source_target_pairs={{0,1},{1,0},{2,3},{3,2},{4,5},{5,4},{6,7},{7,6},{8,9},{9,8},{10,11... | collective-permute-start | bytes 4718600 | tf_op jit(solution)/shard_map/ppermute | solution.py:269
  352.9 16.7 %collective-permute-start.41 = (bf16[1,24,3328]{2,1,0:T(8,128)(2,1)S(1)}, bf16[1,24,3328]{2,1,0:T(8,128)(2,1)S(1)}, u32[]{:S(2)}, u32[]{:S(2)}) collective-permute-start(bf16[1,24,3328]{2,1,0:T(8,128)(2,1)S(1)} %get-tuple-element.159), channel_id=1, source_target_pairs={{0,8},{1,9},{2,10},{3,11},{4,12},{5,13},{6,14},{7,15},{8,16},{9,17... | collective-permute-start | bytes 479240 | tf_op jit(solution)/shard_map/ppermute | solution.py:269
  354.8 18.4 %collective-permute-start.42 = (bf16[1,24,3328]{2,1,0:T(8,128)(2,1)S(1)}, bf16[1,24,3328]{2,1,0:T(8,128)(2,1)S(1)}, u32[]{:S(2)}, u32[]{:S(2)}) collective-permute-start(bf16[1,24,3328]{2,1,0:T(8,128)(2,1)S(1)} %get-tuple-element.160), channel_id=1, source_target_pairs={{0,16},{1,17},{2,18},{3,19},{4,20},{5,21},{6,22},{7,23},{8,24},{9,... | collective-permute-start | bytes 479240 | tf_op jit(solution)/shard_map/ppermute | solution.py:269
  356.5 16.7 %collective-permute-start.43 = (bf16[1,24,3328]{2,1,0:T(8,128)(2,1)S(1)}, bf16[1,24,3328]{2,1,0:T(8,128)(2,1)S(1)}, u32[]{:S(2)}, u32[]{:S(2)}) collective-permute-start(bf16[1,24,3328]{2,1,0:T(8,128)(2,1)S(1)} %get-tuple-element.161), channel_id=1, source_target_pairs={{0,24},{1,25},{2,26},{3,27},{4,28},{5,29},{6,30},{7,31},{8,0},{9,1... | collective-permute-start | bytes 479240 | tf_op jit(solution)/shard_map/ppermute | solution.py:269
  (71 other events, 528.1 us)

commit v3 on v2

--- a/solution.py
+++ b/solution.py
@@ -250,7 +250,7 @@
 NBLOCK = SEQ // BLOCK
 ROWS = 256
 STEPS = SEQ // ROWS
-CHUNK = 512
+CHUNK = 768
 PIECE = 256
 PIECES = 2 * HIDDEN // PIECE
 LOG2E = 1.4426950408889634
@@ -598,8 +598,8 @@
                 out[1, rows, ln] = turn(dk[rows, ln], cr, sn).astype(BF16)
                 out[2, rows, ln] = dv[rows, ln].astype(BF16)
 
-        for i in range(3):
-            deal(core, dot_tn(x[...], out[i]), mine, theirs, slice(i * GROUP, (i + 1) * GROUP))
+        grads = jnp.concatenate([out[i] for i in range(3)], axis=1)
+        deal(core, dot_tn(x[...], grads), mine, theirs, slice(0, 3 * GROUP))
 
     full = lambda shape: pl.BlockSpec(shape, lambda p, b: (0,) * len(shape))
     part = pl.BlockSpec((SEQ, GROUP), lambda p, b: (0, at))
@@ -814,11 +814,8 @@
     def body(c, hid, a, b, d, w, *rest):
         mine, leave, token = rest[-3:]
         token[...] = jnp.zeros_like(token)
-        total = hid[...]
-        for g, ref in enumerate((a, b, d)):
-            for i in range(3):
-                at = i * D + g * GROUP
-                total = total + dot_nt(ref[i], w[:, at : at + GROUP])
+        grads = jnp.concatenate([ref[i] for i in range(3) for ref in (a, b, d)], axis=1)
+        total = hid[...] + dot_nt(grads, w[...])
         own = pl.program_id(0) // half == c[0]
 
         @pl.when(own)
@@ -1184,13 +1181,13 @@
     gu_there, down_there = core_swap(gu_there), core_swap(down_there)
     output, placed = place(core, out, core_swap(out_leave))
     tail_mine, tail_theirs = out_grad(core, ctx, att_grad, sums)
-    gu_keep, gu_send = join_rows(to_here, gu_here, gu_there, 2, deps=(tail_mine, placed))
+    gu_keep, gu_send = join_rows(to_here, gu_here, gu_there, 2, deps=(tail_mine,))
     down_parts = join_rows(deep_first, down_here, down_there, 4, deps=(gu_send,))
     gu_first = first_swap(gu_send)
     passing = depth_shift(down_parts[3], 1)
 
     common = (source,) + tables
-    back0 = attn_backward(0, 0, bounds, saved0, ctx_grad, *common, deps=(gu_send, down_parts[0]))
+    back0 = attn_backward(0, 0, bounds, saved0, ctx_grad, *common, deps=(gu_send, down_parts[0], placed))
     (passing,) = fold(passing, down_parts[2], 1, deps=(back0[3],))
     back1 = attn_backward(0, 1, bounds, saved1, ctx_grad, *common, deps=(passing,))
     passing = depth_shift(passing, 1)

time: 383 us -> 382 us (level)
  transfers between devices with their start and end apart: 46 -> 46, of which waited for: 13 -> 13; matrix products, arithmetic and copies ran while one was open for 5% -> 5% of each run, Pallas kernels for 39% -> 40%
where the time goes in v3:
time: 382 us; the launch traced here: 376 us
  Pallas kernels  237 us (62%)
  waiting for transfers between devices  59.3 us (16%)
  starting transfers between devices  41.2 us (11%)
  local copies, waits for them, and re-layouts  28.2 us (7%)
  other arithmetic  8.95 us (2%)
    pallas_call x1, Pallas kernels, middle(): pl.pallas_call(body, grid_spec=pltpu.PrefetchScalarGridSpec(num_scalar_pr...  81.2 us
    ppermute x46, waiting for transfers between devices, across(): return lax.ppermute(value, ('dp', 'tensor'), pairs)  59.3 us
    pallas_call x3, Pallas kernels, attn_backward(): pl.pallas_call(body, grid_spec=pltpu.PrefetchScalarGridSpec(num_scalar_pr...  56.1 us
    pallas_call x3, Pallas kernels, attn_forward(): pl.pallas_call(body, grid_spec=pltpu.PrefetchScalarGridSpec(num_scalar_pr...  43.3 us
    ppermute x46, starting transfers between devices, across(): return lax.ppermute(value, ('dp', 'tensor'), pairs)  41.2 us
    unnamed x121, local copies, waits for them, and re-layouts  19 us
    pallas_call x2, Pallas kernels, join_rows(): pl.pallas_call(body, grid_spec=pltpu.PrefetchScalarGridSpec(num_scalar_pr...  13.1 us
    pallas_call x1, Pallas kernels, input_back(): pl.pallas_call(body, grid_spec=pltpu.PrefetchScalarGridSpec(num_scalar_pr...  9.17 us
  transfers between devices with their start and end apart: 46, of which 13 were waited for; matrix products, arithmetic and copies ran while one was open for 5% of the time, Pallas kernels for 40%

profile of v3, /device:TPU:0, one launch (start us, length us, event | category | flops | bytes accessed | tf_op | source)
XLA Modules:
  0.0 376.1 jit_solution(14492366128858786160)
XLA Ops:
  1.6 5.0 %collective-permute-start.2 = (bf16[24,2304]{1,0:T(8,128)(2,1)S(1)}, bf16[24,2304]{1,0:T(8,128)(2,1)S(1)}, u32[]{:S(2)}, u32[]{:S(2)}) collective-permute-start(bf16[24,2304]{1,0:T(8,128)(2,1)S(1)} %bitcast.52), channel_id=1, source_target_pairs={{0,24},{1,25},{2,26},{3,27},{4,28},{5,29},{6,30},{7,31},{8,0},{9,1... | collective-permute-start | bytes 331784 | tf_op jit(solution)/shard_map/ppermute | solution.py:269
  11.2 2.6 constant_dynamic-slice_fusion
  14.5 8.1 %collective-permute-done.1 = bf16[24,2304]{1,0:T(8,128)(2,1)S(1)} collective-permute-done((bf16[24,2304]{1,0:T(8,128)(2,1)S(1)}, bf16[24,2304]{1,0:T(8,128)(2,1)S(1)}, u32[]{:S(2)}, u32[]{:S(2)}) %collective-permute-start.1) | collective-permute-done | bytes 110624 | tf_op jit(solution)/shard_map/ppermute | solution.py:269
  31.1 5.5 %collective-permute-done.5.refs_2_ = bf16[48,3072]{1,0:T(8,128)(2,1)S(1)} collective-permute-done((bf16[48,3072]{1,0:T(8,128)(2,1)S(1)}, bf16[48,3072]{1,0:T(8,128)(2,1)S(1)}, u32[]{:S(2)}, u32[]{:S(2)}) %collective-permute-start.5) | collective-permute-done | bytes 294944 | tf_op jit(solution)/shard_map/ppermute | solution.py:269
  42.2 10.3 %collective-permute-done.7.b = bf16[8,24,2304]{2,1,0:T(8,128)(2,1)} collective-permute-done((bf16[8,24,2304]{2,1,0:T(8,128)(2,1)S(1)}, bf16[8,24,2304]{2,1,0:T(8,128)(2,1)}, u32[]{:S(2)}, u32[]{:S(2)}) %collective-permute-start.7) | collective-permute-done | bytes 884768 | tf_op jit(solution)/shard_map/ppermute | solution.py:269
  59.5 4.8 %assemble.1 = bf16[32,24,2304]{2,1,0:T(8,128)(2,1)} custom-call(s32[32]{0:T(128)} %pad_add_fusion.2.idx, bf16[8,24,2304]{2,1,0:T(8,128)(2,1)} %copy-done.6, bf16[8,24,2304]{2,1,0:T(8,128)(2,1)} %collective-permute-done.7.b, bf16[8,24,2304]{2,1,0:T(8,128)(2,1)} %copy-done.51, bf16[8,24,2304]{2,1,0:T(8,128)(2,1)} %collective-permute-done.9.d, ...), custom_call_target="tpu_custom_call" | custom-call | bytes 7077888 | tf_op jit(solution)/shard_map/assemble/pallas_call | solution.py:398
  64.3 14.3 %attn_forward.3 = (bf16[1024,256]{1,0:T(8,128)(2,1)}, bf16[1024,256]{1,0:T(8,128)(2,1)}, bf16[1024,256]{1,0:T(8,128)(2,1)}, bf16[1024,256]{1,0:T(8,128)(2,1)}, f32[1,8,1024]{2,1,0:T(8,128)}) custom-call(s32[9]{0:T(128)} %pad_add_fusion.1.bnd, bf16[1024,768]{1,0:T(8,128)(2,1)} %copy-done.4, bf16[768,2304]{1,0:T(8,128)(2,1)} %bitcast.39, ...), custom_call_target="tpu_custom_call" | custom-call | flops 5502926848 | bytes 8388608 | tf_op jit(solution)/shard_map/attn_forward/pallas_call | solution.py:502
  80.9 3.0 pile.10.rest_0_.refs_0_
  85.1 14.3 %attn_forward.4 = (bf16[1024,256]{1,0:T(8,128)(2,1)}, bf16[1024,256]{1,0:T(8,128)(2,1)}, bf16[1024,256]{1,0:T(8,128)(2,1)}, bf16[1024,256]{1,0:T(8,128)(2,1)}, f32[1,8,1024]{2,1,0:T(8,128)}) custom-call(s32[9]{0:T(128)} %pad_add_fusion.1.bnd, bf16[1024,768]{1,0:T(8,128)(2,1)} %copy-done.4, bf16[768,2304]{1,0:T(8,128)(2,1)} %bitcast.42, ...), custom_call_target="tpu_custom_call" | custom-call | flops 5502926848 | bytes 8388608 | tf_op jit(solution)/shard_map/attn_forward/pallas_call | solution.py:502
  99.4 4.2 %collective-permute-done.15.refs_2_ = bf16[2,48,2048]{2,1,0:T(8,128)(2,1)S(1)} collective-permute-done((bf16[2,48,2048]{2,1,0:T(8,128)(2,1)S(1)}, bf16[2,48,2048]{2,1,0:T(8,128)(2,1)S(1)}, u32[]{:S(2)}, u32[]{:S(2)}) %collective-permute-start.15) | collective-permute-done | bytes 393248 | tf_op jit(solution)/shard_map/ppermute | solution.py:269
  106.9 6.3 %collective-permute-done.16.refs_1_ = bf16[8,48,3072]{2,1,0:T(8,128)(2,1)} collective-permute-done((bf16[8,48,3072]{2,1,0:T(8,128)(2,1)}, bf16[8,48,3072]{2,1,0:T(8,128)(2,1)}, u32[]{:S(2)}, u32[]{:S(2)}) %collective-permute-start.16) | collective-permute-done | bytes 2359328 | tf_op jit(solution)/shard_map/ppermute | solution.py:269
  113.7 14.7 %attn_forward.5 = (bf16[1024,256]{1,0:T(8,128)(2,1)}, bf16[1024,256]{1,0:T(8,128)(2,1)}, bf16[1024,256]{1,0:T(8,128)(2,1)}, bf16[1024,256]{1,0:T(8,128)(2,1)}, f32[1,8,1024]{2,1,0:T(8,128)}) custom-call(s32[9]{0:T(128)} %pad_add_fusion.1.bnd, bf16[1024,768]{1,0:T(8,128)(2,1)} %copy-done.4, bf16[768,2304]{1,0:T(8,128)(2,1)} %bitcast.45, ...), custom_call_target="tpu_custom_call" | custom-call | flops 5502926848 | bytes 8388608 | tf_op jit(solution)/shard_map/attn_forward/pallas_call | solution.py:502
  130.8 3.0 collective-permute-done.21.refs_7_
  133.8 81.2 %middle.1 = (bf16[512,768]{1,0:T(8,128)(2,1)}, bf16[512,768]{1,0:T(8,128)(2,1)}, bf16[2,768,1536]{2,1,0:T(8,128)(2,1)}, bf16[2,768,1536]{2,1,0:T(8,128)(2,1)}, b...) custom-call(s32[65]{0:T(128)} %concatenate.21.idx, ...), custom_call_target="tpu_custom_call" | custom-call | flops 45902462976 | bytes 41943040 | tf_op jit(solution)/shard_map/middle/pallas_call | solution.py:1050
  217.0 4.5 %out_grad.1 = (bf16[16,24,1024]{2,1,0:T(8,128)(2,1)}, bf16[16,24,1024]{2,1,0:T(8,128)(2,1)}) custom-call(s32[1]{0:T(128)} %bitcast.c, bf16[1024,256]{1,0:T(8,128)(2,1)} %get-tuple-element.88.ctx0.refs_0_.o, bf16[1024,256]{1,0:T(8,128)(2,1)} %get-tuple-element.90.ctx1.refs_1_.o, bf16[1024,256]{1,0:T(8,128)(2,1)} %get-tuple-element.92.ctx2.refs_2_.o, ...), custom_call_target="tpu_custom_call" | custom-call | flops 1207959552 | bytes 8388608 | tf_op jit(solution)/shard_map/out_grad/pallas_call | solution.py:688
  221.9 5.6 %collective-permute-done.22.b = bf16[512,768]{1,0:T(8,128)(2,1)S(1)} collective-permute-done((bf16[512,768]{1,0:T(8,128)(2,1)}, bf16[512,768]{1,0:T(8,128)(2,1)S(1)}, u32[]{:S(2)}, u32[]{:S(2)}) %collective-permute-start.22) | collective-permute-done | bytes 786464 | tf_op jit(solution)/shard_map/ppermute | solution.py:269
  228.3 3.1 place.2
  231.5 7.9 %join_rows.2 = (bf16[8,48,3072]{2,1,0:T(8,128)(2,1)}, bf16[8,48,3072]{2,1,0:T(8,128)(2,1)}) custom-call(s32[16]{0:T(128)} %fusion.16.idx, bf16[2,768,1536]{2,1,0:T(8,128)(2,1)} %get-tuple-element.103.a, bf16[2,768,1536]{2,1,0:T(8,128)(2,1)} %collective-permute-done.23.b, bf16[16,24,1024]{2,1,0:T(8,128)(2,1)} %get-tuple-element.107.rest_0_.refs_2_), custom_call_target="tpu_custom_call" | custom-call | flops 2359296 | bytes 14155776 | tf_op jit(solution)/shard_map/join_rows/pallas_call | solution.py:662
  241.2 5.2 %join_rows.3 = (bf16[4,48,1536]{2,1,0:T(8,128)(2,1)}, bf16[4,48,1536]{2,1,0:T(8,128)(2,1)}, bf16[4,48,1536]{2,1,0:T(8,128)(2,1)}, bf16[4,48,1536]{2,1,0:T(8,128)(2,1)}) custom-call(s32[16]{0:T(128)} %fusion.21.idx, bf16[1,768,1536]{2,1,0:T(8,128)(2,1)} %get-tuple-element.109.a, bf16[1,768,1536]{2,1,0:T(8,128)(2,1)} %copy-done.50, ...), custom_call_target="tpu_custom_call" | custom-call | flops 1179648 | bytes 7077888 | tf_op jit(solution)/shard_map/join_rows/pallas_call | solution.py:662
  246.4 18.6 %attn_backward.3 = (bf16[3,1024,256]{2,1,0:T(8,128)(2,1)}, bf16[16,24,768]{2,1,0:T(8,128)(2,1)}, bf16[16,24,768]{2,1,0:T(8,128)(2,1)}, f32[8,128]{1,0:T(8,128)}) custom-call(s32[9]{0:T(128)} %pad_add_fusion.1.bnd, bf16[1024,256]{1,0:T(8,128)(2,1)} %get-tuple-element.99.q, bf16[1024,256]{1,0:T(8,128)(2,1)} %get-tuple-element.100.k, ...), custom_call_target="tpu_custom_call" | custom-call | flops 11945377792 | bytes 10485760 | tf_op jit(solution)/shard_map/attn_backward/pallas_call | solution.py:609
  267.6 18.8 %attn_backward.4 = (bf16[3,1024,256]{2,1,0:T(8,128)(2,1)}, bf16[16,24,768]{2,1,0:T(8,128)(2,1)}, bf16[16,24,768]{2,1,0:T(8,128)(2,1)}, f32[8,128]{1,0:T(8,128)}) custom-call(s32[9]{0:T(128)} %pad_add_fusion.1.bnd, bf16[1024,256]{1,0:T(8,128)(2,1)} %get-tuple-element.114.q, bf16[1024,256]{1,0:T(8,128)(2,1)} %get-tuple-element.115.k, ...), custom_call_target="tpu_custom_call" | custom-call | flops 11945377792 | bytes 10485760 | tf_op jit(solution)/shard_map/attn_backward/pallas_call | solution.py:609
  292.2 3.3 fold.11
  297.7 3.0 join_dealt.2
  303.0 18.7 %attn_backward.5 = (bf16[3,1024,256]{2,1,0:T(8,128)(2,1)}, bf16[16,24,768]{2,1,0:T(8,128)(2,1)}, bf16[16,24,768]{2,1,0:T(8,128)(2,1)}, f32[8,128]{1,0:T(8,128)}) custom-call(s32[9]{0:T(128)} %pad_add_fusion.1.bnd, bf16[1024,256]{1,0:T(8,128)(2,1)} %get-tuple-element.121.q, bf16[1024,256]{1,0:T(8,128)(2,1)} %get-tuple-element.122.k, ...), custom_call_target="tpu_custom_call" | custom-call | flops 11945377792 | bytes 10485760 | tf_op jit(solution)/shard_map/attn_backward/pallas_call | solution.py:609
  326.8 3.2 collective-permute-start.36
  332.0 5.0 %collective-permute-done.36.a = bf16[1,48,3072]{2,1,0:T(8,128)(2,1)S(1)} collective-permute-done((bf16[1,48,3072]{2,1,0:T(8,128)(2,1)S(1)}, bf16[1,48,3072]{2,1,0:T(8,128)(2,1)S(1)}, u32[]{:S(2)}, u32[]{:S(2)}) %collective-permute-start.36) | collective-permute-done | bytes 294944 | tf_op jit(solution)/shard_map/ppermute | solution.py:269
  338.6 9.2 %input_back.1 = (f32[512,768]{1,0:T(8,128)}, f32[512,768]{1,0:T(8,128)}, f32[8,128]{1,0:T(8,128)}) custom-call(s32[1]{0:T(128)} %bitcast.c, f32[1024,768]{1,0:T(8,128)} %get-tuple-element.98.hid, bf16[3,1024,256]{2,1,0:T(8,128)(2,1)} %get-tuple-element.113.a, bf16[3,1024,256]{2,1,0:T(8,128)(2,1)} %get-tuple-element.120.b, ...), custom_call_target="tpu_custom_call" | custom-call | flops 3623878656 | bytes 16777216 | tf_op jit(solution)/shard_map/input_back/pallas_call | solution.py:831
  352.0 3.0 collective-permute-start.42
  354.9 2.9 collective-permute-start.43
  358.5 3.9 %collective-permute-done.44.a = bf16[1,48,3072]{2,1,0:T(8,128)(2,1)S(1)} collective-permute-done((bf16[1,48,3072]{2,1,0:T(8,128)(2,1)S(1)}, bf16[1,48,3072]{2,1,0:T(8,128)(2,1)S(1)}, u32[]{:S(2)}, u32[]{:S(2)}) %collective-permute-start.44) | collective-permute-done | bytes 294944 | tf_op jit(solution)/shard_map/ppermute | solution.py:269
  363.8 4.2 %place.3 = (f32[2,512,768]{2,1,0:T(8,128)}, f32[8,128]{1,0:T(8,128)}) custom-call(s32[1]{0:T(128)} %bitcast.c, f32[512,768]{1,0:T(8,128)} %get-tuple-element.150.a, f32[512,768]{1,0:T(8,128)} %collective-permute-done.40.b), custom_call_target="tpu_custom_call" | custom-call | bytes 1572864 | tf_op jit(solution)/shard_map/place/pallas_call | solution.py:364
  368.0 4.3 %collective-permute-done.42.c = bf16[1,24,3328]{2,1,0:T(8,128)(2,1)S(1)} collective-permute-done((bf16[1,24,3328]{2,1,0:T(8,128)(2,1)S(1)}, bf16[1,24,3328]{2,1,0:T(8,128)(2,1)S(1)}, u32[]{:S(2)}, u32[]{:S(2)}) %collective-permute-start.42) | collective-permute-done | bytes 159776 | tf_op jit(solution)/shard_map/ppermute | solution.py:269
  (256 shorter events, 72.7 us)
Async XLA Ops:
  6.6 16.0 %collective-permute-start.1 = (bf16[24,2304]{1,0:T(8,128)(2,1)S(1)}, bf16[24,2304]{1,0:T(8,128)(2,1)S(1)}, u32[]{:S(2)}, u32[]{:S(2)}) collective-permute-start(bf16[24,2304]{1,0:T(8,128)(2,1)S(1)} %bitcast.53), channel_id=1, source_target_pairs={{0,16},{1,17},{2,18},{3,19},{4,20},{5,21},{6,22},{7,23},{8,24},{9,... | collective-permute-start | bytes 331784 | tf_op jit(solution)/shard_map/ppermute | solution.py:269
  6.6 16.0 %collective-permute-start = (bf16[24,2304]{1,0:T(8,128)(2,1)S(1)}, bf16[24,2304]{1,0:T(8,128)(2,1)S(1)}, u32[]{:S(2)}, u32[]{:S(2)}) collective-permute-start(bf16[24,2304]{1,0:T(8,128)(2,1)S(1)} %bitcast.54), channel_id=1, source_target_pairs={{0,8},{1,9},{2,10},{3,11},{4,12},{5,13},{6,14},{7,15},{8,16},{9,17... | collective-permute-start | bytes 331784 | tf_op jit(solution)/shard_map/ppermute | solution.py:269
  8.6 14.0 %collective-permute-start.3 = (bf16[48,3072]{1,0:T(8,128)(2,1)S(1)}, bf16[48,3072]{1,0:T(8,128)(2,1)S(1)}, u32[]{:S(2)}, u32[]{:S(2)}) collective-permute-start(bf16[48,3072]{1,0:T(8,128)(2,1)S(1)} %bitcast.51), channel_id=1, source_target_pairs={{0,8},{1,9},{2,10},{3,11},{4,12},{5,13},{6,14},{7,15},{8,16},{9,17... | collective-permute-start | bytes 884744 | tf_op jit(solution)/shard_map/ppermute | solution.py:269
  13.8 15.1 %collective-permute-start.6 = (bf16[512,768]{1,0:T(8,128)(2,1)}, bf16[512,768]{1,0:T(8,128)(2,1)}, u32[]{:S(2)}, u32[]{:S(2)}) collective-permute-start(bf16[512,768]{1,0:T(8,128)(2,1)} %get-tuple-element.201), channel_id=1, source_target_pairs={{0,1},{1,0},{2,3},{3,2},{4,5},{5,4},{6,7},{7,6},{8,9},{9,8},{10,11... | collective-permute-start | bytes 2359304 | tf_op jit(solution)/shard_map/ppermute | solution.py:269
  23.2 13.3 %collective-permute-start.4 = (bf16[4,24,2304]{2,1,0:T(8,128)(2,1)S(1)}, bf16[4,24,2304]{2,1,0:T(8,128)(2,1)S(1)}, u32[]{:S(2)}, u32[]{:S(2)}) collective-permute-start(bf16[4,24,2304]{2,1,0:T(8,128)(2,1)S(1)} %pile.6.refs_0_), channel_id=1, source_target_pairs={{0,2},{1,5},{2,0},{3,7},{4,6},{5,1},{6,4},{7,3},{8,10},{9,13},{10,... | collective-permute-start | bytes 1327112 | tf_op jit(solution)/shard_map/ppermute | solution.py:269
  37.2 15.3 %collective-permute-start.7 = (bf16[8,24,2304]{2,1,0:T(8,128)(2,1)S(1)}, bf16[8,24,2304]{2,1,0:T(8,128)(2,1)}, u32[]{:S(2)}, u32[]{:S(2)}) collective-permute-start(bf16[8,24,2304]{2,1,0:T(8,128)(2,1)S(1)} %pile.7.a), channel_id=1, source_target_pairs={{0,4},{1,3},{2,6},{3,1},{4,0},{5,7},{6,2},{7,5},{8,12},{9,11},{10,... | collective-permute-start | bytes 2654216 | tf_op jit(solution)/shard_map/ppermute | solution.py:269
  38.1 14.6 %collective-permute-start.10 = (bf16[48,3072]{1,0:T(8,128)(2,1)S(1)}, bf16[48,3072]{1,0:T(8,128)(2,1)S(1)}, u32[]{:S(2)}, u32[]{:S(2)}) collective-permute-start(bf16[48,3072]{1,0:T(8,128)(2,1)S(1)} %collective-permute-done.5.refs_2_), channel_id=1, source_target_pairs={{0,8},{1,9},{2,10},{3,11},{4,12},{5,13},{6,14},{7,15},{8,16},{9,17... | collective-permute-start | bytes 884744 | tf_op jit(solution)/shard_map/ppermute | solution.py:269
  39.1 16.7 %collective-permute-start.11 = (bf16[48,2048]{1,0:T(8,128)(2,1)S(1)}, bf16[48,2048]{1,0:T(8,128)(2,1)S(1)}, u32[]{:S(2)}, u32[]{:S(2)}) collective-permute-start(bf16[48,2048]{1,0:T(8,128)(2,1)S(1)} %get-tuple-element.202), channel_id=1, source_target_pairs={{0,2},{1,5},{2,0},{3,7},{4,6},{5,1},{6,4},{7,3},{8,10},{9,13},{10,... | collective-permute-start | bytes 589832 | tf_op jit(solution)/shard_map/ppermute | solution.py:269
  42.1 16.5 %collective-permute-start.8 = (bf16[8,24,2304]{2,1,0:T(8,128)(2,1)S(1)}, bf16[8,24,2304]{2,1,0:T(8,128)(2,1)S(1)}, u32[]{:S(2)}, u32[]{:S(2)}) collective-permute-start(bf16[8,24,2304]{2,1,0:T(8,128)(2,1)S(1)} %pile.7.a), channel_id=1, source_target_pairs={{0,1},{1,0},{2,3},{3,2},{4,5},{5,4},{6,7},{7,6},{8,9},{9,8},{10,11... | collective-permute-start | bytes 2654216 | tf_op jit(solution)/shard_map/ppermute | solution.py:269
  53.1 25.6 %collective-permute-start.12 = (bf16[4,48,3072]{2,1,0:T(8,128)(2,1)S(1)}, bf16[4,48,3072]{2,1,0:T(8,128)(2,1)}, u32[]{:S(2)}, u32[]{:S(2)}) collective-permute-start(bf16[4,48,3072]{2,1,0:T(8,128)(2,1)S(1)} %pile.8.refs_2_.rest_0_.refs_0_), channel_id=1, source_target_pairs={{0,2},{1,5},{2,0},{3,7},{4,6},{5,1},{6,4},{7,3},{8,10},{9,13},{10,... | collective-permute-start | bytes 3538952 | tf_op jit(solution)/shard_map/ppermute | solution.py:269
  56.3 22.3 %collective-permute-start.14 = (bf16[2,48,2048]{2,1,0:T(8,128)(2,1)S(1)}, bf16[2,48,2048]{2,1,0:T(8,128)(2,1)S(1)}, u32[]{:S(2)}, u32[]{:S(2)}) collective-permute-start(bf16[2,48,2048]{2,1,0:T(8,128)(2,1)S(1)} %pile.9.rest_1_.refs_0_), channel_id=1, source_target_pairs={{0,24},{1,25},{2,26},{3,27},{4,28},{5,29},{6,30},{7,31},{8,0},{9,1... | collective-permute-start | bytes 1179656 | tf_op jit(solution)/shard_map/ppermute | solution.py:269
  56.9 21.7 %collective-permute-start.13 = (bf16[2,48,2048]{2,1,0:T(8,128)(2,1)S(1)}, bf16[2,48,2048]{2,1,0:T(8,128)(2,1)S(1)}, u32[]{:S(2)}, u32[]{:S(2)}) collective-permute-start(bf16[2,48,2048]{2,1,0:T(8,128)(2,1)S(1)} %pile.9.rest_1_.refs_0_), channel_id=1, source_target_pairs={{0,8},{1,9},{2,10},{3,11},{4,12},{5,13},{6,14},{7,15},{8,16},{9,17... | collective-permute-start | bytes 1179656 | tf_op jit(solution)/shard_map/ppermute | solution.py:269
  84.0 29.2 %collective-permute-start.16 = (bf16[8,48,3072]{2,1,0:T(8,128)(2,1)}, bf16[8,48,3072]{2,1,0:T(8,128)(2,1)}, u32[]{:S(2)}, u32[]{:S(2)}) collective-permute-start(bf16[8,48,3072]{2,1,0:T(8,128)(2,1)} %pile.10.rest_0_.refs_0_), channel_id=1, source_target_pairs={{0,4},{1,3},{2,6},{3,1},{4,0},{5,7},{6,2},{7,5},{8,12},{9,11},{10,... | collective-permute-start | bytes 7077896 | tf_op jit(solution)/shard_map/ppermute | solution.py:269
  84.3 19.3 %collective-permute-start.15 = (bf16[2,48,2048]{2,1,0:T(8,128)(2,1)S(1)}, bf16[2,48,2048]{2,1,0:T(8,128)(2,1)S(1)}, u32[]{:S(2)}, u32[]{:S(2)}) collective-permute-start(bf16[2,48,2048]{2,1,0:T(8,128)(2,1)S(1)} %copy-done.15), channel_id=1, source_target_pairs={{0,16},{1,17},{2,18},{3,19},{4,20},{5,21},{6,22},{7,23},{8,24},{9,... | collective-permute-start | bytes 1179656 | tf_op jit(solution)/shard_map/ppermute | solution.py:269
  105.2 24.9 %collective-permute-start.19 = (bf16[8,48,2048]{2,1,0:T(8,128)(2,1)S(1)}, bf16[8,48,2048]{2,1,0:T(8,128)(2,1)}, u32[]{:S(2)}, u32[]{:S(2)}) collective-permute-start(bf16[8,48,2048]{2,1,0:T(8,128)(2,1)S(1)} %pile.11.rest_0_.refs_4_), channel_id=1, source_target_pairs={{0,4},{1,3},{2,6},{3,1},{4,0},{5,7},{6,2},{7,5},{8,12},{9,11},{10,... | collective-permute-start | bytes 4718600 | tf_op jit(solution)/shard_map/ppermute | solution.py:269
  106.9 23.9 %collective-permute-start.17 = (bf16[8,48,3072]{2,1,0:T(8,128)(2,1)}, bf16[8,48,3072]{2,1,0:T(8,128)(2,1)}, u32[]{:S(2)}, u32[]{:S(2)}) collective-permute-start(bf16[8,48,3072]{2,1,0:T(8,128)(2,1)} %pile.10.rest_0_.refs_0_), channel_id=1, source_target_pairs={{0,1},{1,0},{2,3},{3,2},{4,5},{5,4},{6,7},{7,6},{8,9},{9,8},{10,11... | collective-permute-start | bytes 7077896 | tf_op jit(solution)/shard_map/ppermute | solution.py:269
  113.2 20.6 %collective-permute-start.18 = (bf16[8,48,3072]{2,1,0:T(8,128)(2,1)}, bf16[8,48,3072]{2,1,0:T(8,128)(2,1)}, u32[]{:S(2)}, u32[]{:S(2)}) collective-permute-start(bf16[8,48,3072]{2,1,0:T(8,128)(2,1)} %collective-permute-done.16.refs_1_), channel_id=1, source_target_pairs={{0,1},{1,0},{2,3},{3,2},{4,5},{5,4},{6,7},{7,6},{8,9},{9,8},{10,11... | collective-permute-start | bytes 7077896 | tf_op jit(solution)/shard_map/ppermute | solution.py:269
  113.2 17.6 %collective-permute-start.20 = (bf16[8,48,2048]{2,1,0:T(8,128)(2,1)S(1)}, bf16[8,48,2048]{2,1,0:T(8,128)(2,1)}, u32[]{:S(2)}, u32[]{:S(2)}) collective-permute-start(bf16[8,48,2048]{2,1,0:T(8,128)(2,1)S(1)} %pile.11.rest_0_.refs_4_), channel_id=1, source_target_pairs={{0,1},{1,0},{2,3},{3,2},{4,5},{5,4},{6,7},{7,6},{8,9},{9,8},{10,11... | collective-permute-start | bytes 4718600 | tf_op jit(solution)/shard_map/ppermute | solution.py:269
  215.0 16.5 %collective-permute-start.23 = (bf16[2,768,1536]{2,1,0:T(8,128)(2,1)}, bf16[2,768,1536]{2,1,0:T(8,128)(2,1)}, u32[]{:S(2)}, u32[]{:S(2)}) collective-permute-start(bf16[2,768,1536]{2,1,0:T(8,128)(2,1)} %get-tuple-element.104), channel_id=1, source_target_pairs={{0,1},{1,0},{2,3},{3,2},{4,5},{5,4},{6,7},{7,6},{8,9},{9,8},{10,11... | collective-permute-start | bytes 14155784 | tf_op jit(solution)/shard_map/ppermute | solution.py:269
  215.2 24.6 %collective-permute-start.24 = (bf16[1,768,1536]{2,1,0:T(8,128)(2,1)}, bf16[1,768,1536]{2,1,0:T(8,128)(2,1)S(1)}, u32[]{:S(2)}, u32[]{:S(2)}) collective-permute-start(bf16[1,768,1536]{2,1,0:T(8,128)(2,1)} %get-tuple-element.110), channel_id=1, source_target_pairs={{0,1},{1,0},{2,3},{3,2},{4,5},{5,4},{6,7},{7,6},{8,9},{9,8},{10,11... | collective-permute-start | bytes 7077896 | tf_op jit(solution)/shard_map/ppermute | solution.py:269
  221.5 76.1 %collective-permute-start.29 = (bf16[16,24,1024]{2,1,0:T(8,128)(2,1)}, bf16[16,24,1024]{2,1,0:T(8,128)(2,1)S(1)}, u32[]{:S(2)}, u32[]{:S(2)}) collective-permute-start(bf16[16,24,1024]{2,1,0:T(8,128)(2,1)} %get-tuple-element.132), channel_id=1, source_target_pairs={{0,1},{1,0},{2,3},{3,2},{4,5},{5,4},{6,7},{7,6},{8,9},{9,8},{10,11... | collective-permute-start | bytes 2359304 | tf_op jit(solution)/shard_map/ppermute | solution.py:269
  239.4 52.8 %collective-permute-start.26 = (bf16[8,48,3072]{2,1,0:T(8,128)(2,1)}, bf16[8,48,3072]{2,1,0:T(8,128)(2,1)}, u32[]{:S(2)}, u32[]{:S(2)}) collective-permute-start(bf16[8,48,3072]{2,1,0:T(8,128)(2,1)} %get-tuple-element.108.rest_0_), channel_id=1, source_target_pairs={{0,2},{1,5},{2,0},{3,7},{4,6},{5,1},{6,4},{7,3},{8,10},{9,13},{10,... | collective-permute-start | bytes 7077896 | tf_op jit(solution)/shard_map/ppermute | solution.py:269
  246.4 18.7 %collective-permute-start.25 = (bf16[4,48,1536]{2,1,0:T(8,128)(2,1)}, bf16[4,48,1536]{2,1,0:T(8,128)(2,1)S(1)}, u32[]{:S(2)}, u32[]{:S(2)}) collective-permute-start(bf16[4,48,1536]{2,1,0:T(8,128)(2,1)} %get-tuple-element.117), channel_id=1, source_target_pairs={{0,8},{1,9},{2,10},{3,11},{4,12},{5,13},{6,14},{7,15},{8,16},{9,17... | collective-permute-start | bytes 1769480 | tf_op jit(solution)/shard_map/ppermute | solution.py:269
  265.0 32.6 %collective-permute-start.27 = (bf16[16,24,768]{2,1,0:T(8,128)(2,1)}, bf16[16,24,768]{2,1,0:T(8,128)(2,1)}, u32[]{:S(2)}, u32[]{:S(2)}) collective-permute-start(bf16[16,24,768]{2,1,0:T(8,128)(2,1)} %get-tuple-element.130), channel_id=1, source_target_pairs={{0,1},{1,0},{2,3},{3,2},{4,5},{5,4},{6,7},{7,6},{8,9},{9,8},{10,11... | collective-permute-start | bytes 1769480 | tf_op jit(solution)/shard_map/ppermute | solution.py:269
  266.7 19.9 %collective-permute-start.30 = (bf16[4,48,1536]{2,1,0:T(8,128)(2,1)}, bf16[4,48,1536]{2,1,0:T(8,128)(2,1)S(1)}, u32[]{:S(2)}, u32[]{:S(2)}) collective-permute-start(bf16[4,48,1536]{2,1,0:T(8,128)(2,1)} %fold.10.rest_0_), channel_id=1, source_target_pairs={{0,8},{1,9},{2,10},{3,11},{4,12},{5,13},{6,14},{7,15},{8,16},{9,17... | collective-permute-start | bytes 1769480 | tf_op jit(solution)/shard_map/ppermute | solution.py:269
  290.5 33.3 %collective-permute-start.32 = (bf16[4,48,1536]{2,1,0:T(8,128)(2,1)S(1)}, bf16[4,48,1536]{2,1,0:T(8,128)(2,1)}, u32[]{:S(2)}, u32[]{:S(2)}) collective-permute-start(bf16[4,48,1536]{2,1,0:T(8,128)(2,1)S(1)} %fold.12.refs_6_.rest_2_), channel_id=1, source_target_pairs={{0,8},{1,9},{2,10},{3,11},{4,12},{5,13},{6,14},{7,15},{8,16},{9,17... | collective-permute-start | bytes 1769480 | tf_op jit(solution)/shard_map/ppermute | solution.py:269
  296.6 25.1 %collective-permute-start.33 = (bf16[4,48,3072]{2,1,0:T(8,128)(2,1)}, bf16[4,48,3072]{2,1,0:T(8,128)(2,1)S(1)}, u32[]{:S(2)}, u32[]{:S(2)}) collective-permute-start(bf16[4,48,3072]{2,1,0:T(8,128)(2,1)} %get-tuple-element.127.refs_7_.rest_0_), channel_id=1, source_target_pairs={{0,4},{1,3},{2,6},{3,1},{4,0},{5,7},{6,2},{7,5},{8,12},{9,11},{10,... | collective-permute-start | bytes 3538952 | tf_op jit(solution)/shard_map/ppermute | solution.py:269
  301.6 28.4 %collective-permute-start.34 = (bf16[8,24,2560]{2,1,0:T(8,128)(2,1)}, bf16[8,24,2560]{2,1,0:T(8,128)(2,1)S(1)}, u32[]{:S(2)}, u32[]{:S(2)}) collective-permute-start(bf16[8,24,2560]{2,1,0:T(8,128)(2,1)} %get-tuple-element.134.rest_1_), channel_id=1, source_target_pairs={{0,2},{1,5},{2,0},{3,7},{4,6},{5,1},{6,4},{7,3},{8,10},{9,13},{10,... | collective-permute-start | bytes 2949128 | tf_op jit(solution)/shard_map/ppermute | solution.py:269
  348.8 15.0 %collective-permute-start.40 = (f32[512,768]{1,0:T(8,128)}, f32[512,768]{1,0:T(8,128)}, u32[]{:S(2)}, u32[]{:S(2)}) collective-permute-start(f32[512,768]{1,0:T(8,128)} %get-tuple-element.156), channel_id=1, source_target_pairs={{0,1},{1,0},{2,3},{3,2},{4,5},{5,4},{6,7},{7,6},{8,9},{9,8},{10,11... | collective-permute-start | bytes 4718600 | tf_op jit(solution)/shard_map/ppermute | solution.py:269
  350.9 17.1 %collective-permute-start.41 = (bf16[1,24,3328]{2,1,0:T(8,128)(2,1)S(1)}, bf16[1,24,3328]{2,1,0:T(8,128)(2,1)S(1)}, u32[]{:S(2)}, u32[]{:S(2)}) collective-permute-start(bf16[1,24,3328]{2,1,0:T(8,128)(2,1)S(1)} %get-tuple-element.159), channel_id=1, source_target_pairs={{0,8},{1,9},{2,10},{3,11},{4,12},{5,13},{6,14},{7,15},{8,16},{9,17... | collective-permute-start | bytes 479240 | tf_op jit(solution)/shard_map/ppermute | solution.py:269
  352.0 20.3 %collective-permute-start.42 = (bf16[1,24,3328]{2,1,0:T(8,128)(2,1)S(1)}, bf16[1,24,3328]{2,1,0:T(8,128)(2,1)S(1)}, u32[]{:S(2)}, u32[]{:S(2)}) collective-permute-start(bf16[1,24,3328]{2,1,0:T(8,128)(2,1)S(1)} %get-tuple-element.160), channel_id=1, source_target_pairs={{0,16},{1,17},{2,18},{3,19},{4,20},{5,21},{6,22},{7,23},{8,24},{9,... | collective-permute-start | bytes 479240 | tf_op jit(solution)/shard_map/ppermute | solution.py:269
  354.9 17.3 %collective-permute-start.43 = (bf16[1,24,3328]{2,1,0:T(8,128)(2,1)S(1)}, bf16[1,24,3328]{2,1,0:T(8,128)(2,1)S(1)}, u32[]{:S(2)}, u32[]{:S(2)}) collective-permute-start(bf16[1,24,3328]{2,1,0:T(8,128)(2,1)S(1)} %get-tuple-element.161), channel_id=1, source_target_pairs={{0,24},{1,25},{2,26},{3,27},{4,28},{5,29},{6,30},{7,31},{8,0},{9,1... | collective-permute-start | bytes 479240 | tf_op jit(solution)/shard_map/ppermute | solution.py:269
  (71 other events, 518.4 us)
